TPU v7x, 256 devices: a whole 4x4x8 slice. The times are simulated.
256 devices in a mesh: ctx: 32 (over z, x_lo, core), grp: 8 (over y, x_hi).
Axes of the slice: x: 4 (x_hi: 2, x_lo: 2; x = x_hi * 2 + x_lo), y: 4, z: 8, core: 2. Of those that a mesh axis runs over, the one named last changes fastest.
Arguments:
- prompt_x: bfloat16 [2, 16384, 8192], P(None, 'ctx', 'grp'), may hold values from -6 to 6
- prompt_b: bfloat16 [2, 16384, 2048], P(None, 'ctx', 'grp'), may hold values from -6 to 6
- prompt_c: bfloat16 [2, 16384, 2048], P(None, 'ctx', 'grp'), may hold values from -0.375 to 0.375
- prompt_step: float32 [2, 128, 16384], P(None, 'grp', 'ctx'), may hold values from 0.005 to 0.05
- prompt_decay: float32 [2, 128, 16384], P(None, 'grp', 'ctx'), may hold values from -1 to 0
- skip_weight: float32 [128], P('grp'), may hold values from 0.5 to 1.5
- decode_x: bfloat16 [4, 32, 128, 64], P(None, None, 'grp', 'ctx'), may hold values from -6 to 6
- decode_b: bfloat16 [4, 32, 2048], P(None, None, 'grp'), may hold values from -6 to 6
- decode_c: bfloat16 [4, 32, 2048], P(None, None, 'grp'), may hold values from -0.375 to 0.375
- decode_step: float32 [4, 32, 128], P(None, None, 'grp'), may hold values from 0.05 to 0.5
- decode_decay: float32 [4, 32, 128], P(None, None, 'grp'), may hold values from -0.5 to -0.01
- out_proj: bfloat16 [128, 64, 8192], P('grp', 'ctx'), may hold values from -0.0625 to 0.0625
- norm_gain: float32 [8192], replicated, may hold values from 0.5 to 1.5
- lm_head: bfloat16 [8192, 65536], P(None, ('ctx', 'grp')), may hold values from -11.932427 to 11.932427
- mask_words: int32 [16, 2048], P(None, ('ctx', 'grp')), may hold values from -2147483648 to 2147483646, as said below
- state_ids: int32 [4, 32], replicated, may hold values from 0 to 15
- chosen: int32 [4, 32], replicated, may hold values from 0 to 65535, as said below
Outputs:
- prompt_y: bfloat16 [2, 16384, 8192], P(None, 'ctx', 'grp')
- decode_state: float32 [32, 128, 64, 256], P(None, 'grp', 'ctx')
- chosen_logprob: float32 [4, 32], replicated
Inputs may be any that keep to these rules, and one draw needn't show every extreme that they name: `mask_words`: bit b of word w in row q says whether token 32 w + b is allowed in automaton state q. Every chosen token is allowed by the mask row of its row's automaton state at that step.
All inputs are finite; a program needn't handle non-finite values.
Results may differ from a plain program's by a relative error of at most 0.0054.
Values sent between devices are 32-bit elements; how exact they have to be, the bound alone decides.
No kernel may reach another device: no remote copies, remote signals or barrier semaphores. Data moves between devices by JAX's collectives and lax.ppermute only.
A program may use at most 128 MiB of HBM per device.

v0:
```python
import jax
import jax.numpy as jnp
from jax import lax
from jax.sharding import Mesh
from jax.sharding import PartitionSpec as P

BLOCK = 256
STEPS = 4
CTX = ("ctx_0", "ctx_1", "ctx_2")
GRP = ("grp_0", "grp_1")
CTX_GRP = ("ctx_0", "ctx_1", "ctx_2", "grp_0", "grp_1")


NEG_BIG = -1e30
EPS = 1e-05


def nothing_yet(value, identity):
    return jax.tree.map(
        lambda part, zero: jnp.zeros_like(part) + jnp.asarray(zero, part.dtype), value, identity
    )


def entering_2(value, axes, combine, identity):
    before = start = nothing_yet(value, identity)
    total = value
    for axis in reversed(axes):
        devices, position = (lax.axis_size(axis), lax.axis_index(axis))
        pieces = jax.tree.map(lambda part: lax.all_gather(part, axis), total)
        inside, total = (start, start)
        for k in range(devices):
            passed = k < position
            total = combine(total, jax.tree.map(lambda part: part[k], pieces))
            inside = jax.tree.map(lambda new, old: jnp.where(passed, new, old), total, inside)
        before = combine(inside, before)
    return before


def from_everyone(value, axis):
    devices = lax.axis_size(axis)
    return lax.all_to_all(
        jnp.broadcast_to(value[None], (devices, *value.shape)), axis, 0, 0, tiled=True
    )


def folded_in_pairs(pieces, combine):
    while len(jax.tree.leaves(pieces)[0]) > 1:
        pieces = jax.vmap(combine)(*(pieces[side::2] for side in (0, 1)))
    return pieces[0]


def prefix(value, axis, combine, identity):
    devices, position = (lax.axis_size(axis), lax.axis_index(axis))
    passed = jnp.arange(devices) > position

    def kept(part, zero, own):
        part = jnp.where(
            passed.reshape(-1, *(1 for _ in own.shape)), part, jnp.asarray(zero, own.dtype)
        )
        return part[::-1]

    pieces = from_everyone(value, axis)
    return folded_in_pairs(kept(pieces, identity, value), combine)


def in_blocks(value, dim, devices):
    before, after = (value.shape[:dim], value.shape[dim + 1 :])
    return jnp.moveaxis(value.reshape(*before, devices, -1, *after), dim, 0)


def sent_and_summed(value, axis, dim):
    pieces = in_blocks(value, dim, lax.axis_size(axis))
    arrived = lax.all_to_all(pieces, axis, split_axis=0, concat_axis=0, tiled=True)
    return arrived.sum(axis=0)


def gathered_once(value, axis):
    leaves = jax.tree.leaves(value)
    turns = sorted(range(len(leaves)), key=lambda k: -leaves[k].size)
    width = (1, *leaves[turns[0]].shape)[-1]
    lines = [
        jnp.pad(leaves[k].reshape(-1), (0, -leaves[k].size % width)).reshape(-1, width)
        for k in turns
    ]
    both, at, found = (lax.all_gather(jnp.concatenate(lines), axis), 0, {})
    for k, line in zip(turns, lines):
        share = both[:, at : at + len(line)].reshape(len(both), -1)
        found[k] = share[:, : leaves[k].size].reshape(-1, *leaves[k].shape)
        at += len(line)
    numbers = iter(range(len(leaves)))
    return jax.tree.map(lambda _: found[next(numbers)], value)


def combined_by_axis(value, axes, combine):
    for axis in axes:
        pieces = gathered_once(value, axis)
        value = jax.tree.map(lambda part: part[0], pieces)
        for k in range(1, lax.axis_size(axis)):
            value = combine(value, jax.tree.map(lambda part: part[k], pieces))
    return value


def combine_pair(earlier, later):
    return (earlier[0] + later[0], jnp.exp(later[0])[:, :, None, None] * earlier[1] + later[1])


def add_logs(earlier, later):
    return earlier + later


def merge_parts(first, second):
    joint_max = jnp.maximum(first[0], second[0])
    joint_total = first[1] * jnp.exp(first[0] - joint_max) + second[1] * jnp.exp(
        second[0] - joint_max
    )
    return (joint_max, joint_total, first[2] + second[2])


def by_block(values, seq_count, block_count):
    head_count = values.shape[1]
    shaped = values.reshape(seq_count, head_count, block_count, BLOCK)
    return shaped.transpose(0, 2, 1, 3).reshape(seq_count * block_count, head_count, BLOCK)


def body(
    prompt_x,
    prompt_b,
    prompt_c,
    prompt_step,
    prompt_decay,
    skip_weight,
    decode_x,
    decode_b,
    decode_c,
    decode_step,
    decode_decay,
    out_proj,
    norm_gain,
    lm_head,
    mask_words,
    state_ids,
    chosen,
):
    seq_count, tok_count, feature_width = prompt_x.shape
    state_dim = prompt_b.shape[2]
    head_count = prompt_step.shape[1]
    head_dim = feature_width // head_count
    block_count = tok_count // BLOCK
    flat_count = seq_count * block_count
    x_blocks = prompt_x.reshape(flat_count, BLOCK, head_count, head_dim)
    b_blocks = prompt_b.reshape(flat_count, BLOCK, state_dim)
    c_blocks = prompt_c.reshape(flat_count, BLOCK, state_dim)
    step_blocks = by_block(prompt_step, seq_count, block_count)
    running = jnp.cumsum(by_block(prompt_decay, seq_count, block_count), axis=2)
    block_total = running[:, :, BLOCK - 1]
    row_pos = lax.broadcasted_iota(jnp.int32, (BLOCK, BLOCK), 0)
    col_pos = lax.broadcasted_iota(jnp.int32, (BLOCK, BLOCK), 1)
    log_gap = jnp.where(
        col_pos <= row_pos, running[:, :, :, None] - running[:, :, None, :], -jnp.inf
    )
    scores = jnp.einsum("fqn,fkn->fqk", c_blocks, b_blocks, preferred_element_type=jnp.float32)
    mix_weights = (scores[:, None] * jnp.exp(log_gap) * step_blocks[:, :, None, :]).astype(
        jnp.bfloat16
    )
    y_inner = jnp.einsum(
        "fhqk,fkhp->fqhp", mix_weights, x_blocks, preferred_element_type=jnp.float32
    )
    to_end = jnp.transpose(step_blocks * jnp.exp(block_total[:, :, None] - running), (0, 2, 1))
    scaled_x = (x_blocks * to_end[:, :, :, None]).astype(jnp.bfloat16)
    end_states = jnp.einsum(
        "fkhp,fkn->fhpn", scaled_x, b_blocks, preferred_element_type=jnp.float32
    )
    end_states = end_states.reshape(seq_count, block_count, head_count, head_dim, state_dim)
    block_logs = block_total.reshape(seq_count, block_count, head_count)
    run_log = jnp.zeros((seq_count, head_count), jnp.float32)
    run_state = jnp.zeros((seq_count, head_count, head_dim, state_dim), jnp.float32)
    before_log = []
    before_state = []
    for block_index in range(block_count):
        before_log.append(run_log)
        before_state.append(run_state)
        run_state = (
            jnp.exp(block_logs[:, block_index])[:, :, None, None] * run_state
            + end_states[:, block_index]
        )
        run_log = run_log + block_logs[:, block_index]
    incoming = entering_2(
        (run_log, run_state),
        CTX,
        combine_pair,
        (jnp.zeros_like(run_log), jnp.zeros_like(run_state)),
    )[1]
    entering_list = []
    for block_index in range(block_count):
        entering_list.append(
            jnp.exp(before_log[block_index])[:, :, None, None] * incoming
            + before_state[block_index]
        )
    entering = (
        jnp.stack(entering_list, axis=1)
        .reshape(flat_count, head_count, head_dim, state_dim)
        .astype(jnp.bfloat16)
    )
    y_carry = jnp.einsum("fqn,fhpn->fqhp", c_blocks, entering, preferred_element_type=jnp.float32)
    growth = jnp.transpose(jnp.exp(running), (0, 2, 1))[:, :, :, None]
    prompt_y = y_inner + growth * y_carry + skip_weight[None, None, :, None] * x_blocks
    prompt_y = prompt_y.astype(jnp.bfloat16).reshape(seq_count, tok_count, feature_width)
    later_log = prefix(run_log, CTX, add_logs, jnp.zeros_like(run_log))
    weighted = jnp.exp(later_log)[:, :, None, None] * run_state
    owned_state = sent_and_summed(weighted, CTX, 2)
    row_count = decode_x.shape[1]
    state_rows = jnp.repeat(owned_state, row_count // seq_count, axis=0)
    mask_bits = (
        (
            jnp.right_shift(mask_words[:, :, None], jnp.arange(32, dtype=jnp.int32)[None, None, :])
            & 1
        )
        .reshape(mask_words.shape[0], -1)
        .astype(jnp.float32)
    )
    vocab_local = lm_head.shape[1]
    first_column = (lax.axis_index(CTX) * lax.axis_size(GRP) + lax.axis_index(GRP)) * vocab_local
    columns = first_column + jnp.arange(vocab_local, dtype=jnp.int32)
    state_range = jnp.arange(mask_words.shape[0], dtype=jnp.int32)
    logprob_rows = []
    for step_index in range(STEPS):
        decay_now = jnp.exp(decode_decay[step_index])
        inject = (decode_step[step_index][:, :, None] * decode_x[step_index])[
            :, :, :, None
        ] * decode_b[step_index][:, None, None, :]
        state_rows = decay_now[:, :, None, None] * state_rows + inject
        step_y = jnp.einsum(
            "rhpn,rn->rhp",
            state_rows,
            decode_c[step_index].astype(jnp.float32),
            precision=lax.Precision.HIGHEST,
        )
        step_y = (step_y + skip_weight[None, :, None] * decode_x[step_index]).astype(jnp.bfloat16)
        partial_value = jnp.einsum(
            "rhp,hpd->rd", step_y, out_proj, preferred_element_type=jnp.float32
        )
        layer_out = lax.psum(partial_value, CTX_GRP)
        normed = (
            layer_out
            * lax.rsqrt(jnp.mean(layer_out * layer_out, axis=1, keepdims=True) + EPS)
            * norm_gain
        ).astype(jnp.bfloat16)
        logits = jnp.dot(normed, lm_head, preferred_element_type=jnp.float32)
        onehot = (state_ids[step_index][:, None] == state_range[None, :]).astype(jnp.float32)
        allowed = jnp.dot(onehot, mask_bits, precision=lax.Precision.HIGHEST) > 0.5
        row_max = jnp.max(jnp.where(allowed, logits, NEG_BIG), axis=1)
        row_total = jnp.sum(jnp.where(allowed, jnp.exp(logits - row_max[:, None]), 0.0), axis=1)
        picked = jnp.sum(
            jnp.where(columns[None, :] == chosen[step_index][:, None], logits, 0.0), axis=1
        )
        joint_max, joint_total, joint_pick = combined_by_axis(
            (row_max, row_total, picked), CTX_GRP, merge_parts
        )
        logprob_rows.append(joint_pick - joint_max - jnp.log(joint_total))
    return (prompt_y, state_rows, jnp.stack(logprob_rows))


def solution(mesh):
    finer = Mesh(mesh.devices.reshape(8, 2, 2, 4, 2), ("ctx_0", "ctx_1", "ctx_2", "grp_0", "grp_1"))
    in_specs = (
        P(None, CTX, GRP),
        P(None, CTX, GRP),
        P(None, CTX, GRP),
        P(None, GRP, CTX),
        P(None, GRP, CTX),
        P(GRP),
        P(None, None, GRP, CTX),
        P(None, None, GRP),
        P(None, None, GRP),
        P(None, None, GRP),
        P(None, None, GRP),
        P(GRP, CTX, None),
        P(),
        P(None, CTX_GRP),
        P(None, CTX_GRP),
        P(),
        P(),
    )
    out_specs = (P(None, CTX, GRP), P(None, GRP, CTX, None), P())
    return jax.shard_map(body, mesh=finer, in_specs=in_specs, out_specs=out_specs, check_vma=False)
```

profile of v0, /device:TPU:2, one launch (start us, length us, event | category | flops | bytes accessed | tf_op | source)
XLA Modules:
  0.0 889.0 jit_solution(14336859841816264910)
XLA Ops:
  12.3 6.4 reshape.5087
  18.7 4.8 copy.169
  32.5 20.2 %all-gather.46.cloned.1.call-done = f32[2,2,16,64,256]{4,3,2,1,0:T(8,128)} async-done(((f32[1,2,16,64,256]{4,3,2,1,0:T(8,128)}), f32[2,2,16,64,256]{4,3,2,1,0:T(8,128)}) %all-gather.46.cloned.1.call-update) | async-done | bytes 4194320 | tf_op jit(solution)/shard_map/all_gather | solution.py:29
  60.2 4.7 all-gather.21
  65.0 57.3 %all-gather.48.cloned.1.call-done = f32[2,2,16,64,256]{4,3,2,1,0:T(8,128)} async-done(((f32[1,2,16,64,256]{4,3,2,1,0:T(8,128)}), f32[2,2,16,64,256]{4,3,2,1,0:T(8,128)}) %all-gather.48.cloned.1.call-update) | async-done | bytes 4194320 | tf_op jit(solution)/shard_map/all_gather | solution.py:29
  130.4 8.8 all-to-all-start
  139.2 16.5 %all_gather.146 = f32[8,2,16]{2,1,0:T(2,128)S(1)} all-gather(f32[1,2,16]{2,1,0:T(2,128)S(1)} %bitcast.1630), channel_id=1, replica_groups=mesh['ctx_0'=8,'ctx_1'=2,'ctx_2'=2,'grp_0'=4,'grp_1'=2] {'ctx_0'}, dimensions={0}, use_global_device_ids=true | all-gather | bytes 1152 | tf_op jit(solution)/shard_map/all_gather | solution.py:29
  160.2 144.6 %all-gather.50.cloned.1.call-done = f32[8,2,16,64,256]{4,3,2,1,0:T(8,128)} async-done(((f32[1,2,16,64,256]{4,3,2,1,0:T(8,128)}), f32[8,2,16,64,256]{4,3,2,1,0:T(8,128)}) %all-gather.50.cloned.1.call-update) | async-done | bytes 16777232 | tf_op jit(solution)/shard_map/all_gather | solution.py:29
  304.8 9.2 %fusion.362 = (f32[1,2,16,64,256]{4,3,2,1,0:T(8,128)S(1)}, f32[1,2,16,64,256]{4,3,2,1,0:T(8,128)S(1)}, f32[1,2,16,64,256]{4,3,2,1,0:T(8,128)S(1)}, f32[1,2,16,64...) fusion(f32[8,2,16,64,256]{4,3,2,1,0:T(8,128)} %all-gather.50.cl, ...), kind=kLoop, calls=%fused_computation.701 | loop fusion | bytes 33554432 | tf_op jit(solution)/shard_map/slice | solution.py:33
  314.8 19.7 %fusion.360 = (bf16[2,1,16,64,256]{4,2,3,0,1:T(8,128)(2,1)}, f32[2,1,16,64,256]{4,2,3,0,1:T(8,128)S(1)}) fusion(pred[]{:T(512)S(6)} %gt.61, f32[1,2,16,64,256]{4,3,2,1,0:T(8,128)S(1)} %copy-done.3, f32[1,2,16,64,256]{4,3,2,1,0:T(8,128)S(1)} %get-tuple-element.79, f32[2,16]{1,0:T(2,128)S(1)} %bitcast.1618, f32[2,16]{1,0:T(2,128)S(1)} %bitcast.1620, ...), kind=kLoop, calls=%fused_computation.700 | loop fusion | flops 19922944 | bytes 28313356 | tf_op jit(solution)/shard_map/convert.8
  343.5 6.0 all-to-all-start.1
  359.8 39.9 %all-to-all-done.1 = f32[32,2,16,2,256]{4,3,2,1,0:T(2,128)S(1)} async-done(((f32[32,2,16,2,256]{4,3,2,1,0:T(2,128)}), f32[32,2,16,2,256]{4,3,2,1,0:T(2,128)S(1)}, u32[]{:S(2)}, u32[]{:S(2)}) %all-to-all-start.1) | async-done | bytes 2097184 | tf_op jit(solution)/shard_map/all_to_all | solution.py:73
  400.6 7.6 multiply_add_fusion.2
  427.7 5.6 fusion.9
  433.3 4.8 copy.225
  438.0 6.7 reshape.5086
  444.8 247.4 %all-reduce.3.cloned.1.call-done = (f32[32,8192]{1,0:T(8,128)}, f32[32,8192]{1,0:T(8,128)}, f32[32,8192]{1,0:T(8,128)}, f32[32,8192]{1,0:T(8,128)}) async-done(((f32[32,8192]{1,0:T(8,128)}, f32[32,8192]{1,0:T(8,128)}, f32[32,8192]{1,0:T(8,128)}, f32[32,8192]{1,0:T(8,128)}), (f32[32,8192]{1,0:T(8,128)}, f32[32,8192]{1,0:T(8,128)}, f32[32,8192]{1,0:T(8,128)}, ...) | async-done | bytes 4194320 | tf_op jit(solution)/shard_map/psum | solution.py:242
  703.3 23.0 %all-gather.22 = f32[8,3,32]{2,1,0:T(4,128)S(1)} all-gather(f32[1,3,32]{2,1,0:T(4,128)S(1)} %maximum_bitcast_fusion), channel_id=3, replica_groups=mesh['ctx_0'=8,'ctx_1'=2,'ctx_2'=2,'grp_0'=4,'grp_1'=2] {'ctx_0'}, dimensions={0}, use_global_device_ids=true | all-gather | bytes 3456 | tf_op jit(solution)/shard_map/all_gather | solution.py:85
  726.3 4.4 all-gather.23
  732.6 10.4 %all-gather.25 = f32[4,3,32]{2,1,0:T(4,128)S(1)} all-gather(f32[1,3,32]{2,1,0:T(4,128)S(1)} %maximum_bitcast_fusion.3), channel_id=6, replica_groups=mesh['ctx_0'=8,'ctx_1'=2,'ctx_2'=2,'grp_0'=4,'grp_1'=2] {'grp_0'}, dimensions={0}, use_global_device_ids=true | all-gather | bytes 1920 | tf_op jit(solution)/shard_map/all_gather | solution.py:85
  743.1 21.3 %all-gather.27 = f32[8,3,32]{2,1,0:T(4,128)S(1)} all-gather(f32[1,3,32]{2,1,0:T(4,128)S(1)} %maximum_bitcast_fusion.5), channel_id=8, replica_groups=mesh['ctx_0'=8,'ctx_1'=2,'ctx_2'=2,'grp_0'=4,'grp_1'=2] {'ctx_0'}, dimensions={0}, use_global_device_ids=true | all-gather | bytes 3456 | tf_op jit(solution)/shard_map/all_gather | solution.py:85
  764.4 4.4 all-gather.28
  770.7 10.6 %all-gather.30 = f32[4,3,32]{2,1,0:T(4,128)S(1)} all-gather(f32[1,3,32]{2,1,0:T(4,128)S(1)} %maximum_bitcast_fusion.8), channel_id=11, replica_groups=mesh['ctx_0'=8,'ctx_1'=2,'ctx_2'=2,'grp_0'=4,'grp_1'=2] {'grp_0'}, dimensions={0}, use_global_device_ids=true | all-gather | bytes 1920 | tf_op jit(solution)/shard_map/all_gather | solution.py:85
  781.4 21.4 %all-gather.32 = f32[8,3,32]{2,1,0:T(4,128)S(1)} all-gather(f32[1,3,32]{2,1,0:T(4,128)S(1)} %maximum_bitcast_fusion.10), channel_id=13, replica_groups=mesh['ctx_0'=8,'ctx_1'=2,'ctx_2'=2,'grp_0'=4,'grp_1'=2] {'ctx_0'}, dimensions={0}, use_global_device_ids=true | all-gather | bytes 3456 | tf_op jit(solution)/shard_map/all_gather | solution.py:85
  802.8 4.4 all-gather.33
  809.1 10.4 %all-gather.35 = f32[4,3,32]{2,1,0:T(4,128)S(1)} all-gather(f32[1,3,32]{2,1,0:T(4,128)S(1)} %maximum_bitcast_fusion.13), channel_id=16, replica_groups=mesh['ctx_0'=8,'ctx_1'=2,'ctx_2'=2,'grp_0'=4,'grp_1'=2] {'grp_0'}, dimensions={0}, use_global_device_ids=true | all-gather | bytes 1920 | tf_op jit(solution)/shard_map/all_gather | solution.py:85
  819.6 21.3 %all-gather.37 = f32[8,3,32]{2,1,0:T(4,128)S(1)} all-gather(f32[1,3,32]{2,1,0:T(4,128)S(1)} %maximum_bitcast_fusion.15), channel_id=18, replica_groups=mesh['ctx_0'=8,'ctx_1'=2,'ctx_2'=2,'grp_0'=4,'grp_1'=2] {'ctx_0'}, dimensions={0}, use_global_device_ids=true | all-gather | bytes 3456 | tf_op jit(solution)/shard_map/all_gather | solution.py:85
  847.3 10.6 %all-gather.40 = f32[4,3,32]{2,1,0:T(4,128)S(1)} all-gather(f32[1,3,32]{2,1,0:T(4,128)S(1)} %maximum_bitcast_fusion.18), channel_id=21, replica_groups=mesh['ctx_0'=8,'ctx_1'=2,'ctx_2'=2,'grp_0'=4,'grp_1'=2] {'grp_0'}, dimensions={0}, use_global_device_ids=true | all-gather | bytes 1920 | tf_op jit(solution)/shard_map/all_gather | solution.py:85
  857.9 5.9 all-gather.26
  863.8 5.9 all-gather.31
  869.7 5.9 all-gather.36
  875.6 5.9 all-gather.41
  (271 shorter events, 97.8 us)
Async XLA Ops:
  7.2 17.3 %copy-start = (bf16[2,512,256]{2,1,0:T(8,128)(2,1)S(1)}, bf16[2,512,256]{2,1,0:T(8,128)(2,1)}, u32[]{:S(2)}) copy-start(bf16[2,512,256]{2,1,0:T(8,128)(2,1)} %param.18) | copy-start | bytes 1572868
  7.2 45.5 %all-gather.46.cloned.1.call-start = ((), (), s32[]{:S(2)}) async-start(), calls=%async_computation.2 | async-start | bytes 6291456 | tf_op jit(solution)/shard_map/all_gather | solution.py:29
  25.7 2.4 copy-start.8
  25.7 2.4 copy-start.9
  30.6 91.7 %all-gather.48.cloned.1.call-start = ((), (), s32[]{:S(2)}) async-start(), calls=%async_computation.3 | async-start | bytes 6291456 | tf_op jit(solution)/shard_map/all_gather | solution.py:29
  60.2 244.6 %all-gather.50.cloned.1.call-start = ((), (), s32[]{:S(2)}) async-start(), calls=%async_computation.4 | async-start | bytes 18874368 | tf_op jit(solution)/shard_map/all_gather | solution.py:29
  124.8 2.3 copy-start.4
  130.4 29.7 %all-to-all-start = ((f32[32,2,16]{2,1,0:T(2,128)}), f32[32,2,16]{2,1,0:T(2,128)S(1)}, u32[]{:S(2)}, u32[]{:S(2)}) async-start(f32[32,2,16]{2,1,0:T(2,128)} %broadcast_in_dim.43), calls=%async_computation | async-start | bytes 65536 | tf_op jit(solution)/shard_map/all_to_all | solution.py:41
  304.8 9.2 %copy-start.3 = (f32[1,2,16,64,256]{4,3,2,1,0:T(8,128)S(1)}, f32[1,2,16,64,256]{4,3,2,1,0:T(8,128)}, u32[]{:S(2)}) copy-start(f32[1,2,16,64,256]{4,3,2,1,0:T(8,128)} %copy-done.2) | copy-start | bytes 6291460
  304.8 9.2 %copy-start.5 = (f32[1,2,16,64,256]{4,3,2,1,0:T(8,128)S(1)}, f32[1,2,16,64,256]{4,3,2,1,0:T(8,128)}, u32[]{:S(2)}) copy-start(f32[1,2,16,64,256]{4,3,2,1,0:T(8,128)} %copy-done.4) | copy-start | bytes 6291460
  304.8 10.0 %copy-start.7 = (f32[1,2,16,64,256]{4,3,2,1,0:T(8,128)S(1)}, f32[1,2,16,64,256]{4,3,2,1,0:T(8,128)}, u32[]{:S(2)}) copy-start(f32[1,2,16,64,256]{4,3,2,1,0:T(8,128)} %copy-done.6) | copy-start | bytes 6291460
  314.8 19.7 %copy-start.10 = (f32[2,1,16,64,256]{4,3,2,1,0:T(8,128)S(1)}, f32[2,1,16,64,256]{4,3,2,1,0:T(8,128)}, u32[]{:S(2)}) copy-start(f32[2,1,16,64,256]{4,3,2,1,0:T(8,128)} %copy-done.9) | copy-start | bytes 6291460
  334.5 2.6 copy-start.14
  343.5 6.2 copy-start.34
  343.5 6.2 copy-start.28
  343.5 9.1 %copy-start.35 = (f32[4,32,16]{1,2,0:T(8,128)S(1)}, f32[4,32,16]{1,2,0:T(8,128)}, u32[]{:S(2)}) copy-start(f32[4,32,16]{1,2,0:T(8,128)} %param.27) | copy-start | bytes 24580
  343.5 11.8 %copy-start.37 = (s32[16,8]{0,1:T(8,128)S(1)}, s32[16,8]{0,1:T(8,128)}, u32[]{:S(2)}) copy-start(s32[16,8]{0,1:T(8,128)} %param.31) | copy-start | bytes 1540
  343.5 14.0 %copy-start.42 = (s32[4,32]{1,0:T(4,128)S(1)}, s32[4,32]{1,0:T(4,128)}, u32[]{:S(2)}) copy-start(s32[4,32]{1,0:T(4,128)} %param.32) | copy-start | bytes 1540
  343.5 14.5 %copy-start.43 = (s32[4,32]{1,0:T(4,128)S(1)}, s32[4,32]{1,0:T(4,128)}, u32[]{:S(2)}) copy-start(s32[4,32]{1,0:T(4,128)} %param.33) | copy-start | bytes 1540
  343.5 15.1 %copy-start.31 = (bf16[4,32,256]{2,1,0:T(8,128)(2,1)S(1)}, bf16[4,32,256]{2,1,0:T(8,128)(2,1)}, u32[]{:S(2)}) copy-start(bf16[4,32,256]{2,1,0:T(8,128)(2,1)} %param.25) | copy-start | bytes 196612
  343.5 15.7 %copy-start.30 = (bf16[4,32,256]{2,1,0:T(8,128)(2,1)S(1)}, bf16[4,32,256]{2,1,0:T(8,128)(2,1)}, u32[]{:S(2)}) copy-start(bf16[4,32,256]{2,1,0:T(8,128)(2,1)} %param.24) | copy-start | bytes 196612
  343.5 56.2 %all-to-all-start.1 = ((f32[32,2,16,2,256]{4,3,2,1,0:T(2,128)}), f32[32,2,16,2,256]{4,3,2,1,0:T(2,128)S(1)}, u32[]{:S(2)}, u32[]{:S(2)}) async-start(f32[32,2,16,2,256]{4,3,2,1,0:T(2,128)} %copy.196), calls=%async_computation.1 | async-start | bytes 4194304 | tf_op jit(solution)/shard_map/all_to_all | solution.py:73
  349.6 342.7 %all-reduce.3.cloned.1.call-start = ((), (), s32[]{:S(2)}) async-start(), calls=%async_computation.5 | async-start | bytes 8388608 | tf_op jit(solution)/shard_map/psum | solution.py:242
  400.6 7.7 copy-start.27
  408.2 9.4 %copy-start.16 = (f32[32,16,2,256]{3,2,1,0:T(2,128)}, f32[32,16,2,256]{3,2,1,0:T(2,128)S(1)}, u32[]{:S(2)}) copy-start(f32[32,16,2,256]{3,2,1,0:T(2,128)S(1)} %get-tuple-element.62) | copy-start | bytes 3145732
  408.2 5.4 copy-start.26
  408.3 9.4 %copy-start.29 = (bf16[4,32,16,2]{1,3,2,0:T(2,128)(2,1)S(1)}, bf16[4,32,16,2]{1,3,2,0:T(2,128)(2,1)}, u32[]{:S(2)}) copy-start(bf16[4,32,16,2]{1,3,2,0:T(2,128)(2,1)} %param.23) | copy-start | bytes 24580
  408.3 9.4 %copy-start.45 = (f32[16]{0:T(128)S(1)}, f32[16]{0:T(128)}, u32[]{:S(2)}) copy-start(f32[16]{0:T(128)} %param.22) | copy-start | bytes 196
  410.2 7.6 copy-start.11
  444.8 249.3 %copy-start.23 = (f32[8192]{0:T(1024)S(1)}, f32[8192]{0:T(1024)}, u32[]{:S(2)}) copy-start(f32[8192]{0:T(1024)} %param.29) | copy-start | bytes 98308
  694.1 3.5 copy-start.1
  694.2 3.7 copy-start.19
  (24 other events, 38.5 us)
Sparse Core Ops, SparseCore 0:
  30.7 21.9 all-gather.45
  60.3 61.9 all-gather.47
  129.8 174.8 all-gather.49
  423.6 268.6 all-reduce.2
where the time goes:
time: 899 us; the launch traced here: 889 us
  waiting for transfers between devices  510 us (57%)
  blocking collectives  200 us (22%)
  local copies, waits for them, and re-layouts  69.7 us (8%)
  other arithmetic  50 us (6%)
  matrix products  29.1 us (3%)
  between operations  15.3 us (2%)
  starting transfers between devices  15.1 us (2%)
    psum x1, waiting for transfers between devices, body(): layer_out = lax.psum(partial_value, CTX_GRP)  247 us
    all_gather x3, waiting for transfers between devices, entering_2(): pieces = jax.tree.map(lambda part: lax.all_gather(part, axis), total)  222 us
    all_gather x20, blocking collectives, gathered_once(): both, at, found = (lax.all_gather(jnp.concatenate(lines), axis), 0, {})  177 us
    all_to_all x1, waiting for transfers between devices, sent_and_summed(): lax.all_to_all(pieces, axis, split_axis=0, concat_axis=0, tiled=True)  39.9 us
    all_gather x3, blocking collectives, entering_2(): pieces = jax.tree.map(lambda part: lax.all_gather(part, axis), total)  23 us
    another operation x5, other arithmetic  22.1 us
    unnamed x104, local copies, waits for them, and re-layouts  20.7 us
  transfers between devices with their start and end apart: 6, of which 5 were waited for; matrix products, arithmetic and copies ran while one was open for 4% of the time, Pallas kernels for 0%

commit v1 on v0

v1 whole, which is shorter than its diff:
```python
import jax
import jax.numpy as jnp
import numpy as np
from jax import lax
from jax.experimental import pallas as pl
from jax.experimental.pallas import tpu as pltpu
from jax.sharding import Mesh
from jax.sharding import PartitionSpec as P

BLOCK = 256
STEPS = 4
Z, XL, CO, Y, XH = "z", "xl", "co", "y", "xh"
CTX = (Z, XL, CO)
GRP = (Y, XH)
ALL = (Z, XL, CO, Y, XH)
ZX = (Z, XL)
CG = (CO, Y, XH)

NEG_BIG = -1e30
EPS = 1e-05
F32 = jnp.float32
BF16 = jnp.bfloat16
HI = lax.Precision.HIGHEST


def size_of(axes):
    return int(np.prod([lax.axis_size(a) for a in axes]))


def iota(shape, dim):
    return lax.broadcasted_iota(jnp.int32, shape, dim)


def dot(a, b, dims, precision=None):
    return lax.dot_general(a, b, (dims, ((), ())), precision=precision, preferred_element_type=F32)


def swapped(value):
    return lax.ppermute(value, CO, [(0, 1), (1, 0)])


def told(value, axes):
    many = size_of(axes)
    return lax.all_to_all(
        jnp.broadcast_to(value[None], (many, *value.shape)), axes, 0, 0, tiled=True
    )


def column(row, rows, per):
    width = row.shape[1]
    pick = iota((rows, width), 1) == iota((rows, width), 0) // per
    return jnp.sum(jnp.where(pick, row, 0.0), axis=1, keepdims=True)


def local_index(feature, my_core, head_dim, zx, p2, heads):
    h, p = feature // head_dim, feature % head_dim
    chip, rest = p // (2 * p2), p % (2 * p2)
    side = (rest // p2) ^ my_core
    return ((side * zx + chip) * heads + h) * p2 + rest % p2


def states_kernel(zx, p2, core, x, b, step, decay, e0, keep, send, run_out, logs):
    tokens, width = x.shape[1], x.shape[2]
    heads = step.shape[1]
    head_dim = width // heads
    half = width // 2
    blocks = tokens // BLOCK
    upper = (iota((BLOCK, BLOCK), 0) <= iota((BLOCK, BLOCK), 1)).astype(F32)
    expand = (iota((heads, width), 1) // head_dim == iota((heads, width), 0)).astype(F32)
    goes = local_index(iota((1, width), 1), core[0], head_dim, zx, p2, heads)
    perm_t = (iota((width, width), 0) == goes).astype(BF16)
    of_row = (iota((width, heads), 0) // p2 % heads == iota((width, heads), 1)).astype(F32)
    lane = iota((heads, BLOCK), 1) == iota((heads, BLOCK), 0)
    state = None
    total_row = jnp.zeros((1, BLOCK), F32)
    for k in range(blocks):
        at = slice(k * BLOCK, (k + 1) * BLOCK)
        run = dot(decay[0, :, at], upper, ((1,), (0,)), HI)
        run_out[0, :, at] = run
        total = jnp.broadcast_to(run[:, BLOCK - 1 :], (heads, BLOCK))
        to_end = step[0, :, at] * jnp.exp(total - run)
        spread = dot(to_end.T, expand, ((1,), (0,)), HI)
        scaled = (x[0, at].astype(F32) * spread).astype(BF16)
        moved = dot(perm_t, scaled, ((1,), (1,))).astype(BF16)
        own = dot(moved, b[0, at], ((1,), (0,)))
        total_row = total_row + jnp.sum(jnp.where(lane, total, 0.0), axis=0, keepdims=True)
        if k == 0:
            state = own
            e0[0] = own
            logs[0] = jnp.broadcast_to(total_row, (8, BLOCK))
        else:
            state = dot(of_row, jnp.exp(total), ((1,), (0,)), HI) * state + own
    keep[0] = state[:half]
    send[0, :half] = state[half:]
    send[0, half:] = jnp.broadcast_to(total_row, (8, BLOCK))


def pair_kernel(zx, p2, heads, core, keep, own_log, came, out):
    rows = heads * p2
    first = core[0] == 0
    half = zx * rows
    for s in range(keep.shape[0]):
        mine = own_log[s, :1]
        other = came[s, half : half + 1]
        f_mine = jnp.where(first, jnp.exp(column(other, rows, p2)), 1.0)
        f_came = jnp.where(first, 1.0, jnp.exp(column(mine, rows, p2)))
        for k in range(zx):
            at = slice(k * rows, (k + 1) * rows)
            out[k, s * rows : (s + 1) * rows] = f_mine * keep[s, at] + f_came * came[s, at]
            out[k, 2 * rows + s * 4 : 2 * rows + s * 4 + 4] = jnp.broadcast_to(
                mine + other, (4, mine.shape[1])
            )


def scan_kernel(
    p2, heads, pieces, c_q, b_q, cum, x_q, step_q, skip_col, enter, step_y, row_state
):
    zx = pieces.shape[0]
    rows = heads * p2
    many = x_q.shape[1]
    half = many // 2
    per = half // STEPS
    final = jnp.zeros((2 * rows, pieces.shape[2]), F32)
    for k in range(zx):
        enter[k] = final
        fac = jnp.concatenate(
            [
                jnp.exp(column(pieces[k, 2 * rows + 4 * s : 2 * rows + 4 * s + 1], rows, p2))
                for s in range(2)
            ],
            axis=0,
        )
        final = fac * final + pieces[k, : 2 * rows]
    cums = cum[...]
    grow = jnp.exp(cums)
    xs = x_q[...] * step_q[...] * jnp.exp(-cums)
    c_all = c_q[...].astype(F32)
    b_all = b_q[...].astype(F32)
    from_state = [
        dot(final[s * rows : (s + 1) * rows], c_all, ((1,), (1,)), HI) for s in range(2)
    ]
    lane = iota((rows, many), 1)
    seen = jnp.where(lane < half, from_state[0], from_state[1])
    cross = dot(b_all, c_all, ((1,), (1,)), HI)
    earlier, later = iota((many, many), 0), iota((many, many), 1)
    same = (earlier // half == later // half) & (earlier % per == later % per)
    cross = jnp.where(same & (earlier <= later), cross, 0.0)
    seen = seen + dot(xs, cross, ((1,), (0,)), HI)
    y = grow * seen + skip_col[...] * x_q[...]
    step_y[...] = y.astype(BF16).astype(F32)
    for s in range(2):
        for r in range(per):
            value = final[s * rows : (s + 1) * rows]
            for i in range(STEPS):
                q = s * half + i * per + r
                value = value + xs[:, q : q + 1] * b_all[q : q + 1]
            row_state[s * per + r] = grow[:, q : q + 1] * value


def project_kernel(y, w, out):
    groups, rows, many = y.shape
    left = y[...].reshape(groups * rows, many).T.astype(BF16)
    right = w[...].reshape(groups * rows, w.shape[2]).astype(BF16)
    out[...] = dot(left, right, ((1,), (0,)))


def logits_kernel(core, own, other, gain, head, allowed, chosen, out):
    blocks, many, width = own.shape
    half = blocks * width
    total = jnp.zeros((many, 1), F32)
    for ref in (own, other):
        for k in range(blocks):
            part = ref[k]
            total = total + jnp.sum(part * part, axis=1, keepdims=True)
    scale = lax.rsqrt(total / (2 * half) + EPS)
    acc = jnp.zeros((head.shape[1], many), F32)
    for side, ref in enumerate((own, other)):
        start = (core[0] ^ side) * half
        for k in range(blocks):
            at = pl.ds(pl.multiple_of(start + k * width, width), width)
            normed = (ref[k] * scale * gain[:, at]).astype(BF16)
            acc = acc + dot(head[at], normed, ((0,), (1,)))
    ok = allowed[...] > 0.5
    top = jnp.max(jnp.where(ok, acc, NEG_BIG), axis=0, keepdims=True)
    total = jnp.sum(jnp.where(ok, jnp.exp(acc - top), 0.0), axis=0, keepdims=True)
    hit = iota(acc.shape, 0) == chosen[...]
    picked = jnp.sum(jnp.where(hit, acc, 0.0), axis=0, keepdims=True)
    out[0:1] = top
    out[1:2] = total
    out[2:3] = picked
    out[3:8] = jnp.zeros((5, many), F32)


def outputs_kernel(zx, p2, core, x, b, c, step, run, logs, own, other, e0, skip, out):
    width = x.shape[2]
    heads = step.shape[1]
    head_dim = width // heads
    rows = heads * p2
    k = pl.program_id(1)
    xb, cb = x[0], c[0]
    running, steps = run[0], step[0]
    run_t = running.T
    causal = iota((BLOCK, BLOCK), 1) <= iota((BLOCK, BLOCK), 0)
    scores = jnp.where(causal, dot(cb, b[0], ((1,), (1,))), 0.0)
    enter = jnp.concatenate(
        [own[:, 0].reshape(zx * rows, -1), other[:, 0].reshape(zx * rows, -1)], axis=0
    )
    fade = jnp.where(k == 0, 1.0, jnp.exp(column(logs[0, :1], rows, p2)))
    later = jnp.where(k == 0, 0.0, 1.0)
    n = enter.shape[1]
    enter = (enter.reshape(2 * zx, rows, n) * fade[None]).reshape(width, n) + later * e0[0]
    goes = local_index(iota((width, 1), 0), core[0], head_dim, zx, p2, heads)
    perm = (iota((width, width), 1) == goes).astype(BF16)
    enter = dot(perm, enter.astype(BF16), ((1,), (0,))).astype(BF16)
    carry = dot(cb, enter, ((1,), (1,)))
    expand = (iota((heads, width), 1) // head_dim == iota((heads, width), 0)).astype(F32)
    growth = dot(jnp.exp(run_t), expand, ((1,), (0,)), HI)
    base = growth * carry + skip[...] * xb.astype(F32)
    pair = 2 * head_dim
    left = iota((BLOCK, pair), 1) < head_dim
    for j in range(heads // 2):
        at = slice(j * pair, (j + 1) * pair)
        halves = []
        for h in (2 * j, 2 * j + 1):
            gap = jnp.minimum(run_t[:, h : h + 1] - running[h : h + 1], 0.0)
            mix = (scores * jnp.exp(gap) * steps[h : h + 1]).astype(BF16)
            halves.append(dot(mix, xb[:, at], ((1,), (0,))))
        inner = jnp.where(left, halves[0], halves[1])
        out[0, :, at] = (inner + base[:, at]).astype(BF16)


def merge(parts):
    top = jnp.max(parts[:, 0], axis=0)
    total = jnp.sum(parts[:, 1] * jnp.exp(parts[:, 0] - top), axis=0)
    picked = jnp.sum(parts[:, 2], axis=0)
    return top, total, picked


def full(shape):
    return pl.BlockSpec(shape, lambda *_: (0,) * len(shape))


def call(kernel, outs, name, *args, smem=(), limit=None):
    specs = [
        pl.BlockSpec(memory_space=pltpu.SMEM) if k in smem else full(a.shape)
        for k, a in enumerate(args)
    ]
    many = isinstance(outs, tuple)
    return pl.pallas_call(
        kernel,
        grid=(1,),
        in_specs=specs,
        out_specs=tuple(full(o.shape) for o in outs) if many else full(outs.shape),
        out_shape=outs,
        name=name,
    )(*args)


def shaped(*shape, dtype=F32):
    return jax.ShapeDtypeStruct(shape, dtype)


def body(
    prompt_x,
    prompt_b,
    prompt_c,
    prompt_step,
    prompt_decay,
    skip_weight,
    decode_x,
    decode_b,
    decode_c,
    decode_step,
    decode_decay,
    out_proj,
    norm_gain,
    lm_head,
    mask_words,
    state_ids,
    chosen,
):
    seqs, tokens, width = prompt_x.shape
    n = prompt_b.shape[2]
    heads = prompt_step.shape[1]
    zx, cg, grp = size_of(ZX), size_of(CG), size_of(GRP)
    p2 = decode_x.shape[3]
    rows = heads * p2
    half = width // 2
    blocks = tokens // BLOCK
    decode_rows = decode_x.shape[1]
    per = decode_rows // seqs
    many = STEPS * decode_rows
    core = lax.axis_index(CO).astype(jnp.int32)[None]

    model = out_proj.shape[2]
    wide = model // cg
    w_rows = out_proj.astype(F32).reshape(rows, cg, wide).transpose(1, 0, 2)
    w_own = lax.all_to_all(w_rows, CG, 0, 0, tiled=True)

    def by_q(value):
        shape = value.shape[2:]
        value = value.reshape(STEPS, seqs, per, *shape)
        return jnp.moveaxis(value, 1, 0).reshape(many, *shape)

    c_q, b_q = by_q(decode_c), by_q(decode_b)
    cum_q = jnp.repeat(by_q(jnp.cumsum(decode_decay, axis=0)).T, p2, axis=0)
    step_q = jnp.repeat(by_q(decode_step).T, p2, axis=0)
    x_q = by_q(decode_x.astype(F32).reshape(STEPS, decode_rows, rows)).T
    skip_col = jnp.repeat(skip_weight, p2)[:, None]
    vocab = lm_head.shape[1]
    first = (lax.axis_index(CTX) * size_of(GRP) + lax.axis_index(GRP)) * vocab
    chosen_q = (by_q(chosen) - first)[None]
    ids_q = by_q(state_ids)
    bits = (
        jnp.right_shift(mask_words[:, :, None], jnp.arange(32, dtype=jnp.int32)[None, None]) & 1
    ).reshape(mask_words.shape[0], vocab)
    onehot = (ids_q[None] == jnp.arange(mask_words.shape[0])[:, None]).astype(BF16)
    allowed = dot(bits.astype(BF16), onehot, ((0,), (0,)))

    by_s = lambda *shape: pl.BlockSpec((1, *shape), lambda s: (s,) + (0,) * len(shape))
    e0, keep, send, run, logs = pl.pallas_call(
        lambda *refs: states_kernel(zx, p2, *refs),
        grid=(seqs,),
        in_specs=[
            pl.BlockSpec(memory_space=pltpu.SMEM),
            by_s(tokens, width),
            by_s(tokens, n),
            by_s(heads, tokens),
            by_s(heads, tokens),
        ],
        out_specs=(
            by_s(width, n),
            by_s(half, n),
            by_s(half + 8, n),
            by_s(heads, tokens),
            by_s(8, n),
        ),
        out_shape=(
            shaped(seqs, width, n),
            shaped(seqs, half, n),
            shaped(seqs, half + 8, n),
            shaped(seqs, heads, tokens),
            shaped(seqs, 8, n),
        ),
        name="states",
    )(core, prompt_x, prompt_b, prompt_step, prompt_decay)
    came = swapped(send)
    own_log = send[:, half:]
    pieces = call(
        lambda *refs: pair_kernel(zx, p2, heads, *refs),
        shaped(zx, 2 * rows + 8, n),
        "pair",
        core,
        keep,
        own_log,
        came,
        smem=(0,),
    )
    pieces = lax.all_to_all(pieces, ZX, 0, 0, tiled=True)
    enter, step_y, row_state = call(
        lambda *refs: scan_kernel(p2, heads, *refs),
        (shaped(zx, 2 * rows, n), shaped(rows, many), shaped(decode_rows, rows, n)),
        "scan",
        pieces,
        c_q,
        b_q,
        cum_q,
        x_q,
        step_q,
        skip_col,
    )
    decode_state = row_state.reshape(decode_rows, heads, p2, n)

    ys = told(step_y, CG)
    partial = call(project_kernel, shaped(many, wide), "project", ys, w_own)
    partial = lax.all_to_all(partial.reshape(zx, many // zx, wide), ZX, 0, 0, tiled=True)
    summed = jnp.sum(partial, axis=0)
    own_cols = told(summed, ZX).reshape(many, wide)
    own_half = told(own_cols, GRP)
    other_half = swapped(own_half)

    parts = call(
        logits_kernel,
        shaped(8, many),
        "logits",
        core,
        own_half,
        other_half,
        norm_gain[None],
        lm_head,
        allowed,
        chosen_q,
        smem=(0,),
    )
    parts = jnp.stack(merge(told(parts[:3], (Z, CO))))
    top, total, picked = merge(told(parts, (XL, Y, XH)))
    logprob = picked - top - jnp.log(total)
    logprob = logprob.reshape(seqs, STEPS, per).transpose(1, 0, 2).reshape(STEPS, decode_rows)

    back = lax.all_to_all(enter, ZX, 0, 0, tiled=True).reshape(zx, seqs, rows, n)
    is_first = core[0] == 0

    def after(log_row, value, state):
        fade = jnp.exp(jnp.repeat(log_row[:, 0, :heads], p2, axis=1))[None, :, :, None]
        state = state[:, :half].reshape(seqs, zx, rows, n).transpose(1, 0, 2, 3)
        return fade * value + state

    for_me = jnp.where(is_first, back, after(came[:, half:], back, came))
    for_other = jnp.where(is_first, after(own_log, back, keep), back)
    other_side = swapped(for_other)

    at_k = lambda *shape: pl.BlockSpec((1, BLOCK, *shape), lambda s, k: (s, k, 0))
    lanes_k = pl.BlockSpec((1, heads, BLOCK), lambda s, k: (s, 0, k))
    states_s = pl.BlockSpec((zx, 1, rows, n), lambda s, k: (0, s, 0, 0))
    prompt_y = pl.pallas_call(
        lambda *refs: outputs_kernel(zx, p2, *refs),
        grid=(seqs, blocks),
        in_specs=[
            pl.BlockSpec(memory_space=pltpu.SMEM),
            at_k(width),
            at_k(n),
            at_k(n),
            lanes_k,
            lanes_k,
            pl.BlockSpec((1, 8, n), lambda s, k: (s, 0, 0)),
            states_s,
            states_s,
            pl.BlockSpec((1, width, n), lambda s, k: (s, 0, 0)),
            full((1, width)),
        ],
        out_specs=at_k(width),
        out_shape=shaped(seqs, tokens, width, dtype=BF16),
        name="outputs",
    )(
        core,
        prompt_x,
        prompt_b,
        prompt_c,
        prompt_step,
        run,
        logs,
        for_me,
        other_side,
        e0,
        jnp.repeat(skip_weight, width // heads)[None],
    )
    return (prompt_y, decode_state, logprob)


def solution(mesh):
    ctx, grp = mesh.devices.shape
    shape = (ctx // 4, 2, 2, grp // 2, 2)
    finer = Mesh(mesh.devices.reshape(shape), ALL)
    in_specs = (
        P(None, CTX, GRP),
        P(None, CTX, GRP),
        P(None, CTX, GRP),
        P(None, GRP, CTX),
        P(None, GRP, CTX),
        P(GRP),
        P(None, None, GRP, CTX),
        P(None, None, GRP),
        P(None, None, GRP),
        P(None, None, GRP),
        P(None, None, GRP),
        P(GRP, CTX, None),
        P(),
        P(None, ALL),
        P(None, ALL),
        P(),
        P(),
    )
    out_specs = (P(None, CTX, GRP), P(None, GRP, CTX, None), P())
    return jax.shard_map(body, mesh=finer, in_specs=in_specs, out_specs=out_specs, check_vma=False)
```

time: 899 us -> 240 us (0.27)
  waiting for transfers between devices: 510 us -> 59.1 us
  blocking collectives: 200 us -> 85.1 us
  local copies, waits for them, and re-layouts: 69.7 us -> 17.7 us
  other arithmetic: 50 us -> 3.64 us
  Pallas kernels: 0 us -> 43.7 us
  matrix products: 29.1 us -> 0.86 us
  between operations: 15.3 us -> 0.89 us
  starting transfers between devices: 15.1 us -> 27 us
    psum x1 -> x0, waiting for transfers between devices: 247 us -> none  [body(): layer_out = lax.psum(partial_value, CTX_GRP)]
    all_gather x3 -> x0, waiting for transfers between devices: 222 us -> none  [entering_2(): pieces = jax.tree.map(lambda part: lax.all_gather(part, axis), total)]
    all_gather x23 -> x0, blocking collectives: 200 us -> none  [the longest x20 177 us: gathered_once(): both, at, found = (lax.all_gather(jnp.concatenate(lines), axis), 0, {})]
    all_to_all x0 -> x5, blocking collectives: none -> 85.1 us  [the longest x4 69.6 us: told(): lax.all_to_all(jnp.broadcast_to(value[None], (many, *value.shape)), axes,...]
    pallas_call x0 -> x6, Pallas kernels: none -> 43.7 us  [the longest x1 16.9 us: body(): pl.pallas_call(lambda *refs: outputs_kernel(zx, p2, *refs), grid=(seqs, b...]
    dot_general x20 -> x1, matrix products: 29.1 us -> 0.86 us  [dot(): lax.dot_general(a, b, (dims, ((), ())), precision=precision, preferred_el...]
    another operation x7 -> x2, other arithmetic: 22.9 us -> 0.12 us  [the longest x1 0.11 us: body(): cum_q = jnp.repeat(by_q(jnp.cumsum(decode_decay, axis=0)).T, p2, axis=0)]
    unnamed x104 -> x33, local copies, waits for them, and re-layouts: 20.7 us -> 1.14 us
  transfers between devices with their start and end apart: 6 -> 7, of which waited for: 5 -> 4; matrix products, arithmetic and copies ran while one was open for 4% -> 8% of each run, Pallas kernels for 0% -> 11%
where the time goes in v1:
time: 240 us; the launch traced here: 238 us
  blocking collectives  85.1 us (35%)
  waiting for transfers between devices  59.1 us (25%)
  Pallas kernels  43.7 us (18%)
  starting transfers between devices  27 us (11%)
  local copies, waits for them, and re-layouts  17.7 us (7%)
  other arithmetic  3.64 us (2%)
    all_to_all x4, blocking collectives, told(): lax.all_to_all(jnp.broadcast_to(value[None], (many, *value.shape)), axes,...  69.6 us
    all_to_all x1, waiting for transfers between devices, body(): pieces = lax.all_to_all(pieces, ZX, 0, 0, tiled=True)  28.5 us
    all_to_all x1, waiting for transfers between devices, body(): lax.all_to_all(enter, ZX, 0, 0, tiled=True).reshape(zx, seqs, rows, n)  21.6 us
    pallas_call x1, Pallas kernels, body(): pl.pallas_call(lambda *refs: outputs_kernel(zx, p2, *refs), grid=(seqs, b...  16.9 us
    all_to_all x1, blocking collectives, body(): lax.all_to_all(partial.reshape(zx, many // zx, wide), ZX, 0, 0, tiled=True)  15.5 us
    pallas_call x4, Pallas kernels, call(): pl.pallas_call(kernel, grid=(1,), in_specs=specs, out_specs=tuple((full(o...  14.9 us
    pallas_call x1, Pallas kernels, body(): pl.pallas_call(lambda *refs: states_kernel(zx, p2, *refs), grid=(seqs,),...  11.9 us
    all_to_all x1, starting transfers between devices, body(): pieces = lax.all_to_all(pieces, ZX, 0, 0, tiled=True)  9.94 us
  transfers between devices with their start and end apart: 7, of which 4 were waited for; matrix products, arithmetic and copies ran while one was open for 8% of the time, Pallas kernels for 11%

profile of v1, /device:TPU:2, one launch (start us, length us, event | category | flops | bytes accessed | tf_op | source)
XLA Modules:
  0.0 237.9 jit_solution(748083332279512112)
XLA Ops:
  0.6 11.9 %states.1 = (f32[2,1024,256]{2,1,0:T(8,128)}, f32[2,512,256]{2,1,0:T(8,128)}, f32[2,520,256]{2,1,0:T(8,128)}, f32[2,16,512]{2,1,0:T(8,128)}, f32[2,8,256]{2,1,0:T(8,128)}) custom-call(s32[1]{0:T(128)} %bitcast.refs_0_.core, bf16[2,512,1024]{2,1,0:T(8,128)(2,1)} %refs_1_.3, bf16[2,512,256]{2,1,0:T(8,128)(2,1)} %refs_2_.3, f32[2,16,512]{2,1,0:T(8,128)} %refs_4_.3, ...), custom_call_target="tpu_custom_call" | custom-call | tf_op jit(solution)/shard_map/states/pallas_call | solution.py:321
  12.6 1.3 slice.38.refs_2_
  13.9 1.6 collective-permute-done.refs_3_
  15.5 1.0 copy-done.2
  16.5 2.8 %pair.1 = f32[16,72,256]{2,1,0:T(8,128)} custom-call(s32[1]{0:T(128)} %bitcast.refs_0_.core, f32[2,512,256]{2,1,0:T(8,128)} %get-tuple-element.13.refs_1_, f32[2,8,256]{2,1,0:T(8,128)} %slice.38.refs_2_, f32[2,520,256]{2,1,0:T(8,128)} %copy-done.2), custom_call_target="tpu_custom_call" | custom-call | tf_op jit(solution)/shard_map/pair/pallas_call | solution.py:249
  19.3 9.9 %all-to-all-start = ((f32[16,72,256]{2,1,0:T(8,128)}), f32[16,72,256]{2,1,0:T(8,128)S(1)}, u32[]{:S(2)}, u32[]{:S(2)}) async-start(f32[16,72,256]{2,1,0:T(8,128)} %pair.1), calls=%async_computation | async-start | bytes 2359296 | tf_op jit(solution)/shard_map/all_to_all | solution.py:359
  29.6 1.6 copy.84
  31.2 28.5 %all-to-all-done.refs_0_ = f32[16,72,256]{2,1,0:T(8,128)S(1)} async-done(((f32[16,72,256]{2,1,0:T(8,128)}), f32[16,72,256]{2,1,0:T(8,128)S(1)}, u32[]{:S(2)}, u32[]{:S(2)}) %all-to-all-start) | async-done | bytes 1179680 | tf_op jit(solution)/shard_map/all_to_all | solution.py:359
  59.7 6.1 %all-to-all-start.3 = ((f32[16,32,512]{2,1,0:T(8,128)}), f32[16,32,512]{2,1,0:T(8,128)S(1)}, u32[]{:S(2)}, u32[]{:S(2)}) async-start(f32[16,32,512]{2,1,0:T(8,128)} %bitcast.63), calls=%async_computation.3 | async-start | bytes 2097152 | tf_op jit(solution)/shard_map/all_to_all | solution.py:298
  67.8 0.7 copy.64
  70.7 3.9 %scan.1 = (f32[16,64,256]{2,1,0:T(8,128)}, f32[32,128]{1,0:T(8,128)}, f32[32,32,256]{2,1,0:T(8,128)}) custom-call(f32[16,72,256]{2,1,0:T(8,128)} %copy-done.1, bf16[128,256]{1,0:T(8,128)(2,1)} %bitcast.73, bf16[128,256]{1,0:T(8,128)(2,1)} %bitcast.74, f32[32,128]{1,0:T(8,128)} %bitcast.80, f32[32,128]{1,0:T(8,128)} %bitcast.79, f32[32,128]{1,0:T(8,128)} %bitcast.81, ...), custom_call_target="tpu_custom_call" | custom-call | tf_op jit(solution)/shard_map/scan/pallas_call | solution.py:249
  74.6 7.3 %all-to-all-done.3.w = f32[16,32,512]{2,1,0:T(8,128)S(1)} async-done(((f32[16,32,512]{2,1,0:T(8,128)}), f32[16,32,512]{2,1,0:T(8,128)S(1)}, u32[]{:S(2)}, u32[]{:S(2)}) %all-to-all-start.3) | async-done | bytes 1048608 | tf_op jit(solution)/shard_map/all_to_all | solution.py:298
  82.0 0.7 broadcast_in_dim.70
  82.7 14.1 %all_to_all.45.y = f32[16,32,128]{2,1,0:T(8,128)} all-to-all(f32[16,32,128]{2,1,0:T(8,128)S(1)} %broadcast_in_dim.70), channel_id=1, replica_groups=mesh['z'=8,'xl'=2,'co'=2,'y'=4,'xh'=2] {'co','y','xh'}, dimensions={0} | all-to-all | bytes 524288 | tf_op jit(solution)/shard_map/all_to_all | solution.py:44
  96.8 2.3 project.1
  99.1 15.5 %all_to_all.46 = f32[16,8,512]{2,1,0:T(8,128)S(1)} all-to-all(f32[16,8,512]{2,1,0:T(8,128)} %bitcast.68), channel_id=1, replica_groups=mesh['z'=8,'xl'=2,'co'=2,'y'=4,'xh'=2] {'z','xl'}, dimensions={0} | all-to-all | bytes 524288 | tf_op jit(solution)/shard_map/all_to_all | solution.py:376
  114.6 14.1 %all_to_all.47 = f32[16,8,512]{2,1,0:T(8,128)S(1)} all-to-all(f32[16,8,512]{2,1,0:T(8,128)S(1)} %broadcast_in_dim.71), channel_id=1, replica_groups=mesh['z'=8,'xl'=2,'co'=2,'y'=4,'xh'=2] {'z','xl'}, dimensions={0} | all-to-all | bytes 524288 | tf_op jit(solution)/shard_map/all_to_all | solution.py:44
  129.0 29.8 %all_to_all.48.own = f32[8,128,512]{2,1,0:T(8,128)S(1)} all-to-all(f32[8,128,512]{2,1,0:T(8,128)S(1)} %broadcast_in_dim.73), channel_id=1, replica_groups=mesh['z'=8,'xl'=2,'co'=2,'y'=4,'xh'=2] {'y','xh'}, dimensions={0} | all-to-all | bytes 4194304 | tf_op jit(solution)/shard_map/all_to_all | solution.py:44
  158.8 6.0 %all-to-all-start.1 = ((f32[16,64,256]{2,1,0:T(8,128)}), f32[16,64,256]{2,1,0:T(8,128)}, u32[]{:S(2)}, u32[]{:S(2)}) async-start(f32[16,64,256]{2,1,0:T(8,128)} %get-tuple-element.15), calls=%async_computation.1 | async-start | bytes 2097152 | tf_op jit(solution)/shard_map/all_to_all | solution.py:400
  164.8 0.7 slice_exponential_fusion.1
  165.9 1.1 slice.50
  167.0 21.6 %all-to-all-done.1 = f32[16,64,256]{2,1,0:T(8,128)} async-done(((f32[16,64,256]{2,1,0:T(8,128)}), f32[16,64,256]{2,1,0:T(8,128)}, u32[]{:S(2)}, u32[]{:S(2)}) %all-to-all-start.1) | async-done | bytes 1048608 | tf_op jit(solution)/shard_map/all_to_all | solution.py:400
  188.6 3.4 %fusion = (f32[16,2,32,256]{3,2,1,0:T(8,128)S(1)}, f32[16,2,32,256]{3,2,1,0:T(8,128)}) fusion(f32[16,2,32,256]{3,2,1,0:T(8,128)} %bitcast.16, f32[2,16,32,256]{3,2,1,0:T(8,128)} %bitcast.65, f32[2,32]{1,0:T(2,128)S(1)} %exp.39, pred[]{:T(512)S(6)} %eq.18, f32[2,16,32,256]{3,2,1,0:T(8,128)} %bitcast.66, f32[2,32]{1,0:T(2,128)S(1)} %exp.36), kind=kLoop, calls=%fused_computation.1 | loop fusion | flops 1572864 | bytes 5243393 | tf_op jit(solution)/shard_map/jit(_where)/select_n | solution.py:409
  193.2 0.9 fusion.2.allowed
  194.1 5.8 %logits.1 = f32[8,128]{1,0:T(8,128)} custom-call(s32[1]{0:T(128)} %bitcast.refs_0_.core, f32[8,128,512]{2,1,0:T(8,128)} %copy-done, f32[8,128,512]{2,1,0:T(8,128)} %collective-permute-done.2.other, f32[1,8192]{1,0:T(1,128)} %bitcast.84, bf16[8192,256]{1,0:T(8,128)(2,1)} %head.1, f32[256,128]{1,0:T(8,128)} %fusion.2.allowed, s32[1,128]{1,0:T(1,128)} %sub.54.chosen), custom_call_target="tpu_custom_call" | custom-call | tf_op jit(solution)/shard_map/logits/pallas_call | solution.py:249
  199.9 0.7 slice.42
  200.6 11.6 %all_to_all.49 = f32[16,3,128]{2,1,0:T(4,128)S(1)} all-to-all(f32[16,3,128]{2,1,0:T(4,128)S(1)} %broadcast_in_dim.75), channel_id=1, replica_groups=mesh['z'=8,'xl'=2,'co'=2,'y'=4,'xh'=2] {'z','co'}, dimensions={0} | all-to-all | bytes 49152 | tf_op jit(solution)/shard_map/all_to_all | solution.py:44
  213.0 4.8 %all-to-all-start.8 = ((f32[16,3,128]{2,1,0:T(4,128)}), f32[16,3,128]{2,1,0:T(4,128)S(1)}, u32[]{:S(2)}, u32[]{:S(2)}) async-start(f32[16,3,128]{2,1,0:T(4,128)} %broadcast_in_dim.76), calls=%async_computation.8 | async-start | bytes 65536 | tf_op jit(solution)/shard_map/all_to_all | solution.py:44
  217.8 0.7 broadcast_in_dim_reshape.9.refs_10_
  218.5 1.6 reshape.128
  220.1 16.9 %outputs.1 = bf16[2,512,1024]{2,1,0:T(8,128)(2,1)} custom-call(s32[1]{0:T(128)} %bitcast.refs_0_.core, bf16[2,512,1024]{2,1,0:T(8,128)(2,1)} %refs_1_.3, bf16[2,512,256]{2,1,0:T(8,128)(2,1)} %refs_2_.3, bf16[2,512,256]{2,1,0:T(8,128)(2,1)} %refs_3_.3, f32[2,16,512]{2,1,0:T(8,128)} %refs_4_.3, f32[2,16,512]{2,1,0:T(8,128)} %get-tuple-element.11.refs_5_, ...), custom_call_target="tpu_custom_call" | custom-call | tf_op jit(solution)/shard_map/outputs/pallas_call | solution.py:415
  237.2 0.7 reshape.132
  (88 shorter events, 7.3 us)
Async XLA Ops:
  12.5 3.0 %collective-permute-start = (f32[2,520,256]{2,1,0:T(8,128)}, f32[2,520,256]{2,1,0:T(8,128)S(1)}, u32[]{:S(2)}, u32[]{:S(2)}) collective-permute-start(f32[2,520,256]{2,1,0:T(8,128)} %get-tuple-element.14), channel_id=1, source_target_pairs={{0,8},{8,0},{1,9},{9,1},{2,10},{10,2},{3,11},{11,3},{4,12},{12,4},... | collective-permute-start | bytes 3194888 | tf_op jit(solution)/shard_map/ppermute | solution.py:39
  15.5 1.0 copy-start.2
  16.5 12.8 %copy-start.6 = (bf16[16,2,8192]{2,1,0:T(2,128)(2,1)S(1)}, bf16[16,2,8192]{2,1,0:T(2,128)(2,1)}, u32[]{:S(2)}) copy-start(bf16[16,2,8192]{2,1,0:T(2,128)(2,1)} %param.28) | copy-start | bytes 1572868
  19.3 40.4 %all-to-all-start = ((f32[16,72,256]{2,1,0:T(8,128)}), f32[16,72,256]{2,1,0:T(8,128)S(1)}, u32[]{:S(2)}, u32[]{:S(2)}) async-start(f32[16,72,256]{2,1,0:T(8,128)} %pair.1), calls=%async_computation | async-start | bytes 2359296 | tf_op jit(solution)/shard_map/all_to_all | solution.py:359
  29.6 36.3 %copy-start.7 = (bf16[4,32,256]{2,1,0:T(8,128)(2,1)S(1)}, bf16[4,32,256]{2,1,0:T(8,128)(2,1)}, u32[]{:S(2)}) copy-start(bf16[4,32,256]{2,1,0:T(8,128)(2,1)} %param.25) | copy-start | bytes 196612
  29.6 36.9 %copy-start.8 = (bf16[4,32,256]{2,1,0:T(8,128)(2,1)S(1)}, bf16[4,32,256]{2,1,0:T(8,128)(2,1)}, u32[]{:S(2)}) copy-start(bf16[4,32,256]{2,1,0:T(8,128)(2,1)} %param.24) | copy-start | bytes 196612
  29.6 37.6 %copy-start.9 = (f32[4,32,16]{1,2,0:T(8,128)S(1)}, f32[4,32,16]{1,2,0:T(8,128)}, u32[]{:S(2)}) copy-start(f32[4,32,16]{1,2,0:T(8,128)} %param.27) | copy-start | bytes 24580
  29.6 37.9 %copy-start.10 = (bf16[4,32,16,2]{1,3,2,0:T(2,128)(2,1)S(1)}, bf16[4,32,16,2]{1,3,2,0:T(2,128)(2,1)}, u32[]{:S(2)}) copy-start(bf16[4,32,16,2]{1,3,2,0:T(2,128)(2,1)} %param.23) | copy-start | bytes 24580
  31.2 37.2 %copy-start.11 = (f32[4,32,16]{1,2,0:T(8,128)S(1)}, f32[4,32,16]{1,2,0:T(8,128)}, u32[]{:S(2)}) copy-start(f32[4,32,16]{1,2,0:T(8,128)} %param.26) | copy-start | bytes 24580
  31.2 37.5 %copy-start.14 = (f32[16]{0:T(128)S(1)}, f32[16]{0:T(128)}, u32[]{:S(2)}) copy-start(f32[16]{0:T(128)} %param.22) | copy-start | bytes 196
  59.7 11.0 %copy-start.1 = (f32[16,72,256]{2,1,0:T(8,128)}, f32[16,72,256]{2,1,0:T(8,128)S(1)}, u32[]{:S(2)}) copy-start(f32[16,72,256]{2,1,0:T(8,128)S(1)} %all-to-all-done.refs_0_) | copy-start | bytes 3538948
  59.7 22.2 %all-to-all-start.3 = ((f32[16,32,512]{2,1,0:T(8,128)}), f32[16,32,512]{2,1,0:T(8,128)S(1)}, u32[]{:S(2)}, u32[]{:S(2)}) async-start(f32[16,32,512]{2,1,0:T(8,128)} %bitcast.63), calls=%async_computation.3 | async-start | bytes 2097152 | tf_op jit(solution)/shard_map/all_to_all | solution.py:298
  82.0 14.8 %copy-start.4 = (f32[16,32,512]{2,1,0:T(8,128)}, f32[16,32,512]{2,1,0:T(8,128)S(1)}, u32[]{:S(2)}) copy-start(f32[16,32,512]{2,1,0:T(8,128)S(1)} %all-to-all-done.3.w) | copy-start | bytes 3145732
  158.8 8.2 %copy-start = (f32[8,128,512]{2,1,0:T(8,128)}, f32[8,128,512]{2,1,0:T(8,128)S(1)}, u32[]{:S(2)}) copy-start(f32[8,128,512]{2,1,0:T(8,128)S(1)} %all_to_all.48.own) | copy-start | bytes 6291460
  158.8 6.9 %copy-start.3 = (f32[2,520,256]{2,1,0:T(8,128)S(1)}, f32[2,520,256]{2,1,0:T(8,128)}, u32[]{:S(2)}) copy-start(f32[2,520,256]{2,1,0:T(8,128)} %copy-done.2) | copy-start | bytes 3194884
  158.8 29.8 %all-to-all-start.1 = ((f32[16,64,256]{2,1,0:T(8,128)}), f32[16,64,256]{2,1,0:T(8,128)}, u32[]{:S(2)}, u32[]{:S(2)}) async-start(f32[16,64,256]{2,1,0:T(8,128)} %get-tuple-element.15), calls=%async_computation.1 | async-start | bytes 2097152 | tf_op jit(solution)/shard_map/all_to_all | solution.py:400
  164.8 29.3 %collective-permute-start.2 = (f32[8,128,512]{2,1,0:T(8,128)S(1)}, f32[8,128,512]{2,1,0:T(8,128)}, u32[]{:S(2)}, u32[]{:S(2)}) collective-permute-start(f32[8,128,512]{2,1,0:T(8,128)S(1)} %all_to_all.48.own), channel_id=1, source_target_pairs={{0,8},{8,0},{1,9},{9,1},{2,10},{10,2},{3,11},{11,3},{4,12},{12,4},... | collective-permute-start | bytes 6291464 | tf_op jit(solution)/shard_map/ppermute | solution.py:39
  188.6 3.4 %copy-start.12 = (s32[16,8]{0,1:T(8,128)S(1)}, s32[16,8]{0,1:T(8,128)}, u32[]{:S(2)}) copy-start(s32[16,8]{0,1:T(8,128)} %param.31) | copy-start | bytes 1540
  188.6 3.7 %copy-start.13 = (s32[4,32]{1,0:T(4,128)S(1)}, s32[4,32]{1,0:T(4,128)}, u32[]{:S(2)}) copy-start(s32[4,32]{1,0:T(4,128)} %param.32) | copy-start | bytes 1540
  188.6 3.9 %copy-start.15 = (s32[4,32]{1,0:T(4,128)S(1)}, s32[4,32]{1,0:T(4,128)}, u32[]{:S(2)}) copy-start(s32[4,32]{1,0:T(4,128)} %param.33) | copy-start | bytes 1540
  192.0 28.1 %collective-permute-start.1 = (f32[16,2,32,256]{3,2,1,0:T(8,128)S(1)}, f32[16,2,32,256]{3,2,1,0:T(8,128)}, u32[]{:S(2)}, u32[]{:S(2)}) collective-permute-start(f32[16,2,32,256]{3,2,1,0:T(8,128)S(1)} %get-tuple-element.19), channel_id=1, source_target_pairs={{0,8},{8,0},{1,9},{9,1},{2,10},{10,2},{3,11},{11,3},{4,12},{12,4},... | collective-permute-start | bytes 3145736 | tf_op jit(solution)/shard_map/ppermute | solution.py:39
  194.1 24.4 %copy-start.5 = (f32[32,32,256]{2,1,0:T(8,128)S(1)}, f32[32,32,256]{2,1,0:T(8,128)}, u32[]{:S(2)}) copy-start(f32[32,32,256]{2,1,0:T(8,128)} %get-tuple-element.17) | copy-start | bytes 3145732
  213.0 24.1 %all-to-all-start.8 = ((f32[16,3,128]{2,1,0:T(4,128)}), f32[16,3,128]{2,1,0:T(4,128)S(1)}, u32[]{:S(2)}, u32[]{:S(2)}) async-start(f32[16,3,128]{2,1,0:T(4,128)} %broadcast_in_dim.76), calls=%async_computation.8 | async-start | bytes 65536 | tf_op jit(solution)/shard_map/all_to_all | solution.py:44

commit v2 on v1

v2 whole, which is shorter than its diff:
```python
import jax
import jax.numpy as jnp
import numpy as np
from jax import lax
from jax.experimental import pallas as pl
from jax.experimental.pallas import tpu as pltpu
from jax.sharding import Mesh
from jax.sharding import PartitionSpec as P


BLOCK = 256
STEPS = 4
Z, XL, CO, Y, XH = "z", "xl", "co", "y", "xh"
CTX = (Z, XL, CO)
GRP = (Y, XH)
ALL = (Z, XL, CO, Y, XH)
ZX = (Z, XL)
CG = (CO, Y, XH)

NEG_BIG = -1e30
EPS = 1e-05
F32 = jnp.float32
BF16 = jnp.bfloat16
HI = lax.Precision.HIGHEST


def size_of(axes):
    return int(np.prod([lax.axis_size(a) for a in axes]))


def iota(shape, dim):
    return lax.broadcasted_iota(jnp.int32, shape, dim)


def dot(a, b, dims, precision=None):
    return lax.dot_general(a, b, (dims, ((), ())), precision=precision, preferred_element_type=F32)


def in_thirds(value, axis):
    high = value.astype(BF16)
    rest = value - high.astype(F32)
    middle = rest.astype(BF16)
    low = (rest - middle.astype(F32)).astype(BF16)
    return jnp.concatenate([high, middle, low], axis=axis)


def one_hot_thirds(shape, axis, match):
    return jnp.concatenate([match(shape).astype(BF16)] * 3, axis=axis)


def expander(heads, width):
    per = width // heads
    return one_hot_thirds(
        (heads, width), 0, lambda shape: iota(shape, 1) // per == iota(shape, 0)
    )


def swapped(value):
    return lax.ppermute(value, CO, [(0, 1), (1, 0)])


def told(value, axes):
    many = size_of(axes)
    return lax.all_to_all(
        jnp.broadcast_to(value[None], (many, *value.shape)), axes, 0, 0, tiled=True
    )


def column(row, rows, per):
    width = row.shape[1]
    pick = iota((rows, width), 1) == iota((rows, width), 0) // per
    return jnp.sum(jnp.where(pick, row, 0.0), axis=1, keepdims=True)


def local_index(feature, my_core, head_dim, zx, p2, heads):
    h, p = feature // head_dim, feature % head_dim
    chip, rest = p // (2 * p2), p % (2 * p2)
    side = (rest // p2) ^ my_core
    return ((side * zx + chip) * heads + h) * p2 + rest % p2


def states_kernel(zx, p2, core, x, b, step, decay, e0, keep, send, run_out, logs, perm_t):
    tokens, width = x.shape[1], x.shape[2]
    heads = step.shape[1]
    head_dim = width // heads
    half = width // 2
    blocks = tokens // BLOCK

    @pl.when(pl.program_id(0) == 0)
    def _():
        goes = local_index(iota((1, width), 1), core[0], head_dim, zx, p2, heads)
        perm_t[...] = (iota((width, width), 0) == goes).astype(BF16)

    upper = (iota((BLOCK, BLOCK), 0) <= iota((BLOCK, BLOCK), 1)).astype(BF16)
    of_row = one_hot_thirds(
        (width, heads), 1, lambda shape: iota(shape, 0) // p2 % heads == iota(shape, 1)
    )
    lane = iota((heads, BLOCK), 1) == iota((heads, BLOCK), 0)
    total_row = jnp.zeros((1, BLOCK), F32)
    to_end, totals = [], []
    for k in range(blocks):
        at = slice(k * BLOCK, (k + 1) * BLOCK)
        run = dot(in_thirds(decay[0, :, at], 0), upper, ((1,), (0,)))
        run = run[:heads] + run[heads : 2 * heads] + run[2 * heads :]
        run_out[0, :, at] = run
        total = jnp.broadcast_to(run[:, BLOCK - 1 :], (heads, BLOCK))
        to_end.append(step[0, :, at] * jnp.exp(total - run))
        totals.append(total)
        total_row = total_row + jnp.sum(jnp.where(lane, total, 0.0), axis=0, keepdims=True)
        if k == 0:
            logs[0, :4] = jnp.broadcast_to(total_row, (4, BLOCK))
    logs[0, 4:] = jnp.broadcast_to(total_row, (4, BLOCK))
    send[0, half:] = jnp.broadcast_to(total_row, (8, BLOCK))
    ends = in_thirds(jnp.concatenate(to_end, axis=1).T, 1)
    spread = dot(ends, expander(heads, width), ((1,), (0,)))
    scaled = (x[0].astype(F32) * spread).astype(BF16)
    moved = dot(perm_t[...], scaled, ((1,), (1,))).astype(BF16)
    state = None
    for k in range(blocks):
        at = slice(k * BLOCK, (k + 1) * BLOCK)
        own = dot(moved[:, at], b[0, at], ((1,), (0,)))
        if k == 0:
            state = own
            e0[0] = own
        else:
            fade = dot(of_row, in_thirds(jnp.exp(totals[k]), 0), ((1,), (0,)))
            state = fade * state + own
    keep[0] = state[:half]
    send[0, :half] = state[half:]


def pair_kernel(p2, heads, core, keep, logs, came, came_logs, out):
    rows = heads * p2
    first = core[0] == 0
    for s in range(keep.shape[0]):
        mine = logs[s, 4:5]
        other = came_logs[s, :1]
        f_mine = jnp.where(first, jnp.exp(column(other, rows, p2)), 1.0)
        f_came = jnp.where(first, 1.0, jnp.exp(column(mine, rows, p2)))
        for k in range(keep.shape[1] // rows):
            at = slice(k * rows, (k + 1) * rows)
            out[k, s * rows : (s + 1) * rows] = f_mine * keep[s, at] + f_came * came[s, at]
            out[k, 2 * rows + s * 4 : 2 * rows + s * 4 + 4] = jnp.broadcast_to(
                mine + other, (4, mine.shape[1])
            )


def tables_kernel(p2, heads, c_q, b_q, cum, x_q, step_q, skip_col, grow, xs, add):
    rows, many = x_q.shape
    half = many // 2
    per = half // STEPS
    repeat = (iota((rows, heads), 0) // p2 == iota((rows, heads), 1)).astype(F32)
    cums = dot(repeat, cum[...], ((1,), (0,)), HI)
    steps = dot(repeat, step_q[...], ((1,), (0,)), HI)
    growth = jnp.exp(cums)
    inject = x_q[...] * steps * jnp.exp(-cums)
    cross = dot(b_q[...], c_q[...], ((1,), (1,)))
    earlier, later = iota((many, many), 0), iota((many, many), 1)
    same = (earlier // half == later // half) & (earlier % per == later % per)
    cross = jnp.where(same & (earlier <= later), cross, 0.0)
    grow[...] = growth
    xs[...] = inject
    add[...] = growth * dot(inject, cross, ((1,), (0,)), HI) + skip_col[...] * x_q[...]


def scan_kernel(p2, heads, pieces, c_q, grow, add, enter, step_y, last):
    zx = pieces.shape[0]
    rows = heads * p2
    many = c_q.shape[0]
    final = jnp.zeros((2 * rows, pieces.shape[2]), F32)
    for k in range(zx):
        enter[k] = final
        fac = jnp.concatenate(
            [
                jnp.exp(column(pieces[k, 2 * rows + 4 * s : 2 * rows + 4 * s + 1], rows, p2))
                for s in range(2)
            ],
            axis=0,
        )
        final = fac * final + pieces[k, : 2 * rows]
    last[...] = final
    seen = dot(final, c_q[...].astype(F32), ((1,), (1,)), HI)
    lane = iota((rows, many), 1)
    seen = jnp.where(lane < many // 2, seen[:rows], seen[rows:])
    y = grow[...] * seen + add[...]
    step_y[...] = jnp.broadcast_to(y.astype(BF16).astype(F32), step_y.shape)


def rows_kernel(last, b_q, grow, xs, row_state):
    rows, many = xs.shape
    half = many // 2
    per = half // STEPS
    b_all = b_q[...].astype(F32)
    growth, inject = grow[...], xs[...]
    for s in range(2):
        for r in range(per):
            value = last[s * rows : (s + 1) * rows]
            for i in range(STEPS):
                q = s * half + i * per + r
                value = value + inject[:, q : q + 1] * b_all[q : q + 1]
            row_state[s * per + r] = growth[:, q : q + 1] * value


def project_kernel(ny, nxh, place, own, other, *refs):
    pieces, out = refs[:-1], refs[-1]
    left, right = [], []
    for number, piece in enumerate(pieces):
        dy, dx = number // nxh, number % nxh
        at = lax.rem(place[1] + (ny - dy), ny) * nxh + lax.rem(place[2] + (nxh - dx), nxh)
        left += [own[at], other[at]]
        right.append(piece[...].reshape(-1, piece.shape[2]))
    left = jnp.concatenate(left, axis=0).T.astype(BF16)
    right = jnp.concatenate(right, axis=0).astype(BF16)
    out[...] = dot(left, right, ((1,), (0,)))


def logits_kernel(ny, nxh, steps, place, *refs):
    arrays, (gain, head, allowed, chosen, out) = refs[: 2 * len(steps)], refs[2 * len(steps) :]
    many, width = arrays[0].shape
    model = head.shape[0]
    total = jnp.zeros((many, 128), F32)
    for ref in arrays:
        part = ref[...]
        part = part * part
        for k in range(width // 128):
            total = total + part[:, k * 128 : (k + 1) * 128]
    scale = lax.rsqrt(jnp.sum(total, axis=1, keepdims=True) / model + EPS)
    acc = jnp.zeros((many, head.shape[1]), F32)
    for number, ref in enumerate(arrays):
        side, (dy, dx) = number // len(steps), steps[number % len(steps)]
        of_y = lax.rem(place[1] + (ny - dy), ny)
        of_x = lax.rem(place[2] + (nxh - dx), nxh)
        block = ((place[0] ^ side) * ny + of_y) * nxh + of_x
        at = pl.ds(pl.multiple_of(block * width, width), width)
        normed = (ref[...] * scale * gain[:, at]).astype(BF16)
        acc = acc + dot(normed, head[at], ((1,), (0,)))
    acc = acc.T
    ok = allowed[...] > 0.5
    top = jnp.max(jnp.where(ok, acc, NEG_BIG), axis=0, keepdims=True)
    total = jnp.sum(jnp.where(ok, jnp.exp(acc - top), 0.0), axis=0, keepdims=True)
    hit = iota(acc.shape, 0) == chosen[...]
    picked = jnp.sum(jnp.where(hit, acc, 0.0), axis=0, keepdims=True)
    out[...] = jnp.broadcast_to(jnp.concatenate([top, total, picked], axis=0)[None], out.shape)


def inner_kernel(x, b, c, step, run, skip, out):
    width = x.shape[2]
    heads = step.shape[1]
    head_dim = width // heads
    xb = x[0]
    running, steps = run[0], step[0]
    run_t = running.T
    causal = iota((BLOCK, BLOCK), 1) <= iota((BLOCK, BLOCK), 0)
    scores = jnp.where(causal, dot(c[0], b[0], ((1,), (1,))), 0.0)
    pair = 2 * head_dim
    left = iota((BLOCK, pair), 1) < head_dim
    for j in range(heads // 2):
        at = slice(j * pair, (j + 1) * pair)
        halves = []
        for h in (2 * j, 2 * j + 1):
            gap = jnp.minimum(run_t[:, h : h + 1] - running[h : h + 1], 0.0)
            mix = (scores * jnp.exp(gap) * steps[h : h + 1]).astype(BF16)
            halves.append(dot(mix, xb[:, at], ((1,), (0,))))
        inner = jnp.where(left, halves[0], halves[1])
        out[0, :, at] = inner + skip[:, at] * xb[:, at].astype(F32)


def carry_kernel(zx, p2, heads, core, inner, c, run, logs, own, other, e0, *refs):
    out, perm = refs[-2:]
    tokens, width = inner.shape[1], inner.shape[2]
    head_dim = width // heads
    rows = heads * p2
    blocks = tokens // BLOCK
    goes = local_index(iota((width, 1), 0), core[0], head_dim, zx, p2, heads)
    perm[...] = (iota((width, width), 1) == goes).astype(BF16)
    enter = jnp.concatenate(
        [own[:, 0].reshape(zx * rows, -1), other[:, 0].reshape(zx * rows, -1)], axis=0
    )
    n = enter.shape[1]
    fade = jnp.exp(column(logs[0, :1], rows, p2))
    after = (enter.reshape(2 * zx, rows, n) * fade[None]).reshape(width, n) + e0[0]
    both = jnp.concatenate([enter.astype(BF16), after.astype(BF16)], axis=1)
    both = dot(perm[...], both, ((1,), (0,))).astype(BF16)
    growth = dot(in_thirds(jnp.exp(run[0].T), 1), expander(heads, width), ((1,), (0,)))
    for k in range(blocks):
        at = slice(k * BLOCK, (k + 1) * BLOCK)
        carry = dot(c[0, at], both[:, k * n : (k + 1) * n], ((1,), (1,)))
        out[0, at] = (inner[0, at] + growth[at] * carry).astype(BF16)


def merge(parts):
    top = jnp.max(parts[:, 0], axis=0)
    total = jnp.sum(parts[:, 1] * jnp.exp(parts[:, 0] - top), axis=0)
    picked = jnp.sum(parts[:, 2], axis=0)
    return top, total, picked


def full(shape):
    return pl.BlockSpec(shape, lambda *_: (0,) * len(shape))


def call(kernel, outs, *args, smem=(), anywhere=()):
    def spec(k, arg):
        if k in smem:
            return pl.BlockSpec(memory_space=pltpu.SMEM)
        if k in anywhere:
            return pl.BlockSpec(memory_space=pl.ANY)
        return full(arg.shape)

    specs = [spec(k, arg) for k, arg in enumerate(args)]
    many = isinstance(outs, tuple)
    return pl.pallas_call(
        kernel,
        grid=(1,),
        in_specs=specs,
        out_specs=tuple(full(o.shape) for o in outs) if many else full(outs.shape),
        out_shape=outs,
    )(*args)


def shaped(*shape, dtype=F32):
    return jax.ShapeDtypeStruct(shape, dtype)


def body(
    prompt_x,
    prompt_b,
    prompt_c,
    prompt_step,
    prompt_decay,
    skip_weight,
    decode_x,
    decode_b,
    decode_c,
    decode_step,
    decode_decay,
    out_proj,
    norm_gain,
    lm_head,
    mask_words,
    state_ids,
    chosen,
):
    seqs, tokens, width = prompt_x.shape
    n = prompt_b.shape[2]
    heads = prompt_step.shape[1]
    zx, cg, grp = size_of(ZX), size_of(CG), size_of(GRP)
    p2 = decode_x.shape[3]
    rows = heads * p2
    half = width // 2
    blocks = tokens // BLOCK
    decode_rows = decode_x.shape[1]
    per = decode_rows // seqs
    many = STEPS * decode_rows
    core = lax.axis_index(CO).astype(jnp.int32)[None]

    model = out_proj.shape[2]
    wide = model // cg
    ny, nxh = lax.axis_size(Y), lax.axis_size(XH)
    iy, ixh = (lax.axis_index(a).astype(jnp.int32) for a in (Y, XH))
    place = jnp.stack([core[0], iy, ixh])
    grp_steps = [(dy, dx) for dy in range(ny) for dx in range(nxh)]

    def grp_perm(dy, dx):
        return [
            (y * nxh + x, (y + dy) % ny * nxh + (x + dx) % nxh)
            for y in range(ny)
            for x in range(nxh)
        ]

    w_rows = out_proj.astype(F32).reshape(rows, 2, grp, wide).transpose(1, 2, 0, 3)
    w_keep = lax.dynamic_index_in_dim(w_rows, core[0], 0, keepdims=False)
    w_other = lax.dynamic_index_in_dim(w_rows, 1 - core[0], 0, keepdims=False)
    w_came = swapped(w_other)
    w_both = jnp.stack([w_keep, w_came], axis=1)
    w_own = []
    for dy, dx in grp_steps:
        to = (iy + dy) % ny * nxh + (ixh + dx) % nxh
        part = lax.dynamic_index_in_dim(w_both, to, 0, keepdims=False)
        w_own.append(lax.ppermute(part, GRP, grp_perm(dy, dx)) if dy or dx else part)

    def by_q(value):
        shape = value.shape[2:]
        value = value.reshape(STEPS, seqs, per, *shape)
        return jnp.moveaxis(value, 1, 0).reshape(many, *shape)

    c_q, b_q = by_q(decode_c), by_q(decode_b)
    cum_q = by_q(jnp.cumsum(decode_decay, axis=0)).T
    step_q = by_q(decode_step).T
    x_q = by_q(decode_x.astype(F32).reshape(STEPS, decode_rows, rows)).T
    skip_col = jnp.repeat(skip_weight, p2)[:, None]
    vocab = lm_head.shape[1]
    first = (lax.axis_index(CTX) * size_of(GRP) + lax.axis_index(GRP)) * vocab
    chosen_q = (by_q(chosen) - first)[None]
    ids_q = by_q(state_ids)
    bits = (
        jnp.right_shift(mask_words[:, :, None], jnp.arange(32, dtype=jnp.int32)[None, None]) & 1
    ).reshape(mask_words.shape[0], vocab)
    onehot = (ids_q[None] == jnp.arange(mask_words.shape[0])[:, None]).astype(BF16)
    allowed = dot(bits.astype(BF16), onehot, ((0,), (0,)))

    by_s = lambda *shape: pl.BlockSpec((1, *shape), lambda s: (s,) + (0,) * len(shape))
    e0, keep, send, run, logs = pl.pallas_call(
        lambda *refs: states_kernel(zx, p2, *refs),
        grid=(seqs,),
        in_specs=[
            pl.BlockSpec(memory_space=pltpu.SMEM),
            by_s(tokens, width),
            by_s(tokens, n),
            by_s(heads, tokens),
            by_s(heads, tokens),
        ],
        out_specs=(
            by_s(width, n),
            by_s(half, n),
            by_s(half + 8, n),
            by_s(heads, tokens),
            by_s(8, n),
        ),
        out_shape=(
            shaped(seqs, width, n),
            shaped(seqs, half, n),
            shaped(seqs, half + 8, n),
            shaped(seqs, heads, tokens),
            shaped(seqs, 8, n),
        ),
        scratch_shapes=[pltpu.VMEM((width, width), BF16)],
        name="states",
    )(core, prompt_x, prompt_b, prompt_step, prompt_decay)
    at_k = lambda *shape: pl.BlockSpec((1, BLOCK, *shape), lambda s, k: (s, k, 0))
    lanes_k = pl.BlockSpec((1, heads, BLOCK), lambda s, k: (s, 0, k))
    came = swapped(send)
    inner = pl.pallas_call(
        inner_kernel,
        grid=(seqs, blocks),
        in_specs=[at_k(width), at_k(n), at_k(n), lanes_k, lanes_k, full((1, width))],
        out_specs=at_k(width),
        out_shape=shaped(seqs, tokens, width),
        name="inner",
    )(
        prompt_x,
        prompt_b,
        prompt_c,
        prompt_step,
        run,
        jnp.repeat(skip_weight, width // heads)[None],
    )
    chips = zx // 4
    pieces = pl.pallas_call(
        lambda *refs: pair_kernel(p2, heads, *refs),
        grid=(4,),
        in_specs=[
            pl.BlockSpec(memory_space=pltpu.SMEM),
            pl.BlockSpec((seqs, chips * rows, n), lambda j: (0, j, 0)),
            full((seqs, 8, n)),
            pl.BlockSpec((seqs, chips * rows, n), lambda j: (0, j, 0)),
            pl.BlockSpec((seqs, 8, n), lambda j: (0, half // 8, 0)),
        ],
        out_specs=pl.BlockSpec((chips, 2 * rows + 8, n), lambda j: (j, 0, 0)),
        out_shape=shaped(zx, 2 * rows + 8, n),
        name="pair",
    )(core, keep, logs, came, came)
    pieces = lax.all_to_all(pieces, ZX, 0, 0, tiled=True)
    table = shaped(rows, many)
    grow, xs, add = call(
        lambda *refs: tables_kernel(p2, heads, *refs),
        (table, table, table),
        c_q,
        b_q,
        cum_q,
        x_q,
        step_q,
        skip_col,
    )
    enter, step_y, last = call(
        lambda *refs: scan_kernel(p2, heads, *refs),
        (shaped(zx, 2 * rows, n), shaped(grp, rows, many), shaped(2 * rows, n)),
        pieces,
        c_q,
        grow,
        add,
    )
    row_state = call(rows_kernel, shaped(decode_rows, rows, n), last, b_q, grow, xs)
    decode_state = row_state.reshape(decode_rows, heads, p2, n)

    ys = lax.all_to_all(step_y, GRP, 0, 0, tiled=True)
    partial = call(
        lambda *refs: project_kernel(ny, nxh, *refs),
        shaped(many, wide),
        place,
        ys,
        swapped(ys),
        *w_own,
        smem=(0,),
    )
    partial = lax.all_to_all(partial.reshape(zx, many // zx, wide), ZX, 0, 0, tiled=True)
    summed = jnp.sum(partial, axis=0)
    own_cols = told(summed, ZX).reshape(many, wide)
    blocks_y = []
    for dx in range(nxh):
        across = own_cols
        if dx:
            across = lax.ppermute(own_cols, XH, [(i, (i + dx) % nxh) for i in range(nxh)])
        for dy in range(ny):
            shift = [(i, (i + dy) % ny) for i in range(ny)]
            blocks_y.append((dy, dx, lax.ppermute(across, Y, shift) if dy else across))
    steps_y = [(dy, dx) for dy, dx, _ in blocks_y]
    own_half = [value for *_, value in blocks_y]
    other_half = [swapped(value) for value in own_half]
    enter, _ = lax.optimization_barrier((enter, own_cols))

    parts = call(
        lambda *refs: logits_kernel(ny, nxh, steps_y, *refs),
        shaped(size_of((Z, CO)), 3, many),
        place,
        *own_half,
        *other_half,
        norm_gain[None],
        lm_head,
        allowed,
        chosen_q,
        smem=(0,),
    )
    parts = lax.all_to_all(parts, (Z, CO), 0, 0, tiled=True)
    parts = jnp.stack(merge(parts))
    parts = told(parts, (XL, Y, XH))
    top, total, picked = merge(parts)
    logprob = picked - top - jnp.log(total)
    logprob = logprob.reshape(seqs, STEPS, per).transpose(1, 0, 2).reshape(STEPS, decode_rows)

    back = lax.all_to_all(enter, ZX, 0, 0, tiled=True).reshape(zx, seqs, rows, n)
    is_first = core[0] == 0

    def after(log_row, value, state):
        fade = jnp.exp(jnp.repeat(log_row[:, 0, :heads], p2, axis=1))[None, :, :, None]
        state = state[:, :half].reshape(seqs, zx, rows, n).transpose(1, 0, 2, 3)
        return fade * value + state

    for_me = jnp.where(is_first, back, after(came[:, half:], back, came))
    for_other = jnp.where(is_first, after(logs[:, 4:], back, keep), back)
    other_side = swapped(for_other)

    assert blocks == 2
    prompt_y = ()
    for s in range(seqs):
        of_s = lambda *shape, s=s: pl.BlockSpec((1, *shape), lambda _: (s,) + (0,) * len(shape))
        states_s = pl.BlockSpec((zx, 1, rows, n), lambda _, s=s: (0, s, 0, 0))
        prompt_y = pl.pallas_call(
            lambda *refs: carry_kernel(zx, p2, heads, *refs),
            grid=(1,),
            in_specs=[
                pl.BlockSpec(memory_space=pltpu.SMEM),
                of_s(tokens, width),
                of_s(tokens, n),
                of_s(heads, tokens),
                of_s(8, n),
                states_s,
                states_s,
                of_s(width, n),
                *[pl.BlockSpec(memory_space=pl.ANY) for _ in prompt_y],
            ],
            out_specs=of_s(tokens, width),
            out_shape=shaped(seqs, tokens, width, dtype=BF16),
            input_output_aliases={8: 0} if prompt_y else {},
            scratch_shapes=[pltpu.VMEM((width, width), BF16)],
        )(core, inner, prompt_c, run, logs, for_me, other_side, e0, *prompt_y)
        prompt_y = (prompt_y,)
    (prompt_y,) = prompt_y
    return (prompt_y, decode_state, logprob)


def solution(mesh):
    ctx, grp = mesh.devices.shape
    shape = (ctx // 4, 2, 2, grp // 2, 2)
    finer = Mesh(mesh.devices.reshape(shape), ALL)
    in_specs = (
        P(None, CTX, GRP),
        P(None, CTX, GRP),
        P(None, CTX, GRP),
        P(None, GRP, CTX),
        P(None, GRP, CTX),
        P(GRP),
        P(None, None, GRP, CTX),
        P(None, None, GRP),
        P(None, None, GRP),
        P(None, None, GRP),
        P(None, None, GRP),
        P(GRP, CTX, None),
        P(),
        P(None, ALL),
        P(None, ALL),
        P(),
        P(),
    )
    out_specs = (P(None, CTX, GRP), P(None, GRP, CTX, None), P())

    return jax.shard_map(body, mesh=finer, in_specs=in_specs, out_specs=out_specs, check_vma=False)
```

time: 240 us -> 201 us (0.84)
  blocking collectives: 85.1 us -> 31.4 us
  starting transfers between devices: 27 us -> 64.3 us
  waiting for transfers between devices: 59.1 us -> 31.6 us
  local copies, waits for them, and re-layouts: 17.7 us -> 21 us
    all_to_all x4 -> x1, blocking collectives: 69.6 us -> 14.2 us  [told(): lax.all_to_all(jnp.broadcast_to(value[None], (many, *value.shape)), axes,...]
    ppermute x0 -> x14, starting transfers between devices: none -> 27.8 us  [the longest x7 18.8 us: body(): lax.ppermute(part, GRP, grp_perm(dy, dx))]
    all_to_all x1, waiting for transfers between devices: 28.5 us -> 5.54 us  [body(): pieces = lax.all_to_all(pieces, ZX, 0, 0, tiled=True)]
    all_to_all x1, waiting for transfers between devices: 21.6 us -> 0.01 us  [body(): lax.all_to_all(enter, ZX, 0, 0, tiled=True).reshape(zx, seqs, rows, n)]
    ppermute x0 -> x14, waiting for transfers between devices: none -> 14.3 us  [the longest x6 6.58 us: body(): blocks_y.append((dy, dx, lax.ppermute(across, Y, shift) if dy else across))]
    all_to_all x1 -> x2, starting transfers between devices: 6.13 us -> 13.3 us  [the longest x1 7.29 us: body(): parts = lax.all_to_all(parts, (Z, CO), 0, 0, tiled=True)]
    pallas_call x1 -> x4, Pallas kernels: 16.9 us -> 22.6 us  [the longest x2 10.6 us: body(): pl.pallas_call(lambda *refs: carry_kernel(zx, p2, heads, *refs), grid=(1,...]
    unnamed x33 -> x55, local copies, waits for them, and re-layouts: 1.14 us -> 5.88 us
  transfers between devices with their start and end apart: 7 -> 31, of which waited for: 4 -> 14; matrix products, arithmetic and copies ran while one was open for 8% -> 10% of each run, Pallas kernels for 11% -> 11%
where the time goes in v2:
time: 201 us; the launch traced here: 200 us
  starting transfers between devices  64.3 us (32%)
  Pallas kernels  45.9 us (23%)
  waiting for transfers between devices  31.6 us (16%)
  blocking collectives  31.4 us (16%)
  local copies, waits for them, and re-layouts  21 us (10%)
  other arithmetic  3.5 us (2%)
    ppermute x7, starting transfers between devices, body(): lax.ppermute(part, GRP, grp_perm(dy, dx))  18.8 us
    all_to_all x1, blocking collectives, body(): lax.all_to_all(partial.reshape(zx, many // zx, wide), ZX, 0, 0, tiled=True)  17.2 us
    pallas_call x5, Pallas kernels, call(): pl.pallas_call(kernel, grid=(1,), in_specs=specs, out_specs=tuple((full(o...  15.2 us
    all_to_all x1, blocking collectives, told(): lax.all_to_all(jnp.broadcast_to(value[None], (many, *value.shape)), axes,...  14.2 us
    pallas_call x2, Pallas kernels, body(): pl.pallas_call(lambda *refs: carry_kernel(zx, p2, heads, *refs), grid=(1,...  10.6 us
    all_to_all x1, starting transfers between devices, body(): pieces = lax.all_to_all(pieces, ZX, 0, 0, tiled=True)  10.1 us
    ppermute x6, starting transfers between devices, body(): blocks_y.append((dy, dx, lax.ppermute(across, Y, shift) if dy else across))  8.98 us
    pallas_call x1, Pallas kernels, body(): pl.pallas_call(inner_kernel, grid=(seqs, blocks), in_specs=[at_k(width),...  8.17 us
  transfers between devices with their start and end apart: 31, of which 14 were waited for; matrix products, arithmetic and copies ran while one was open for 10% of the time, Pallas kernels for 11%

profile of v2, /device:TPU:2, one launch (start us, length us, event | category | flops | bytes accessed | tf_op | source)
XLA Modules:
  0.0 199.8 jit_solution(13782073073178727094)
XLA Ops:
  0.6 8.1 %states.1 = (f32[2,1024,256]{2,1,0:T(8,128)}, f32[2,512,256]{2,1,0:T(8,128)}, f32[2,520,256]{2,1,0:T(8,128)}, f32[2,16,512]{2,1,0:T(8,128)}, f32[2,8,256]{2,1,0:T(8,128)}) custom-call(s32[1]{0:T(128)} %bitcast.refs_0_, bf16[2,512,1024]{2,1,0:T(8,128)(2,1)} %x.1, bf16[2,512,256]{2,1,0:T(8,128)(2,1)} %b.1, f32[2,16,512]{2,1,0:T(8,128)} %step.1, ...), custom_call_target="tpu_custom_call" | custom-call | tf_op jit(solution)/shard_map/states/pallas_call | solution.py:403
  8.9 2.9 %collective-permute-done.refs_3_.refs_4_ = f32[2,520,256]{2,1,0:T(8,128)S(1)} collective-permute-done((f32[2,520,256]{2,1,0:T(8,128)}, f32[2,520,256]{2,1,0:T(8,128)S(1)}, u32[]{:S(2)}, u32[]{:S(2)}) %collective-permute-start) | collective-permute-done | bytes 1064992 | tf_op jit(solution)/shard_map/ppermute | solution.py:59
  12.7 3.8 %pair.1 = f32[16,72,256]{2,1,0:T(8,128)} custom-call(s32[1]{0:T(128)} %bitcast.refs_0_, f32[2,512,256]{2,1,0:T(8,128)} %get-tuple-element.17.refs_1_, f32[2,8,256]{2,1,0:T(8,128)} %get-tuple-element.16.refs_2_.refs_4_, f32[2,520,256]{2,1,0:T(8,128)} %copy-done, f32[2,520,256]{2,1,0:T(8,128)} %copy-done), custom_call_target="tpu_custom_call" | custom-call | tf_op jit(solution)/shard_map/pair/pallas_call | solution.py:449
  16.5 10.1 %all-to-all-start = ((f32[16,72,256]{2,1,0:T(8,128)}), f32[16,72,256]{2,1,0:T(8,128)S(1)}, u32[]{:S(2)}, u32[]{:S(2)}) async-start(f32[16,72,256]{2,1,0:T(8,128)} %pair.1), calls=%async_computation | async-start | bytes 2359296 | tf_op jit(solution)/shard_map/all_to_all | solution.py:463
  30.1 2.1 %collective-permute-start.3 = (f32[2,32,512]{2,1,0:T(8,128)}, f32[2,32,512]{2,1,0:T(8,128)S(1)}, u32[]{:S(2)}, u32[]{:S(2)}) collective-permute-start(f32[2,32,512]{2,1,0:T(8,128)} %get-tuple-element.31), channel_id=1, source_target_pairs={{0,1},{1,0},{2,3},{3,2},{4,5},{5,4},{6,7},{7,6},{8,9},{9,8},{10,11... | collective-permute-start | bytes 393224 | tf_op jit(solution)/shard_map/ppermute | solution.py:380
  32.2 1.6 collective-permute-start.4
  33.8 2.4 %collective-permute-start.5 = (f32[2,32,512]{2,1,0:T(8,128)S(1)}, f32[2,32,512]{2,1,0:T(8,128)S(1)}, u32[]{:S(2)}, u32[]{:S(2)}) collective-permute-start(f32[2,32,512]{2,1,0:T(8,128)S(1)} %get-tuple-element.33), channel_id=1, source_target_pairs={{0,3},{1,2},{2,5},{3,4},{4,7},{5,6},{6,1},{7,0},{8,11},{9,10},{10,... | collective-permute-start | bytes 393224 | tf_op jit(solution)/shard_map/ppermute | solution.py:380
  44.1 1.9 shard_map.184
  47.6 4.0 %collective-permute-start.9 = (f32[2,32,512]{2,1,0:T(8,128)S(1)}, f32[2,32,512]{2,1,0:T(8,128)S(1)}, u32[]{:S(2)}, u32[]{:S(2)}) collective-permute-start(f32[2,32,512]{2,1,0:T(8,128)S(1)} %get-tuple-element.29), channel_id=1, source_target_pairs={{0,7},{1,6},{2,1},{3,0},{4,3},{5,2},{6,5},{7,4},{8,15},{9,14},{10,... | collective-permute-start | bytes 393224 | tf_op jit(solution)/shard_map/ppermute | solution.py:380
  51.5 5.5 %all-to-all-done.refs_0_ = f32[16,72,256]{2,1,0:T(8,128)S(1)} async-done(((f32[16,72,256]{2,1,0:T(8,128)}), f32[16,72,256]{2,1,0:T(8,128)S(1)}, u32[]{:S(2)}, u32[]{:S(2)}) %all-to-all-start) | async-done | bytes 1179680 | tf_op jit(solution)/shard_map/all_to_all | solution.py:463
  58.1 2.7 %shard_map.185 = (f32[16,64,256]{2,1,0:T(8,128)}, f32[8,32,128]{2,1,0:T(8,128)}, f32[64,256]{1,0:T(8,128)}) custom-call(f32[16,72,256]{2,1,0:T(8,128)} %copy-done.2, bf16[128,256]{1,0:T(8,128)(2,1)} %bitcast.105, f32[32,128]{1,0:T(8,128)} %get-tuple-element.19.refs_2_.grow, f32[32,128]{1,0:T(8,128)} %get-tuple-element.20.refs_3_), custom_call_target="tpu_custom_call" | custom-call | tf_op jit(solution)/shard_map/pallas_call | solution.py:312
  60.8 6.0 %all-to-all-start.1 = ((f32[8,32,128]{2,1,0:T(8,128)}), f32[8,32,128]{2,1,0:T(8,128)S(1)}, u32[]{:S(2)}, u32[]{:S(2)}) async-start(f32[8,32,128]{2,1,0:T(8,128)} %get-tuple-element.22), calls=%async_computation.1 | async-start | bytes 262144 | tf_op jit(solution)/shard_map/all_to_all | solution.py:486
  66.9 6.0 %collective-permute-start.7 = (f32[2,32,512]{2,1,0:T(8,128)S(1)}, f32[2,32,512]{2,1,0:T(8,128)S(1)}, u32[]{:S(2)}, u32[]{:S(2)}) collective-permute-start(f32[2,32,512]{2,1,0:T(8,128)S(1)} %get-tuple-element.36), channel_id=1, source_target_pairs={{0,5},{1,4},{2,7},{3,6},{4,1},{5,0},{6,3},{7,2},{8,13},{9,12},{10,... | collective-permute-start | bytes 393224 | tf_op jit(solution)/shard_map/ppermute | solution.py:380
  78.6 2.4 %shard_map.186 = f32[128,512]{1,0:T(8,128)} custom-call(s32[3]{0:T(128)} %pad_add_fusion.refs_0_, f32[8,32,128]{2,1,0:T(8,128)} %copy-done.7, f32[8,32,128]{2,1,0:T(8,128)} %copy-done.20, f32[2,32,512]{2,1,0:T(8,128)} %get-tuple-element.30.refs_3_, f32[2,32,512]{2,1,0:T(8,128)} %copy-done.13, f32[2,32,512]{2,1,0:T(8,128)} %copy-done.14, ...), custom_call_target="tpu_custom_call" | custom-call | tf_op jit(solution)/shard_map/pallas_call | solution.py:312
  80.9 17.2 %all_to_all.35 = f32[16,8,512]{2,1,0:T(8,128)S(1)} all-to-all(f32[16,8,512]{2,1,0:T(8,128)} %bitcast.101), channel_id=1, replica_groups=mesh['z'=8,'xl'=2,'co'=2,'y'=4,'xh'=2] {'z','xl'}, dimensions={0} | all-to-all | bytes 524288 | tf_op jit(solution)/shard_map/all_to_all | solution.py:496
  98.2 14.2 %all_to_all.36 = f32[16,8,512]{2,1,0:T(8,128)S(1)} all-to-all(f32[16,8,512]{2,1,0:T(8,128)S(1)} %broadcast_in_dim.19), channel_id=1, replica_groups=mesh['z'=8,'xl'=2,'co'=2,'y'=4,'xh'=2] {'z','xl'}, dimensions={0} | all-to-all | bytes 524288 | tf_op jit(solution)/shard_map/all_to_all | solution.py:64
  112.4 5.0 %all-to-all-start.4 = ((f32[16,64,256]{2,1,0:T(8,128)}), f32[16,64,256]{2,1,0:T(8,128)S(1)}, u32[]{:S(2)}, u32[]{:S(2)}) async-start(f32[16,64,256]{2,1,0:T(8,128)} %get-tuple-element.23), calls=%async_computation.4 | async-start | bytes 2097152 | tf_op jit(solution)/shard_map/all_to_all | solution.py:531
  118.6 3.0 %collective-permute-start.12 = (f32[128,512]{1,0:T(8,128)S(1)}, f32[128,512]{1,0:T(8,128)S(1)}, u32[]{:S(2)}, u32[]{:S(2)}) collective-permute-start(f32[128,512]{1,0:T(8,128)S(1)} %bitcast.97), channel_id=1, source_target_pairs={{0,4},{2,6},{4,0},{6,2},{1,5},{3,7},{5,1},{7,3},{8,12},{10,14},{12... | collective-permute-start | bytes 786440 | tf_op jit(solution)/shard_map/ppermute | solution.py:506
  121.7 5.5 %collective-permute-done.14.refs_5_ = f32[128,512]{1,0:T(8,128)S(1)} collective-permute-done((f32[128,512]{1,0:T(8,128)S(1)}, f32[128,512]{1,0:T(8,128)S(1)}, u32[]{:S(2)}, u32[]{:S(2)}) %collective-permute-start.14) | collective-permute-done | bytes 262176 | tf_op jit(solution)/shard_map/ppermute | solution.py:503
  128.5 3.5 %collective-permute-start.16 = (f32[128,512]{1,0:T(8,128)S(1)}, f32[128,512]{1,0:T(8,128)}, u32[]{:S(2)}, u32[]{:S(2)}) collective-permute-start(f32[128,512]{1,0:T(8,128)S(1)} %collective-permute-done.14.refs_5_), channel_id=1, source_target_pairs={{0,4},{2,6},{4,0},{6,2},{1,5},{3,7},{5,1},{7,3},{8,12},{10,14},{12... | collective-permute-start | bytes 786440 | tf_op jit(solution)/shard_map/ppermute | solution.py:506
  136.5 2.6 %collective-permute-done.15.refs_6_ = f32[128,512]{1,0:T(8,128)} collective-permute-done((f32[128,512]{1,0:T(8,128)S(1)}, f32[128,512]{1,0:T(8,128)}, u32[]{:S(2)}, u32[]{:S(2)}) %collective-permute-start.15) | collective-permute-done | bytes 262176 | tf_op jit(solution)/shard_map/ppermute | solution.py:506
  139.2 2.9 %collective-permute-done.16.refs_7_ = f32[128,512]{1,0:T(8,128)} collective-permute-done((f32[128,512]{1,0:T(8,128)S(1)}, f32[128,512]{1,0:T(8,128)}, u32[]{:S(2)}, u32[]{:S(2)}) %collective-permute-start.16) | collective-permute-done | bytes 262176 | tf_op jit(solution)/shard_map/ppermute | solution.py:506
  145.1 5.3 %shard_map.190 = f32[16,3,128]{2,1,0:T(4,128)} custom-call(s32[3]{0:T(128)} %pad_add_fusion.refs_0_, f32[128,512]{1,0:T(8,128)} %bitcast.100, f32[128,512]{1,0:T(8,128)} %copy-done.9, f32[128,512]{1,0:T(8,128)} %copy-done.10, f32[128,512]{1,0:T(8,128)} %copy-done.11, f32[128,512]{1,0:T(8,128)} %copy-done.8, f32[128,512]{1,0:T(8,128)} %collective-permute-done.15.refs_6_, ...), custom_call_target="tpu_custom_call" | custom-call | tf_op jit(solution)/shard_map/pallas_call | solution.py:312
  150.4 7.3 %all-to-all-start.5 = ((f32[16,3,128]{2,1,0:T(4,128)}), f32[16,3,128]{2,1,0:T(4,128)S(1)}, u32[]{:S(2)}, u32[]{:S(2)}) async-start(f32[16,3,128]{2,1,0:T(4,128)} %shard_map.190), calls=%async_computation.5 | async-start | bytes 65536 | tf_op jit(solution)/shard_map/all_to_all | solution.py:524
  157.8 1.7 fusion
  159.9 5.5 %all-to-all-done.5 = f32[16,3,128]{2,1,0:T(4,128)S(1)} async-done(((f32[16,3,128]{2,1,0:T(4,128)}), f32[16,3,128]{2,1,0:T(4,128)S(1)}, u32[]{:S(2)}, u32[]{:S(2)}) %all-to-all-start.5) | async-done | bytes 24608 | tf_op jit(solution)/shard_map/all_to_all | solution.py:524
  166.1 6.5 %all-to-all-start.6 = ((f32[16,3,128]{2,1,0:T(4,128)}), f32[16,3,128]{2,1,0:T(4,128)S(1)}, u32[]{:S(2)}, u32[]{:S(2)}) async-start(f32[16,3,128]{2,1,0:T(4,128)} %broadcast_in_dim.45), calls=%async_computation.6 | async-start | bytes 65536 | tf_op jit(solution)/shard_map/all_to_all | solution.py:64
  173.4 8.2 %inner.1.refs_1_ = f32[2,512,1024]{2,1,0:T(8,128)} custom-call(bf16[2,512,1024]{2,1,0:T(8,128)(2,1)} %x.1, bf16[2,512,256]{2,1,0:T(8,128)(2,1)} %b.1, bf16[2,512,256]{2,1,0:T(8,128)(2,1)} %refs_2_.5, f32[2,16,512]{2,1,0:T(8,128)} %step.1, f32[2,16,512]{2,1,0:T(8,128)} %get-tuple-element.15.run.refs_3_, f32[1,1024]{1,0:T(1,128)} %broadcast_in_dim_reshape.7.skip), custom_call_target="tpu_custom_call" | custom-call | tf_op jit(solution)/shard_map/inner/pallas_call | solution.py:433
  181.6 2.9 %shard_map.189 = f32[32,32,256]{2,1,0:T(8,128)} custom-call(f32[64,256]{1,0:T(8,128)} %get-tuple-element.25.last, bf16[128,256]{1,0:T(8,128)(2,1)} %bitcast.103, f32[32,128]{1,0:T(8,128)} %get-tuple-element.19.refs_2_.grow, f32[32,128]{1,0:T(8,128)} %get-tuple-element.26.xs), custom_call_target="tpu_custom_call" | custom-call | tf_op jit(solution)/shard_map/pallas_call | solution.py:312
  184.4 2.8 %reshape.127 = f32[32,16,2,256]{3,2,1,0:T(2,128)} reshape(f32[32,32,256]{2,1,0:T(8,128)} %shard_map.189) | data formatting | bytes 2097152 | tf_op jit(solution)/shard_map/reshape | solution.py:484
  189.1 5.3 %shard_map.187.refs_8_ = bf16[2,512,1024]{2,1,0:T(8,128)(2,1)} custom-call(s32[1]{0:T(128)} %bitcast.refs_0_, f32[2,512,1024]{2,1,0:T(8,128)} %inner.1.refs_1_, bf16[2,512,256]{2,1,0:T(8,128)(2,1)} %refs_2_.5, f32[2,16,512]{2,1,0:T(8,128)} %get-tuple-element.15.run.refs_3_, f32[2,8,256]{2,1,0:T(8,128)} %get-tuple-element.16.refs_2_.refs_4_, ...), custom_call_target="tpu_custom_call" | custom-call | tf_op jit(solution)/shard_map/pallas_call | solution.py:548
  194.4 5.3 %shard_map.188 = bf16[2,512,1024]{2,1,0:T(8,128)(2,1)} custom-call(s32[1]{0:T(128)} %bitcast.refs_0_, f32[2,512,1024]{2,1,0:T(8,128)} %inner.1.refs_1_, bf16[2,512,256]{2,1,0:T(8,128)(2,1)} %refs_2_.5, f32[2,16,512]{2,1,0:T(8,128)} %get-tuple-element.15.run.refs_3_, f32[2,8,256]{2,1,0:T(8,128)} %get-tuple-element.16.refs_2_.refs_4_, ...), custom_call_target="tpu_custom_call", output_to_operand_aliasing={{}: (8, {})} | custom-call | tf_op jit(solution)/shard_map/pallas_call | solution.py:548
  (155 shorter events, 34.3 us)
Async XLA Ops:
  8.8 3.0 %collective-permute-start = (f32[2,520,256]{2,1,0:T(8,128)}, f32[2,520,256]{2,1,0:T(8,128)S(1)}, u32[]{:S(2)}, u32[]{:S(2)}) collective-permute-start(f32[2,520,256]{2,1,0:T(8,128)} %get-tuple-element.18), channel_id=1, source_target_pairs={{0,8},{8,0},{1,9},{9,1},{2,10},{10,2},{3,11},{11,3},{4,12},{12,4},... | collective-permute-start | bytes 3194888 | tf_op jit(solution)/shard_map/ppermute | solution.py:59
  16.5 40.5 %all-to-all-start = ((f32[16,72,256]{2,1,0:T(8,128)}), f32[16,72,256]{2,1,0:T(8,128)S(1)}, u32[]{:S(2)}, u32[]{:S(2)}) async-start(f32[16,72,256]{2,1,0:T(8,128)} %pair.1), calls=%async_computation | async-start | bytes 2359296 | tf_op jit(solution)/shard_map/all_to_all | solution.py:463
  27.3 2.0 collective-permute-start.2
  30.1 36.7 %collective-permute-start.3 = (f32[2,32,512]{2,1,0:T(8,128)}, f32[2,32,512]{2,1,0:T(8,128)S(1)}, u32[]{:S(2)}, u32[]{:S(2)}) collective-permute-start(f32[2,32,512]{2,1,0:T(8,128)} %get-tuple-element.31), channel_id=1, source_target_pairs={{0,1},{1,0},{2,3},{3,2},{4,5},{5,4},{6,7},{7,6},{8,9},{9,8},{10,11... | collective-permute-start | bytes 393224 | tf_op jit(solution)/shard_map/ppermute | solution.py:380
  32.2 40.7 %collective-permute-start.4 = (f32[2,32,512]{2,1,0:T(8,128)S(1)}, f32[2,32,512]{2,1,0:T(8,128)S(1)}, u32[]{:S(2)}, u32[]{:S(2)}) collective-permute-start(f32[2,32,512]{2,1,0:T(8,128)S(1)} %get-tuple-element.32), channel_id=1, source_target_pairs={{0,2},{1,3},{2,4},{3,5},{4,6},{5,7},{6,0},{7,1},{8,10},{9,11},{10,... | collective-permute-start | bytes 393224 | tf_op jit(solution)/shard_map/ppermute | solution.py:380
  33.8 40.3 %collective-permute-start.5 = (f32[2,32,512]{2,1,0:T(8,128)S(1)}, f32[2,32,512]{2,1,0:T(8,128)S(1)}, u32[]{:S(2)}, u32[]{:S(2)}) collective-permute-start(f32[2,32,512]{2,1,0:T(8,128)S(1)} %get-tuple-element.33), channel_id=1, source_target_pairs={{0,3},{1,2},{2,5},{3,4},{4,7},{5,6},{6,1},{7,0},{8,11},{9,10},{10,... | collective-permute-start | bytes 393224 | tf_op jit(solution)/shard_map/ppermute | solution.py:380
  46.0 29.7 %collective-permute-start.6 = (f32[2,32,512]{2,1,0:T(8,128)S(1)}, f32[2,32,512]{2,1,0:T(8,128)S(1)}, u32[]{:S(2)}, u32[]{:S(2)}) collective-permute-start(f32[2,32,512]{2,1,0:T(8,128)S(1)} %get-tuple-element.34), channel_id=1, source_target_pairs={{0,4},{1,5},{2,6},{3,7},{4,0},{5,1},{6,2},{7,3},{8,12},{9,13},{10,... | collective-permute-start | bytes 393224 | tf_op jit(solution)/shard_map/ppermute | solution.py:380
  47.6 28.1 %collective-permute-start.9 = (f32[2,32,512]{2,1,0:T(8,128)S(1)}, f32[2,32,512]{2,1,0:T(8,128)S(1)}, u32[]{:S(2)}, u32[]{:S(2)}) collective-permute-start(f32[2,32,512]{2,1,0:T(8,128)S(1)} %get-tuple-element.29), channel_id=1, source_target_pairs={{0,7},{1,6},{2,1},{3,0},{4,3},{5,2},{6,5},{7,4},{8,15},{9,14},{10,... | collective-permute-start | bytes 393224 | tf_op jit(solution)/shard_map/ppermute | solution.py:380
  60.8 14.2 %all-to-all-start.1 = ((f32[8,32,128]{2,1,0:T(8,128)}), f32[8,32,128]{2,1,0:T(8,128)S(1)}, u32[]{:S(2)}, u32[]{:S(2)}) async-start(f32[8,32,128]{2,1,0:T(8,128)} %get-tuple-element.22), calls=%async_computation.1 | async-start | bytes 262144 | tf_op jit(solution)/shard_map/all_to_all | solution.py:486
  66.9 9.7 %collective-permute-start.7 = (f32[2,32,512]{2,1,0:T(8,128)S(1)}, f32[2,32,512]{2,1,0:T(8,128)S(1)}, u32[]{:S(2)}, u32[]{:S(2)}) collective-permute-start(f32[2,32,512]{2,1,0:T(8,128)S(1)} %get-tuple-element.36), channel_id=1, source_target_pairs={{0,5},{1,4},{2,7},{3,6},{4,1},{5,0},{6,3},{7,2},{8,13},{9,12},{10,... | collective-permute-start | bytes 393224 | tf_op jit(solution)/shard_map/ppermute | solution.py:380
  72.9 5.0 %collective-permute-start.8 = (f32[2,32,512]{2,1,0:T(8,128)S(1)}, f32[2,32,512]{2,1,0:T(8,128)S(1)}, u32[]{:S(2)}, u32[]{:S(2)}) collective-permute-start(f32[2,32,512]{2,1,0:T(8,128)S(1)} %get-tuple-element.35), channel_id=1, source_target_pairs={{0,6},{1,7},{2,0},{3,1},{4,2},{5,3},{6,4},{7,5},{8,14},{9,15},{10,... | collective-permute-start | bytes 393224 | tf_op jit(solution)/shard_map/ppermute | solution.py:380
  75.0 2.8 %collective-permute-start.1 = (f32[8,32,128]{2,1,0:T(8,128)S(1)}, f32[8,32,128]{2,1,0:T(8,128)S(1)}, u32[]{:S(2)}, u32[]{:S(2)}) collective-permute-start(f32[8,32,128]{2,1,0:T(8,128)S(1)} %all-to-all-done.1.refs_1_), channel_id=1, source_target_pairs={{0,8},{8,0},{1,9},{9,1},{2,10},{10,2},{3,11},{11,3},{4,12},{12,4},... | collective-permute-start | bytes 393224 | tf_op jit(solution)/shard_map/ppermute | solution.py:59
  80.9 63.0 %copy-start.1 = (f32[2,520,256]{2,1,0:T(8,128)S(1)}, f32[2,520,256]{2,1,0:T(8,128)}, u32[]{:S(2)}) copy-start(f32[2,520,256]{2,1,0:T(8,128)} %copy-done) | copy-start | bytes 3194884
  112.4 38.1 %all-to-all-start.4 = ((f32[16,64,256]{2,1,0:T(8,128)}), f32[16,64,256]{2,1,0:T(8,128)S(1)}, u32[]{:S(2)}, u32[]{:S(2)}) async-start(f32[16,64,256]{2,1,0:T(8,128)} %get-tuple-element.23), calls=%async_computation.4 | async-start | bytes 2097152 | tf_op jit(solution)/shard_map/all_to_all | solution.py:531
  117.4 9.9 %collective-permute-start.14 = (f32[128,512]{1,0:T(8,128)S(1)}, f32[128,512]{1,0:T(8,128)S(1)}, u32[]{:S(2)}, u32[]{:S(2)}) collective-permute-start(f32[128,512]{1,0:T(8,128)S(1)} %bitcast.95), channel_id=1, source_target_pairs={{0,1},{1,0},{2,3},{3,2},{4,5},{5,4},{6,7},{7,6},{8,9},{9,8},{10,11... | collective-permute-start | bytes 786440 | tf_op jit(solution)/shard_map/ppermute | solution.py:503
  117.4 11.1 %collective-permute-start.11 = (f32[128,512]{1,0:T(8,128)S(1)}, f32[128,512]{1,0:T(8,128)S(1)}, u32[]{:S(2)}, u32[]{:S(2)}) collective-permute-start(f32[128,512]{1,0:T(8,128)S(1)} %bitcast.96), channel_id=1, source_target_pairs={{0,2},{2,4},{4,6},{6,0},{1,3},{3,5},{5,7},{7,1},{8,10},{10,12},{12... | collective-permute-start | bytes 786440 | tf_op jit(solution)/shard_map/ppermute | solution.py:506
  118.6 13.4 %collective-permute-start.12 = (f32[128,512]{1,0:T(8,128)S(1)}, f32[128,512]{1,0:T(8,128)S(1)}, u32[]{:S(2)}, u32[]{:S(2)}) collective-permute-start(f32[128,512]{1,0:T(8,128)S(1)} %bitcast.97), channel_id=1, source_target_pairs={{0,4},{2,6},{4,0},{6,2},{1,5},{3,7},{5,1},{7,3},{8,12},{10,14},{12... | collective-permute-start | bytes 786440 | tf_op jit(solution)/shard_map/ppermute | solution.py:506
  121.6 11.4 %collective-permute-start.13 = (f32[128,512]{1,0:T(8,128)S(1)}, f32[128,512]{1,0:T(8,128)S(1)}, u32[]{:S(2)}, u32[]{:S(2)}) collective-permute-start(f32[128,512]{1,0:T(8,128)S(1)} %bitcast.98), channel_id=1, source_target_pairs={{0,6},{2,0},{4,2},{6,4},{1,7},{3,1},{5,3},{7,5},{8,14},{10,8},{12,... | collective-permute-start | bytes 786440 | tf_op jit(solution)/shard_map/ppermute | solution.py:506
  121.7 11.3 %collective-permute-start.18 = (f32[128,512]{1,0:T(8,128)S(1)}, f32[128,512]{1,0:T(8,128)S(1)}, u32[]{:S(2)}, u32[]{:S(2)}) collective-permute-start(f32[128,512]{1,0:T(8,128)S(1)} %bitcast.99), channel_id=1, source_target_pairs={{0,8},{8,0},{1,9},{9,1},{2,10},{10,2},{3,11},{11,3},{4,12},{12,4},... | collective-permute-start | bytes 786440 | tf_op jit(solution)/shard_map/ppermute | solution.py:59
  127.2 11.9 %collective-permute-start.15 = (f32[128,512]{1,0:T(8,128)S(1)}, f32[128,512]{1,0:T(8,128)}, u32[]{:S(2)}, u32[]{:S(2)}) collective-permute-start(f32[128,512]{1,0:T(8,128)S(1)} %collective-permute-done.14.refs_5_), channel_id=1, source_target_pairs={{0,2},{2,4},{4,6},{6,0},{1,3},{3,5},{5,7},{7,1},{8,10},{10,12},{12... | collective-permute-start | bytes 786440 | tf_op jit(solution)/shard_map/ppermute | solution.py:506
  128.5 13.6 %collective-permute-start.16 = (f32[128,512]{1,0:T(8,128)S(1)}, f32[128,512]{1,0:T(8,128)}, u32[]{:S(2)}, u32[]{:S(2)}) collective-permute-start(f32[128,512]{1,0:T(8,128)S(1)} %collective-permute-done.14.refs_5_), channel_id=1, source_target_pairs={{0,4},{2,6},{4,0},{6,2},{1,5},{3,7},{5,1},{7,3},{8,12},{10,14},{12... | collective-permute-start | bytes 786440 | tf_op jit(solution)/shard_map/ppermute | solution.py:506
  131.9 10.1 %collective-permute-start.17 = (f32[128,512]{1,0:T(8,128)S(1)}, f32[128,512]{1,0:T(8,128)}, u32[]{:S(2)}, u32[]{:S(2)}) collective-permute-start(f32[128,512]{1,0:T(8,128)S(1)} %collective-permute-done.14.refs_5_), channel_id=1, source_target_pairs={{0,6},{2,0},{4,2},{6,4},{1,7},{3,1},{5,3},{7,5},{8,14},{10,8},{12,... | collective-permute-start | bytes 786440 | tf_op jit(solution)/shard_map/ppermute | solution.py:506
  133.0 9.6 %collective-permute-start.19 = (f32[128,512]{1,0:T(8,128)S(1)}, f32[128,512]{1,0:T(8,128)}, u32[]{:S(2)}, u32[]{:S(2)}) collective-permute-start(f32[128,512]{1,0:T(8,128)S(1)} %collective-permute-done.11.refs_2_), channel_id=1, source_target_pairs={{0,8},{8,0},{1,9},{9,1},{2,10},{10,2},{3,11},{11,3},{4,12},{12,4},... | collective-permute-start | bytes 786440 | tf_op jit(solution)/shard_map/ppermute | solution.py:59
  134.4 8.2 %collective-permute-start.20 = (f32[128,512]{1,0:T(8,128)S(1)}, f32[128,512]{1,0:T(8,128)}, u32[]{:S(2)}, u32[]{:S(2)}) collective-permute-start(f32[128,512]{1,0:T(8,128)S(1)} %collective-permute-done.12.refs_3_), channel_id=1, source_target_pairs={{0,8},{8,0},{1,9},{9,1},{2,10},{10,2},{3,11},{11,3},{4,12},{12,4},... | collective-permute-start | bytes 786440 | tf_op jit(solution)/shard_map/ppermute | solution.py:59
  139.2 5.0 %collective-permute-start.22 = (f32[128,512]{1,0:T(8,128)S(1)}, f32[128,512]{1,0:T(8,128)}, u32[]{:S(2)}, u32[]{:S(2)}) collective-permute-start(f32[128,512]{1,0:T(8,128)S(1)} %collective-permute-done.14.refs_5_), channel_id=1, source_target_pairs={{0,8},{8,0},{1,9},{9,1},{2,10},{10,2},{3,11},{11,3},{4,12},{12,4},... | collective-permute-start | bytes 786440 | tf_op jit(solution)/shard_map/ppermute | solution.py:59
  142.1 2.1 %collective-permute-start.21 = (f32[128,512]{1,0:T(8,128)}, f32[128,512]{1,0:T(8,128)}, u32[]{:S(2)}, u32[]{:S(2)}) collective-permute-start(f32[128,512]{1,0:T(8,128)} %copy-done.11), channel_id=1, source_target_pairs={{0,8},{8,0},{1,9},{9,1},{2,10},{10,2},{3,11},{11,3},{4,12},{12,4},... | collective-permute-start | bytes 786440 | tf_op jit(solution)/shard_map/ppermute | solution.py:59
  142.1 2.2 %collective-permute-start.23 = (f32[128,512]{1,0:T(8,128)}, f32[128,512]{1,0:T(8,128)}, u32[]{:S(2)}, u32[]{:S(2)}) collective-permute-start(f32[128,512]{1,0:T(8,128)} %collective-permute-done.15.refs_6_), channel_id=1, source_target_pairs={{0,8},{8,0},{1,9},{9,1},{2,10},{10,2},{3,11},{11,3},{4,12},{12,4},... | collective-permute-start | bytes 786440 | tf_op jit(solution)/shard_map/ppermute | solution.py:59
  142.6 2.1 %collective-permute-start.24 = (f32[128,512]{1,0:T(8,128)}, f32[128,512]{1,0:T(8,128)}, u32[]{:S(2)}, u32[]{:S(2)}) collective-permute-start(f32[128,512]{1,0:T(8,128)} %collective-permute-done.16.refs_7_), channel_id=1, source_target_pairs={{0,8},{8,0},{1,9},{9,1},{2,10},{10,2},{3,11},{11,3},{4,12},{12,4},... | collective-permute-start | bytes 786440 | tf_op jit(solution)/shard_map/ppermute | solution.py:59
  142.7 2.4 %collective-permute-start.25 = (f32[128,512]{1,0:T(8,128)}, f32[128,512]{1,0:T(8,128)}, u32[]{:S(2)}, u32[]{:S(2)}) collective-permute-start(f32[128,512]{1,0:T(8,128)} %collective-permute-done.17.refs_8_), channel_id=1, source_target_pairs={{0,8},{8,0},{1,9},{9,1},{2,10},{10,2},{3,11},{11,3},{4,12},{12,4},... | collective-permute-start | bytes 786440 | tf_op jit(solution)/shard_map/ppermute | solution.py:59
  150.4 15.0 %all-to-all-start.5 = ((f32[16,3,128]{2,1,0:T(4,128)}), f32[16,3,128]{2,1,0:T(4,128)S(1)}, u32[]{:S(2)}, u32[]{:S(2)}) async-start(f32[16,3,128]{2,1,0:T(4,128)} %shard_map.190), calls=%async_computation.5 | async-start | bytes 65536 | tf_op jit(solution)/shard_map/all_to_all | solution.py:524
  159.5 28.6 %collective-permute-start.10 = (f32[16,2,32,256]{3,2,1,0:T(8,128)}, f32[16,2,32,256]{3,2,1,0:T(8,128)S(1)}, u32[]{:S(2)}, u32[]{:S(2)}) collective-permute-start(f32[16,2,32,256]{3,2,1,0:T(8,128)} %get-tuple-element.27), channel_id=1, source_target_pairs={{0,8},{8,0},{1,9},{9,1},{2,10},{10,2},{3,11},{11,3},{4,12},{12,4},... | collective-permute-start | bytes 3145736 | tf_op jit(solution)/shard_map/ppermute | solution.py:59
  166.1 21.1 %all-to-all-start.6 = ((f32[16,3,128]{2,1,0:T(4,128)}), f32[16,3,128]{2,1,0:T(4,128)S(1)}, u32[]{:S(2)}, u32[]{:S(2)}) async-start(f32[16,3,128]{2,1,0:T(4,128)} %broadcast_in_dim.45), calls=%async_computation.6 | async-start | bytes 65536 | tf_op jit(solution)/shard_map/all_to_all | solution.py:64
  (26 other events, 345.0 us)

commit v3 on v2

--- a/solution.py
+++ b/solution.py
@@ -129,12 +129,12 @@
     send[0, :half] = state[half:]
 
 
-def pair_kernel(p2, heads, core, keep, logs, came, came_logs, out):
+def pair_kernel(p2, heads, core, keep, logs, came, out):
     rows = heads * p2
     first = core[0] == 0
     for s in range(keep.shape[0]):
         mine = logs[s, 4:5]
-        other = came_logs[s, :1]
+        other = came[s, keep.shape[1] : keep.shape[1] + 1]
         f_mine = jnp.where(first, jnp.exp(column(other, rows, p2)), 1.0)
         f_came = jnp.where(first, 1.0, jnp.exp(column(mine, rows, p2)))
         for k in range(keep.shape[1] // rows):
@@ -201,12 +201,13 @@
             row_state[s * per + r] = growth[:, q : q + 1] * value
 
 
-def project_kernel(ny, nxh, place, own, other, *refs):
+def project_kernel(ny, nxh, own, other, *refs):
     pieces, out = refs[:-1], refs[-1]
+    iy, ixh = lax.axis_index(Y), lax.axis_index(XH)
     left, right = [], []
     for number, piece in enumerate(pieces):
         dy, dx = number // nxh, number % nxh
-        at = lax.rem(place[1] + (ny - dy), ny) * nxh + lax.rem(place[2] + (nxh - dx), nxh)
+        at = lax.rem(iy + (ny - dy), ny) * nxh + lax.rem(ixh + (nxh - dx), nxh)
         left += [own[at], other[at]]
         right.append(piece[...].reshape(-1, piece.shape[2]))
     left = jnp.concatenate(left, axis=0).T.astype(BF16)
@@ -214,26 +215,41 @@
     out[...] = dot(left, right, ((1,), (0,)))
 
 
-def logits_kernel(ny, nxh, steps, place, *refs):
-    arrays, (gain, head, allowed, chosen, out) = refs[: 2 * len(steps)], refs[2 * len(steps) :]
+def logits_kernel(ny, nxh, steps, *refs):
+    number = 2 * len(steps)
+    arrays = refs[:number]
+    gain, head, allowed, chosen, out, got, weights, sems = refs[number:]
     many, width = arrays[0].shape
     model = head.shape[0]
-    total = jnp.zeros((many, 128), F32)
-    for ref in arrays:
-        part = ref[...]
+    core, iy, ixh = (lax.axis_index(a) for a in (CO, Y, XH))
+    starts, waits = [], []
+    for j, ref in enumerate(arrays):
+        dy, dx = steps[j // 2]
+        of_y = lax.rem(iy + (ny - dy), ny)
+        of_x = lax.rem(ixh + (nxh - dx), nxh)
+        block = (((core + j % 2) % 2) * ny + of_y) * nxh + of_x
+        starts.append(pl.multiple_of(block * width, width))
+        pair = (
+            pltpu.make_async_copy(ref, got.at[j], sems.at[2 * j]),
+            pltpu.make_async_copy(
+                head.at[pl.ds(starts[j], width)], weights.at[j], sems.at[2 * j + 1]
+            ),
+        )
+        for copy in pair:
+            copy.start()
+        waits.append(pair)
+    squares = jnp.zeros((many, 128), F32)
+    acc = jnp.zeros((many, head.shape[1]), F32)
+    for j in range(number):
+        for copy in waits[j]:
+            copy.wait()
+        part = got[j]
+        scaled = (part * gain[:, pl.ds(starts[j], width)]).astype(BF16)
+        acc = acc + dot(scaled, weights[j], ((1,), (0,)))
         part = part * part
         for k in range(width // 128):
-            total = total + part[:, k * 128 : (k + 1) * 128]
-    scale = lax.rsqrt(jnp.sum(total, axis=1, keepdims=True) / model + EPS)
-    acc = jnp.zeros((many, head.shape[1]), F32)
-    for number, ref in enumerate(arrays):
-        side, (dy, dx) = number // len(steps), steps[number % len(steps)]
-        of_y = lax.rem(place[1] + (ny - dy), ny)
-        of_x = lax.rem(place[2] + (nxh - dx), nxh)
-        block = ((place[0] ^ side) * ny + of_y) * nxh + of_x
-        at = pl.ds(pl.multiple_of(block * width, width), width)
-        normed = (ref[...] * scale * gain[:, at]).astype(BF16)
-        acc = acc + dot(normed, head[at], ((1,), (0,)))
+            squares = squares + part[:, k * 128 : (k + 1) * 128]
+    acc = acc * lax.rsqrt(jnp.sum(squares, axis=1, keepdims=True) / model + EPS)
     acc = acc.T
     ok = allowed[...] > 0.5
     top = jnp.max(jnp.where(ok, acc, NEG_BIG), axis=0, keepdims=True)
@@ -265,27 +281,34 @@
         out[0, :, at] = inner + skip[:, at] * xb[:, at].astype(F32)
 
 
-def carry_kernel(zx, p2, heads, core, inner, c, run, logs, own, other, e0, *refs):
-    out, perm = refs[-2:]
-    tokens, width = inner.shape[1], inner.shape[2]
+def carry_kernel(
+    zx, p2, heads, core, inner, c, run, logs, own, other, came, came_log, kept, e0, *refs
+):
+    out, both = refs[-2:]
+    width = inner.shape[2]
     head_dim = width // heads
     rows = heads * p2
-    blocks = tokens // BLOCK
-    goes = local_index(iota((width, 1), 0), core[0], head_dim, zx, p2, heads)
-    perm[...] = (iota((width, width), 1) == goes).astype(BF16)
-    enter = jnp.concatenate(
-        [own[:, 0].reshape(zx * rows, -1), other[:, 0].reshape(zx * rows, -1)], axis=0
-    )
-    n = enter.shape[1]
-    fade = jnp.exp(column(logs[0, :1], rows, p2))
-    after = (enter.reshape(2 * zx, rows, n) * fade[None]).reshape(width, n) + e0[0]
-    both = jnp.concatenate([enter.astype(BF16), after.astype(BF16)], axis=1)
-    both = dot(perm[...], both, ((1,), (0,))).astype(BF16)
+
+    @pl.when(pl.program_id(0) == 0)
+    def _():
+        goes = local_index(iota((width, 1), 0), core[0], head_dim, zx, p2, heads)
+        perm = (iota((width, width), 1) == goes).astype(BF16)
+        enter = jnp.concatenate(
+            [own[:, 0].reshape(zx * rows, -1), other[:, 0].reshape(zx * rows, -1)], axis=0
+        )
+        n = enter.shape[1]
+        second = core[0] == 1
+        past = jnp.exp(jnp.where(second, column(came_log[0, :1], rows, p2), 0.0))
+        before = jnp.where(second, jnp.concatenate([came[0], kept[0]], axis=0), 0.0)
+        enter = (enter.reshape(2 * zx, rows, n) * past[None]).reshape(width, n) + before
+        fade = jnp.exp(column(logs[0, :1], rows, p2))
+        after = (enter.reshape(2 * zx, rows, n) * fade[None]).reshape(width, n) + e0[0]
+        for k, value in enumerate((enter, after)):
+            both[k] = dot(perm, value.astype(BF16), ((1,), (0,))).astype(BF16)
+
     growth = dot(in_thirds(jnp.exp(run[0].T), 1), expander(heads, width), ((1,), (0,)))
-    for k in range(blocks):
-        at = slice(k * BLOCK, (k + 1) * BLOCK)
-        carry = dot(c[0, at], both[:, k * n : (k + 1) * n], ((1,), (1,)))
-        out[0, at] = (inner[0, at] + growth[at] * carry).astype(BF16)
+    carry = dot(c[0], both[pl.program_id(0)], ((1,), (1,)))
+    out[0] = (inner[0] + growth * carry).astype(BF16)
 
 
 def merge(parts):
@@ -358,7 +381,6 @@
     wide = model // cg
     ny, nxh = lax.axis_size(Y), lax.axis_size(XH)
     iy, ixh = (lax.axis_index(a).astype(jnp.int32) for a in (Y, XH))
-    place = jnp.stack([core[0], iy, ixh])
     grp_steps = [(dy, dx) for dy in range(ny) for dx in range(nxh)]
 
     def grp_perm(dy, dx):
@@ -445,21 +467,20 @@
         run,
         jnp.repeat(skip_weight, width // heads)[None],
     )
-    chips = zx // 4
     pieces = pl.pallas_call(
         lambda *refs: pair_kernel(p2, heads, *refs),
-        grid=(4,),
+        grid=(1,),
         in_specs=[
             pl.BlockSpec(memory_space=pltpu.SMEM),
-            pl.BlockSpec((seqs, chips * rows, n), lambda j: (0, j, 0)),
+            full((seqs, half, n)),
             full((seqs, 8, n)),
-            pl.BlockSpec((seqs, chips * rows, n), lambda j: (0, j, 0)),
-            pl.BlockSpec((seqs, 8, n), lambda j: (0, half // 8, 0)),
+            full((seqs, half + 8, n)),
         ],
-        out_specs=pl.BlockSpec((chips, 2 * rows + 8, n), lambda j: (j, 0, 0)),
+        out_specs=full((zx, 2 * rows + 8, n)),
         out_shape=shaped(zx, 2 * rows + 8, n),
         name="pair",
-    )(core, keep, logs, came, came)
+    )(core, keep, logs, came)
+    kept_other = swapped(keep)
     pieces = lax.all_to_all(pieces, ZX, 0, 0, tiled=True)
     table = shaped(rows, many)
     grow, xs, add = call(
@@ -485,42 +506,53 @@
 
     ys = lax.all_to_all(step_y, GRP, 0, 0, tiled=True)
     partial = call(
-        lambda *refs: project_kernel(ny, nxh, *refs),
-        shaped(many, wide),
-        place,
-        ys,
-        swapped(ys),
-        *w_own,
-        smem=(0,),
+        lambda *refs: project_kernel(ny, nxh, *refs), shaped(many, wide), ys, swapped(ys), *w_own
     )
     partial = lax.all_to_all(partial.reshape(zx, many // zx, wide), ZX, 0, 0, tiled=True)
     summed = jnp.sum(partial, axis=0)
     own_cols = told(summed, ZX).reshape(many, wide)
-    blocks_y = []
-    for dx in range(nxh):
-        across = own_cols
-        if dx:
-            across = lax.ppermute(own_cols, XH, [(i, (i + dx) % nxh) for i in range(nxh)])
-        for dy in range(ny):
-            shift = [(i, (i + dy) % ny) for i in range(ny)]
-            blocks_y.append((dy, dx, lax.ppermute(across, Y, shift) if dy else across))
+    assert ny == 4 and nxh == 2
+
+    def moved_y(value, by):
+        return lax.ppermute(value, Y, [(i, (i + by) % ny) for i in range(ny)])
+
+    up, down = moved_y(own_cols, 1), moved_y(own_cols, 3)
+    across = lax.ppermute(own_cols, XH, [(0, 1), (1, 0)])
+    up_2 = moved_y(up, 1)
+    across_up, across_down = moved_y(across, 1), moved_y(across, 3)
+    across_2 = moved_y(across_down, 3)
+    blocks_y = [
+        (0, 0, own_cols),
+        (1, 0, up),
+        (3, 0, down),
+        (0, 1, across),
+        (2, 0, up_2),
+        (1, 1, across_up),
+        (3, 1, across_down),
+        (2, 1, across_2),
+    ]
     steps_y = [(dy, dx) for dy, dx, _ in blocks_y]
     own_half = [value for *_, value in blocks_y]
     other_half = [swapped(value) for value in own_half]
     enter, _ = lax.optimization_barrier((enter, own_cols))
 
-    parts = call(
+    halves = [value for pair in zip(own_half, other_half) for value in pair]
+    anywhere = pl.BlockSpec(memory_space=pl.ANY)
+    parts_shape = (size_of((Z, CO)), 3, many)
+    parts = pl.pallas_call(
         lambda *refs: logits_kernel(ny, nxh, steps_y, *refs),
-        shaped(size_of((Z, CO)), 3, many),
-        place,
-        *own_half,
-        *other_half,
-        norm_gain[None],
-        lm_head,
-        allowed,
-        chosen_q,
-        smem=(0,),
-    )
+        grid=(1,),
+        in_specs=[anywhere] * len(halves)
+        + [full((1, model)), anywhere, full(allowed.shape), full(chosen_q.shape)],
+        out_specs=full(parts_shape),
+        out_shape=shaped(*parts_shape),
+        scratch_shapes=[
+            pltpu.VMEM((len(halves), many, wide), F32),
+            pltpu.VMEM((len(halves), wide, vocab), BF16),
+            pltpu.SemaphoreType.DMA((2 * len(halves),)),
+        ],
+        name="logits",
+    )(*halves, norm_gain[None], lm_head, allowed, chosen_q)
     parts = lax.all_to_all(parts, (Z, CO), 0, 0, tiled=True)
     parts = jnp.stack(merge(parts))
     parts = told(parts, (XL, Y, XH))
@@ -529,41 +561,35 @@
     logprob = logprob.reshape(seqs, STEPS, per).transpose(1, 0, 2).reshape(STEPS, decode_rows)
 
     back = lax.all_to_all(enter, ZX, 0, 0, tiled=True).reshape(zx, seqs, rows, n)
-    is_first = core[0] == 0
-
-    def after(log_row, value, state):
-        fade = jnp.exp(jnp.repeat(log_row[:, 0, :heads], p2, axis=1))[None, :, :, None]
-        state = state[:, :half].reshape(seqs, zx, rows, n).transpose(1, 0, 2, 3)
-        return fade * value + state
-
-    for_me = jnp.where(is_first, back, after(came[:, half:], back, came))
-    for_other = jnp.where(is_first, after(logs[:, 4:], back, keep), back)
-    other_side = swapped(for_other)
-
-    assert blocks == 2
+    back_other = swapped(back)
     prompt_y = ()
     for s in range(seqs):
-        of_s = lambda *shape, s=s: pl.BlockSpec((1, *shape), lambda _: (s,) + (0,) * len(shape))
-        states_s = pl.BlockSpec((zx, 1, rows, n), lambda _, s=s: (0, s, 0, 0))
+        of_s = lambda *shape, s=s: pl.BlockSpec((1, *shape), lambda k: (s,) + (0,) * len(shape))
+        at_k = lambda *shape, s=s: pl.BlockSpec((1, BLOCK, *shape), lambda k: (s, k, 0))
+        lanes_k = pl.BlockSpec((1, heads, BLOCK), lambda k, s=s: (s, 0, k))
+        states_s = pl.BlockSpec((zx, 1, rows, n), lambda k, s=s: (0, s, 0, 0))
         prompt_y = pl.pallas_call(
             lambda *refs: carry_kernel(zx, p2, heads, *refs),
-            grid=(1,),
+            grid=(blocks,),
             in_specs=[
                 pl.BlockSpec(memory_space=pltpu.SMEM),
-                of_s(tokens, width),
-                of_s(tokens, n),
-                of_s(heads, tokens),
+                at_k(width),
+                at_k(n),
+                lanes_k,
                 of_s(8, n),
                 states_s,
                 states_s,
+                of_s(half, n),
+                pl.BlockSpec((1, 8, n), lambda k, s=s: (s, half // 8, 0)),
+                of_s(half, n),
                 of_s(width, n),
                 *[pl.BlockSpec(memory_space=pl.ANY) for _ in prompt_y],
             ],
-            out_specs=of_s(tokens, width),
+            out_specs=at_k(width),
             out_shape=shaped(seqs, tokens, width, dtype=BF16),
-            input_output_aliases={8: 0} if prompt_y else {},
-            scratch_shapes=[pltpu.VMEM((width, width), BF16)],
-        )(core, inner, prompt_c, run, logs, for_me, other_side, e0, *prompt_y)
+            input_output_aliases={11: 0} if prompt_y else {},
+            scratch_shapes=[pltpu.VMEM((blocks, width, n), BF16)],
+        )(core, inner, prompt_c, run, logs, back, back_other, came, came, kept_other, e0, *prompt_y)
         prompt_y = (prompt_y,)
     (prompt_y,) = prompt_y
     return (prompt_y, decode_state, logprob)

time: 201 us -> 204 us (1.015)
  waiting for transfers between devices: 31.6 us -> 35.1 us
  starting transfers between devices: 64.3 us -> 67.2 us
  other arithmetic: 3.5 us -> 1.08 us
  local copies, waits for them, and re-layouts: 21 us -> 18.9 us
    pallas_call x3 -> x4, Pallas kernels: 14.4 us -> 20.3 us  [the longest x2 11.9 us: body(): pl.pallas_call(lambda *refs: carry_kernel(zx, p2, heads, *refs), grid=(bl...]
    pallas_call x5 -> x4, Pallas kernels: 15.2 us -> 9.79 us  [call(): pl.pallas_call(kernel, grid=(1,), in_specs=specs, out_specs=tuple((full(o...]
    ppermute x7, waiting for transfers between devices: 12.1 us -> 14.3 us  [the longest x6 7.81 us: moved_y(): return lax.ppermute(value, Y, [(i, (i + by) % ny) for i in range(ny)])]
    unnamed x55 -> x61, local copies, waits for them, and re-layouts: 5.88 us -> 4.76 us
    ppermute x12 -> x13, waiting for transfers between devices: 5.25 us -> 4.37 us  [swapped(): return lax.ppermute(value, CO, [(0, 1), (1, 0)])]
  transfers between devices with their start and end apart: 31 -> 32, of which waited for: 14 -> 11; matrix products, arithmetic and copies ran while one was open for 10% -> 8% of each run, Pallas kernels for 11% -> 10%
where the time goes in v3:
time: 204 us; the launch traced here: 202 us
  starting transfers between devices  67.2 us (33%)
  Pallas kernels  46.4 us (23%)
  waiting for transfers between devices  35.1 us (17%)
  blocking collectives  31.2 us (15%)
  local copies, waits for them, and re-layouts  18.9 us (9%)
    ppermute x7, starting transfers between devices, body(): lax.ppermute(part, GRP, grp_perm(dy, dx))  18.8 us
    all_to_all x1, blocking collectives, body(): lax.all_to_all(partial.reshape(zx, many // zx, wide), ZX, 0, 0, tiled=True)  17 us
    all_to_all x1, blocking collectives, told(): lax.all_to_all(jnp.broadcast_to(value[None], (many, *value.shape)), axes,...  14.2 us
    pallas_call x2, Pallas kernels, body(): pl.pallas_call(lambda *refs: carry_kernel(zx, p2, heads, *refs), grid=(bl...  11.9 us
    ppermute x6, starting transfers between devices, moved_y(): return lax.ppermute(value, Y, [(i, (i + by) % ny) for i in range(ny)])  10.3 us
    all_to_all x1, starting transfers between devices, body(): pieces = lax.all_to_all(pieces, ZX, 0, 0, tiled=True)  9.95 us
    pallas_call x4, Pallas kernels, call(): pl.pallas_call(kernel, grid=(1,), in_specs=specs, out_specs=tuple((full(o...  9.79 us
    all_to_all x1, starting transfers between devices, body(): parts = lax.all_to_all(parts, (Z, CO), 0, 0, tiled=True)  8.25 us
  transfers between devices with their start and end apart: 32, of which 11 were waited for; matrix products, arithmetic and copies ran while one was open for 8% of the time, Pallas kernels for 10%

profile of v3, /device:TPU:2, one launch (start us, length us, event | category | flops | bytes accessed | tf_op | source)
XLA Modules:
  0.0 202.1 jit_solution(14374955720883305798)
XLA Ops:
  0.6 8.1 %states.1 = (f32[2,1024,256]{2,1,0:T(8,128)}, f32[2,512,256]{2,1,0:T(8,128)}, f32[2,520,256]{2,1,0:T(8,128)}, f32[2,16,512]{2,1,0:T(8,128)}, f32[2,8,256]{2,1,0:T(8,128)}) custom-call(s32[1]{0:T(128)} %bitcast.refs_0_, bf16[2,512,1024]{2,1,0:T(8,128)(2,1)} %x.1, bf16[2,512,256]{2,1,0:T(8,128)(2,1)} %b.1, f32[2,16,512]{2,1,0:T(8,128)} %step.1, ...), custom_call_target="tpu_custom_call" | custom-call | tf_op jit(solution)/shard_map/states/pallas_call | solution.py:425
  8.9 2.9 %collective-permute-done.refs_3_.refs_7_.refs_8_ = f32[2,520,256]{2,1,0:T(8,128)S(1)} collective-permute-done((f32[2,520,256]{2,1,0:T(8,128)}, f32[2,520,256]{2,1,0:T(8,128)S(1)}, u32[]{:S(2)}, u32[]{:S(2)}) %collective-permute-start) | collective-permute-done | bytes 1064992 | tf_op jit(solution)/shard_map/ppermute | solution.py:59
  12.7 2.8 %pair.1 = f32[16,72,256]{2,1,0:T(8,128)} custom-call(s32[1]{0:T(128)} %bitcast.refs_0_, f32[2,512,256]{2,1,0:T(8,128)} %get-tuple-element.17.refs_1_, f32[2,8,256]{2,1,0:T(8,128)} %get-tuple-element.16.refs_2_.refs_4_, f32[2,520,256]{2,1,0:T(8,128)} %copy-done), custom_call_target="tpu_custom_call" | custom-call | tf_op jit(solution)/shard_map/pair/pallas_call | solution.py:470
  15.6 10.0 %all-to-all-start = ((f32[16,72,256]{2,1,0:T(8,128)}), f32[16,72,256]{2,1,0:T(8,128)S(1)}, u32[]{:S(2)}, u32[]{:S(2)}) async-start(f32[16,72,256]{2,1,0:T(8,128)} %pair.1), calls=%async_computation | async-start | bytes 2359296 | tf_op jit(solution)/shard_map/all_to_all | solution.py:484
  29.0 2.1 %collective-permute-start.3 = (f32[2,32,512]{2,1,0:T(8,128)}, f32[2,32,512]{2,1,0:T(8,128)S(1)}, u32[]{:S(2)}, u32[]{:S(2)}) collective-permute-start(f32[2,32,512]{2,1,0:T(8,128)} %get-tuple-element.29), channel_id=1, source_target_pairs={{0,1},{1,0},{2,3},{3,2},{4,5},{5,4},{6,7},{7,6},{8,9},{9,8},{10,11... | collective-permute-start | bytes 393224 | tf_op jit(solution)/shard_map/ppermute | solution.py:402
  32.7 2.4 %collective-permute-start.5 = (f32[2,32,512]{2,1,0:T(8,128)S(1)}, f32[2,32,512]{2,1,0:T(8,128)S(1)}, u32[]{:S(2)}, u32[]{:S(2)}) collective-permute-start(f32[2,32,512]{2,1,0:T(8,128)S(1)} %get-tuple-element.31), channel_id=1, source_target_pairs={{0,3},{1,2},{2,5},{3,4},{4,7},{5,6},{6,1},{7,0},{8,11},{9,10},{10,... | collective-permute-start | bytes 393224 | tf_op jit(solution)/shard_map/ppermute | solution.py:402
  43.0 1.9 shard_map.184
  46.4 4.0 %collective-permute-start.9 = (f32[2,32,512]{2,1,0:T(8,128)S(1)}, f32[2,32,512]{2,1,0:T(8,128)S(1)}, u32[]{:S(2)}, u32[]{:S(2)}) collective-permute-start(f32[2,32,512]{2,1,0:T(8,128)S(1)} %get-tuple-element.27), channel_id=1, source_target_pairs={{0,7},{1,6},{2,1},{3,0},{4,3},{5,2},{6,5},{7,4},{8,15},{9,14},{10,... | collective-permute-start | bytes 393224 | tf_op jit(solution)/shard_map/ppermute | solution.py:402
  50.4 5.6 %all-to-all-done.refs_0_ = f32[16,72,256]{2,1,0:T(8,128)S(1)} async-done(((f32[16,72,256]{2,1,0:T(8,128)}), f32[16,72,256]{2,1,0:T(8,128)S(1)}, u32[]{:S(2)}, u32[]{:S(2)}) %all-to-all-start) | async-done | bytes 1179680 | tf_op jit(solution)/shard_map/all_to_all | solution.py:484
  57.0 2.7 %shard_map.185 = (f32[16,64,256]{2,1,0:T(8,128)}, f32[8,32,128]{2,1,0:T(8,128)}, f32[64,256]{1,0:T(8,128)}) custom-call(f32[16,72,256]{2,1,0:T(8,128)} %copy-done.2, bf16[128,256]{1,0:T(8,128)(2,1)} %bitcast.90, f32[32,128]{1,0:T(8,128)} %get-tuple-element.19.refs_2_.grow, f32[32,128]{1,0:T(8,128)} %get-tuple-element.20.refs_3_), custom_call_target="tpu_custom_call" | custom-call | tf_op jit(solution)/shard_map/pallas_call | solution.py:335
  59.7 6.0 %all-to-all-start.1 = ((f32[8,32,128]{2,1,0:T(8,128)}), f32[8,32,128]{2,1,0:T(8,128)S(1)}, u32[]{:S(2)}, u32[]{:S(2)}) async-start(f32[8,32,128]{2,1,0:T(8,128)} %get-tuple-element.22), calls=%async_computation.1 | async-start | bytes 262144 | tf_op jit(solution)/shard_map/all_to_all | solution.py:507
  65.8 6.0 %collective-permute-start.7 = (f32[2,32,512]{2,1,0:T(8,128)S(1)}, f32[2,32,512]{2,1,0:T(8,128)S(1)}, u32[]{:S(2)}, u32[]{:S(2)}) collective-permute-start(f32[2,32,512]{2,1,0:T(8,128)S(1)} %get-tuple-element.34), channel_id=1, source_target_pairs={{0,5},{1,4},{2,7},{3,6},{4,1},{5,0},{6,3},{7,2},{8,13},{9,12},{10,... | collective-permute-start | bytes 393224 | tf_op jit(solution)/shard_map/ppermute | solution.py:402
  77.5 2.4 %shard_map.186 = f32[128,512]{1,0:T(8,128)} custom-call(f32[8,32,128]{2,1,0:T(8,128)} %copy-done.7, f32[8,32,128]{2,1,0:T(8,128)} %copy-done.23, f32[2,32,512]{2,1,0:T(8,128)} %get-tuple-element.28.refs_2_, f32[2,32,512]{2,1,0:T(8,128)} %copy-done.16, f32[2,32,512]{2,1,0:T(8,128)} %copy-done.17, f32[2,32,512]{2,1,0:T(8,128)} %copy-done.18, ...), custom_call_target="tpu_custom_call" | custom-call | tf_op jit(solution)/shard_map/pallas_call | solution.py:335
  79.8 17.0 %all_to_all.35 = f32[16,8,512]{2,1,0:T(8,128)S(1)} all-to-all(f32[16,8,512]{2,1,0:T(8,128)} %bitcast.86), channel_id=1, replica_groups=mesh['z'=8,'xl'=2,'co'=2,'y'=4,'xh'=2] {'z','xl'}, dimensions={0} | all-to-all | bytes 524288 | tf_op jit(solution)/shard_map/all_to_all | solution.py:511
  96.9 14.2 %all_to_all.36 = f32[16,8,512]{2,1,0:T(8,128)S(1)} all-to-all(f32[16,8,512]{2,1,0:T(8,128)S(1)} %broadcast_in_dim.15), channel_id=1, replica_groups=mesh['z'=8,'xl'=2,'co'=2,'y'=4,'xh'=2] {'z','xl'}, dimensions={0} | all-to-all | bytes 524288 | tf_op jit(solution)/shard_map/all_to_all | solution.py:64
  111.1 5.0 %all-to-all-start.4 = ((f32[16,64,256]{2,1,0:T(8,128)}), f32[16,64,256]{2,1,0:T(8,128)S(1)}, u32[]{:S(2)}, u32[]{:S(2)}) async-start(f32[16,64,256]{2,1,0:T(8,128)} %get-tuple-element.23), calls=%async_computation.4 | async-start | bytes 2097152 | tf_op jit(solution)/shard_map/all_to_all | solution.py:563
  117.3 2.1 %collective-permute-start.15 = (f32[128,512]{1,0:T(8,128)S(1)}, f32[128,512]{1,0:T(8,128)S(1)}, u32[]{:S(2)}, u32[]{:S(2)}) collective-permute-start(f32[128,512]{1,0:T(8,128)S(1)} %bitcast.83), channel_id=1, source_target_pairs={{0,6},{2,0},{4,2},{6,4},{1,7},{3,1},{5,3},{7,5},{8,14},{10,8},{12,... | collective-permute-start | bytes 786440 | tf_op jit(solution)/shard_map/ppermute | solution.py:517
  119.4 6.5 %collective-permute-done.17.refs_6_ = f32[128,512]{1,0:T(8,128)S(1)} collective-permute-done((f32[128,512]{1,0:T(8,128)S(1)}, f32[128,512]{1,0:T(8,128)S(1)}, u32[]{:S(2)}, u32[]{:S(2)}) %collective-permute-start.17) | collective-permute-done | bytes 262176 | tf_op jit(solution)/shard_map/ppermute | solution.py:520
  126.0 3.2 %collective-permute-start.23 = (f32[128,512]{1,0:T(8,128)S(1)}, f32[128,512]{1,0:T(8,128)S(1)}, u32[]{:S(2)}, u32[]{:S(2)}) collective-permute-start(f32[128,512]{1,0:T(8,128)S(1)} %collective-permute-done.17.refs_6_), channel_id=1, source_target_pairs={{0,6},{2,0},{4,2},{6,4},{1,7},{3,1},{5,3},{7,5},{8,14},{10,8},{12,... | collective-permute-start | bytes 786440 | tf_op jit(solution)/shard_map/ppermute | solution.py:517
  129.9 3.2 %collective-permute-done.23.refs_12_ = f32[128,512]{1,0:T(8,128)S(1)} collective-permute-done((f32[128,512]{1,0:T(8,128)S(1)}, f32[128,512]{1,0:T(8,128)S(1)}, u32[]{:S(2)}, u32[]{:S(2)}) %collective-permute-start.23) | collective-permute-done | bytes 262176 | tf_op jit(solution)/shard_map/ppermute | solution.py:517
  133.0 3.7 %collective-permute-start.25 = (f32[128,512]{1,0:T(8,128)S(1)}, f32[128,512]{1,0:T(8,128)}, u32[]{:S(2)}, u32[]{:S(2)}) collective-permute-start(f32[128,512]{1,0:T(8,128)S(1)} %collective-permute-done.23.refs_12_), channel_id=1, source_target_pairs={{0,6},{2,0},{4,2},{6,4},{1,7},{3,1},{5,3},{7,5},{8,14},{10,8},{12,... | collective-permute-start | bytes 786440 | tf_op jit(solution)/shard_map/ppermute | solution.py:517
  136.7 1.8 collective-permute-done.19.refs_8_
  138.6 2.8 %collective-permute-done.21.refs_10_ = f32[128,512]{1,0:T(8,128)S(1)} collective-permute-done((f32[128,512]{1,0:T(8,128)S(1)}, f32[128,512]{1,0:T(8,128)S(1)}, u32[]{:S(2)}, u32[]{:S(2)}) %collective-permute-start.21) | collective-permute-done | bytes 262176 | tf_op jit(solution)/shard_map/ppermute | solution.py:517
  144.6 5.5 %logits.1 = f32[16,3,128]{2,1,0:T(4,128)} custom-call(f32[128,512]{1,0:T(8,128)} %bitcast.85, f32[128,512]{1,0:T(8,128)} %copy-done.11, f32[128,512]{1,0:T(8,128)} %copy-done.9, f32[128,512]{1,0:T(8,128)} %copy-done.15, f32[128,512]{1,0:T(8,128)} %copy-done.10, f32[128,512]{1,0:T(8,128)} %collective-permute-done.16.refs_5_, f32[128,512]{1,0:T(8,128)} %copy-done.8, ...), custom_call_target="tpu_custom_call" | custom-call | tf_op jit(solution)/shard_map/logits/pallas_call | solution.py:542
  150.2 8.2 %all-to-all-start.5 = ((f32[16,3,128]{2,1,0:T(4,128)}), f32[16,3,128]{2,1,0:T(4,128)S(1)}, u32[]{:S(2)}, u32[]{:S(2)}) async-start(f32[16,3,128]{2,1,0:T(4,128)} %logits.1), calls=%async_computation.5 | async-start | bytes 65536 | tf_op jit(solution)/shard_map/all_to_all | solution.py:556
  159.0 7.1 %all-to-all-done.5 = f32[16,3,128]{2,1,0:T(4,128)S(1)} async-done(((f32[16,3,128]{2,1,0:T(4,128)}), f32[16,3,128]{2,1,0:T(4,128)S(1)}, u32[]{:S(2)}, u32[]{:S(2)}) %all-to-all-start.5) | async-done | bytes 24608 | tf_op jit(solution)/shard_map/all_to_all | solution.py:556
  166.8 6.5 %all-to-all-start.6 = ((f32[16,3,128]{2,1,0:T(4,128)}), f32[16,3,128]{2,1,0:T(4,128)S(1)}, u32[]{:S(2)}, u32[]{:S(2)}) async-start(f32[16,3,128]{2,1,0:T(4,128)} %broadcast_in_dim.17), calls=%async_computation.6 | async-start | bytes 65536 | tf_op jit(solution)/shard_map/all_to_all | solution.py:64
  174.1 8.2 %inner.1.refs_1_ = f32[2,512,1024]{2,1,0:T(8,128)} custom-call(bf16[2,512,1024]{2,1,0:T(8,128)(2,1)} %x.1, bf16[2,512,256]{2,1,0:T(8,128)(2,1)} %b.1, bf16[2,512,256]{2,1,0:T(8,128)(2,1)} %refs_2_.5, f32[2,16,512]{2,1,0:T(8,128)} %step.1, f32[2,16,512]{2,1,0:T(8,128)} %get-tuple-element.15.run.refs_3_, f32[1,1024]{1,0:T(1,128)} %broadcast_in_dim_reshape.7.skip), custom_call_target="tpu_custom_call" | custom-call | tf_op jit(solution)/shard_map/inner/pallas_call | solution.py:455
  182.3 2.8 %shard_map.189 = f32[32,32,256]{2,1,0:T(8,128)} custom-call(f32[64,256]{1,0:T(8,128)} %get-tuple-element.25.last, bf16[128,256]{1,0:T(8,128)(2,1)} %bitcast.88, f32[32,128]{1,0:T(8,128)} %get-tuple-element.19.refs_2_.grow, f32[32,128]{1,0:T(8,128)} %get-tuple-element.26.xs), custom_call_target="tpu_custom_call" | custom-call | tf_op jit(solution)/shard_map/pallas_call | solution.py:335
  185.1 2.8 %reshape.103 = f32[32,16,2,256]{3,2,1,0:T(2,128)} reshape(f32[32,32,256]{2,1,0:T(8,128)} %shard_map.189) | data formatting | bytes 2097152 | tf_op jit(solution)/shard_map/reshape | solution.py:505
  190.1 5.9 %shard_map.187.refs_11_ = bf16[2,512,1024]{2,1,0:T(8,128)(2,1)} custom-call(s32[1]{0:T(128)} %bitcast.refs_0_, f32[2,512,1024]{2,1,0:T(8,128)} %inner.1.refs_1_, bf16[2,512,256]{2,1,0:T(8,128)(2,1)} %refs_2_.5, f32[2,16,512]{2,1,0:T(8,128)} %get-tuple-element.15.run.refs_3_, f32[2,8,256]{2,1,0:T(8,128)} %get-tuple-element.16.refs_2_.refs_4_, ...), custom_call_target="tpu_custom_call" | custom-call | tf_op jit(solution)/shard_map/pallas_call | solution.py:571
  196.1 6.0 %shard_map.188 = bf16[2,512,1024]{2,1,0:T(8,128)(2,1)} custom-call(s32[1]{0:T(128)} %bitcast.refs_0_, f32[2,512,1024]{2,1,0:T(8,128)} %inner.1.refs_1_, bf16[2,512,256]{2,1,0:T(8,128)(2,1)} %refs_2_.5, f32[2,16,512]{2,1,0:T(8,128)} %get-tuple-element.15.run.refs_3_, f32[2,8,256]{2,1,0:T(8,128)} %get-tuple-element.16.refs_2_.refs_4_, ...), custom_call_target="tpu_custom_call", output_to_operand_aliasing={{}: (11, {})} | custom-call | tf_op jit(solution)/shard_map/pallas_call | solution.py:571
  (153 shorter events, 31.2 us)
Async XLA Ops:
  8.8 3.0 %collective-permute-start = (f32[2,520,256]{2,1,0:T(8,128)}, f32[2,520,256]{2,1,0:T(8,128)S(1)}, u32[]{:S(2)}, u32[]{:S(2)}) collective-permute-start(f32[2,520,256]{2,1,0:T(8,128)} %get-tuple-element.18), channel_id=1, source_target_pairs={{0,8},{8,0},{1,9},{9,1},{2,10},{10,2},{3,11},{11,3},{4,12},{12,4},... | collective-permute-start | bytes 3194888 | tf_op jit(solution)/shard_map/ppermute | solution.py:59
  15.6 40.4 %all-to-all-start = ((f32[16,72,256]{2,1,0:T(8,128)}), f32[16,72,256]{2,1,0:T(8,128)S(1)}, u32[]{:S(2)}, u32[]{:S(2)}) async-start(f32[16,72,256]{2,1,0:T(8,128)} %pair.1), calls=%async_computation | async-start | bytes 2359296 | tf_op jit(solution)/shard_map/all_to_all | solution.py:484
  26.2 2.0 collective-permute-start.2
  29.0 36.7 %collective-permute-start.3 = (f32[2,32,512]{2,1,0:T(8,128)}, f32[2,32,512]{2,1,0:T(8,128)S(1)}, u32[]{:S(2)}, u32[]{:S(2)}) collective-permute-start(f32[2,32,512]{2,1,0:T(8,128)} %get-tuple-element.29), channel_id=1, source_target_pairs={{0,1},{1,0},{2,3},{3,2},{4,5},{5,4},{6,7},{7,6},{8,9},{9,8},{10,11... | collective-permute-start | bytes 393224 | tf_op jit(solution)/shard_map/ppermute | solution.py:402
  31.1 40.7 %collective-permute-start.4 = (f32[2,32,512]{2,1,0:T(8,128)S(1)}, f32[2,32,512]{2,1,0:T(8,128)S(1)}, u32[]{:S(2)}, u32[]{:S(2)}) collective-permute-start(f32[2,32,512]{2,1,0:T(8,128)S(1)} %get-tuple-element.30), channel_id=1, source_target_pairs={{0,2},{1,3},{2,4},{3,5},{4,6},{5,7},{6,0},{7,1},{8,10},{9,11},{10,... | collective-permute-start | bytes 393224 | tf_op jit(solution)/shard_map/ppermute | solution.py:402
  32.7 40.3 %collective-permute-start.5 = (f32[2,32,512]{2,1,0:T(8,128)S(1)}, f32[2,32,512]{2,1,0:T(8,128)S(1)}, u32[]{:S(2)}, u32[]{:S(2)}) collective-permute-start(f32[2,32,512]{2,1,0:T(8,128)S(1)} %get-tuple-element.31), channel_id=1, source_target_pairs={{0,3},{1,2},{2,5},{3,4},{4,7},{5,6},{6,1},{7,0},{8,11},{9,10},{10,... | collective-permute-start | bytes 393224 | tf_op jit(solution)/shard_map/ppermute | solution.py:402
  44.9 29.0 %collective-permute-start.6 = (f32[2,32,512]{2,1,0:T(8,128)S(1)}, f32[2,32,512]{2,1,0:T(8,128)S(1)}, u32[]{:S(2)}, u32[]{:S(2)}) collective-permute-start(f32[2,32,512]{2,1,0:T(8,128)S(1)} %get-tuple-element.32), channel_id=1, source_target_pairs={{0,4},{1,5},{2,6},{3,7},{4,0},{5,1},{6,2},{7,3},{8,12},{9,13},{10,... | collective-permute-start | bytes 393224 | tf_op jit(solution)/shard_map/ppermute | solution.py:402
  46.4 27.5 %collective-permute-start.9 = (f32[2,32,512]{2,1,0:T(8,128)S(1)}, f32[2,32,512]{2,1,0:T(8,128)S(1)}, u32[]{:S(2)}, u32[]{:S(2)}) collective-permute-start(f32[2,32,512]{2,1,0:T(8,128)S(1)} %get-tuple-element.27), channel_id=1, source_target_pairs={{0,7},{1,6},{2,1},{3,0},{4,3},{5,2},{6,5},{7,4},{8,15},{9,14},{10,... | collective-permute-start | bytes 393224 | tf_op jit(solution)/shard_map/ppermute | solution.py:402
  59.7 14.2 %all-to-all-start.1 = ((f32[8,32,128]{2,1,0:T(8,128)}), f32[8,32,128]{2,1,0:T(8,128)S(1)}, u32[]{:S(2)}, u32[]{:S(2)}) async-start(f32[8,32,128]{2,1,0:T(8,128)} %get-tuple-element.22), calls=%async_computation.1 | async-start | bytes 262144 | tf_op jit(solution)/shard_map/all_to_all | solution.py:507
  65.8 9.7 %collective-permute-start.7 = (f32[2,32,512]{2,1,0:T(8,128)S(1)}, f32[2,32,512]{2,1,0:T(8,128)S(1)}, u32[]{:S(2)}, u32[]{:S(2)}) collective-permute-start(f32[2,32,512]{2,1,0:T(8,128)S(1)} %get-tuple-element.34), channel_id=1, source_target_pairs={{0,5},{1,4},{2,7},{3,6},{4,1},{5,0},{6,3},{7,2},{8,13},{9,12},{10,... | collective-permute-start | bytes 393224 | tf_op jit(solution)/shard_map/ppermute | solution.py:402
  71.8 5.0 %collective-permute-start.8 = (f32[2,32,512]{2,1,0:T(8,128)S(1)}, f32[2,32,512]{2,1,0:T(8,128)S(1)}, u32[]{:S(2)}, u32[]{:S(2)}) collective-permute-start(f32[2,32,512]{2,1,0:T(8,128)S(1)} %get-tuple-element.33), channel_id=1, source_target_pairs={{0,6},{1,7},{2,0},{3,1},{4,2},{5,3},{6,4},{7,5},{8,14},{9,15},{10,... | collective-permute-start | bytes 393224 | tf_op jit(solution)/shard_map/ppermute | solution.py:402
  73.9 2.8 %collective-permute-start.1 = (f32[8,32,128]{2,1,0:T(8,128)S(1)}, f32[8,32,128]{2,1,0:T(8,128)S(1)}, u32[]{:S(2)}, u32[]{:S(2)}) collective-permute-start(f32[8,32,128]{2,1,0:T(8,128)S(1)} %all-to-all-done.1.refs_0_), channel_id=1, source_target_pairs={{0,8},{8,0},{1,9},{9,1},{2,10},{10,2},{3,11},{11,3},{4,12},{12,4},... | collective-permute-start | bytes 393224 | tf_op jit(solution)/shard_map/ppermute | solution.py:59
  111.1 39.1 %all-to-all-start.4 = ((f32[16,64,256]{2,1,0:T(8,128)}), f32[16,64,256]{2,1,0:T(8,128)S(1)}, u32[]{:S(2)}, u32[]{:S(2)}) async-start(f32[16,64,256]{2,1,0:T(8,128)} %get-tuple-element.23), calls=%async_computation.4 | async-start | bytes 2097152 | tf_op jit(solution)/shard_map/all_to_all | solution.py:563
  116.1 9.9 %collective-permute-start.17 = (f32[128,512]{1,0:T(8,128)S(1)}, f32[128,512]{1,0:T(8,128)S(1)}, u32[]{:S(2)}, u32[]{:S(2)}) collective-permute-start(f32[128,512]{1,0:T(8,128)S(1)} %bitcast.81), channel_id=1, source_target_pairs={{0,1},{1,0},{2,3},{3,2},{4,5},{5,4},{6,7},{7,6},{8,9},{9,8},{10,11... | collective-permute-start | bytes 786440 | tf_op jit(solution)/shard_map/ppermute | solution.py:520
  116.1 13.0 %collective-permute-start.13 = (f32[128,512]{1,0:T(8,128)S(1)}, f32[128,512]{1,0:T(8,128)S(1)}, u32[]{:S(2)}, u32[]{:S(2)}) collective-permute-start(f32[128,512]{1,0:T(8,128)S(1)} %bitcast.82), channel_id=1, source_target_pairs={{0,2},{2,4},{4,6},{6,0},{1,3},{3,5},{5,7},{7,1},{8,10},{10,12},{12... | collective-permute-start | bytes 786440 | tf_op jit(solution)/shard_map/ppermute | solution.py:517
  117.3 12.0 %collective-permute-start.15 = (f32[128,512]{1,0:T(8,128)S(1)}, f32[128,512]{1,0:T(8,128)S(1)}, u32[]{:S(2)}, u32[]{:S(2)}) collective-permute-start(f32[128,512]{1,0:T(8,128)S(1)} %bitcast.83), channel_id=1, source_target_pairs={{0,6},{2,0},{4,2},{6,4},{1,7},{3,1},{5,3},{7,5},{8,14},{10,8},{12,... | collective-permute-start | bytes 786440 | tf_op jit(solution)/shard_map/ppermute | solution.py:517
  119.4 10.0 %collective-permute-start.12 = (f32[128,512]{1,0:T(8,128)S(1)}, f32[128,512]{1,0:T(8,128)S(1)}, u32[]{:S(2)}, u32[]{:S(2)}) collective-permute-start(f32[128,512]{1,0:T(8,128)S(1)} %bitcast.84), channel_id=1, source_target_pairs={{0,8},{8,0},{1,9},{9,1},{2,10},{10,2},{3,11},{11,3},{4,12},{12,4},... | collective-permute-start | bytes 786440 | tf_op jit(solution)/shard_map/ppermute | solution.py:59
  126.0 7.1 %collective-permute-start.23 = (f32[128,512]{1,0:T(8,128)S(1)}, f32[128,512]{1,0:T(8,128)S(1)}, u32[]{:S(2)}, u32[]{:S(2)}) collective-permute-start(f32[128,512]{1,0:T(8,128)S(1)} %collective-permute-done.17.refs_6_), channel_id=1, source_target_pairs={{0,6},{2,0},{4,2},{6,4},{1,7},{3,1},{5,3},{7,5},{8,14},{10,8},{12,... | collective-permute-start | bytes 786440 | tf_op jit(solution)/shard_map/ppermute | solution.py:517
  129.2 9.4 %collective-permute-start.19 = (f32[128,512]{1,0:T(8,128)S(1)}, f32[128,512]{1,0:T(8,128)S(1)}, u32[]{:S(2)}, u32[]{:S(2)}) collective-permute-start(f32[128,512]{1,0:T(8,128)S(1)} %collective-permute-done.13.refs_2_), channel_id=1, source_target_pairs={{0,2},{2,4},{4,6},{6,0},{1,3},{3,5},{5,7},{7,1},{8,10},{10,12},{12... | collective-permute-start | bytes 786440 | tf_op jit(solution)/shard_map/ppermute | solution.py:517
  129.2 12.2 %collective-permute-start.21 = (f32[128,512]{1,0:T(8,128)S(1)}, f32[128,512]{1,0:T(8,128)S(1)}, u32[]{:S(2)}, u32[]{:S(2)}) collective-permute-start(f32[128,512]{1,0:T(8,128)S(1)} %collective-permute-done.17.refs_6_), channel_id=1, source_target_pairs={{0,2},{2,4},{4,6},{6,0},{1,3},{3,5},{5,7},{7,1},{8,10},{10,12},{12... | collective-permute-start | bytes 786440 | tf_op jit(solution)/shard_map/ppermute | solution.py:517
  129.3 12.1 %collective-permute-start.14 = (f32[128,512]{1,0:T(8,128)S(1)}, f32[128,512]{1,0:T(8,128)S(1)}, u32[]{:S(2)}, u32[]{:S(2)}) collective-permute-start(f32[128,512]{1,0:T(8,128)S(1)} %collective-permute-done.13.refs_2_), channel_id=1, source_target_pairs={{0,8},{8,0},{1,9},{9,1},{2,10},{10,2},{3,11},{11,3},{4,12},{12,4},... | collective-permute-start | bytes 786440 | tf_op jit(solution)/shard_map/ppermute | solution.py:59
  129.4 12.5 %collective-permute-start.16 = (f32[128,512]{1,0:T(8,128)S(1)}, f32[128,512]{1,0:T(8,128)}, u32[]{:S(2)}, u32[]{:S(2)}) collective-permute-start(f32[128,512]{1,0:T(8,128)S(1)} %collective-permute-done.15.refs_4_), channel_id=1, source_target_pairs={{0,8},{8,0},{1,9},{9,1},{2,10},{10,2},{3,11},{11,3},{4,12},{12,4},... | collective-permute-start | bytes 786440 | tf_op jit(solution)/shard_map/ppermute | solution.py:59
  133.0 9.0 %collective-permute-start.25 = (f32[128,512]{1,0:T(8,128)S(1)}, f32[128,512]{1,0:T(8,128)}, u32[]{:S(2)}, u32[]{:S(2)}) collective-permute-start(f32[128,512]{1,0:T(8,128)S(1)} %collective-permute-done.23.refs_12_), channel_id=1, source_target_pairs={{0,6},{2,0},{4,2},{6,4},{1,7},{3,1},{5,3},{7,5},{8,14},{10,8},{12,... | collective-permute-start | bytes 786440 | tf_op jit(solution)/shard_map/ppermute | solution.py:517
  138.6 5.9 %collective-permute-start.18 = (f32[128,512]{1,0:T(8,128)S(1)}, f32[128,512]{1,0:T(8,128)}, u32[]{:S(2)}, u32[]{:S(2)}) collective-permute-start(f32[128,512]{1,0:T(8,128)S(1)} %collective-permute-done.17.refs_6_), channel_id=1, source_target_pairs={{0,8},{8,0},{1,9},{9,1},{2,10},{10,2},{3,11},{11,3},{4,12},{12,4},... | collective-permute-start | bytes 786440 | tf_op jit(solution)/shard_map/ppermute | solution.py:59
  141.4 3.1 %collective-permute-start.24 = (f32[128,512]{1,0:T(8,128)S(1)}, f32[128,512]{1,0:T(8,128)}, u32[]{:S(2)}, u32[]{:S(2)}) collective-permute-start(f32[128,512]{1,0:T(8,128)S(1)} %collective-permute-done.23.refs_12_), channel_id=1, source_target_pairs={{0,8},{8,0},{1,9},{9,1},{2,10},{10,2},{3,11},{11,3},{4,12},{12,4},... | collective-permute-start | bytes 786440 | tf_op jit(solution)/shard_map/ppermute | solution.py:59
  141.4 3.1 %collective-permute-start.20 = (f32[128,512]{1,0:T(8,128)S(1)}, f32[128,512]{1,0:T(8,128)}, u32[]{:S(2)}, u32[]{:S(2)}) collective-permute-start(f32[128,512]{1,0:T(8,128)S(1)} %collective-permute-done.19.refs_8_), channel_id=1, source_target_pairs={{0,8},{8,0},{1,9},{9,1},{2,10},{10,2},{3,11},{11,3},{4,12},{12,4},... | collective-permute-start | bytes 786440 | tf_op jit(solution)/shard_map/ppermute | solution.py:59
  141.9 2.6 %collective-permute-start.22 = (f32[128,512]{1,0:T(8,128)S(1)}, f32[128,512]{1,0:T(8,128)}, u32[]{:S(2)}, u32[]{:S(2)}) collective-permute-start(f32[128,512]{1,0:T(8,128)S(1)} %collective-permute-done.21.refs_10_), channel_id=1, source_target_pairs={{0,8},{8,0},{1,9},{9,1},{2,10},{10,2},{3,11},{11,3},{4,12},{12,4},... | collective-permute-start | bytes 786440 | tf_op jit(solution)/shard_map/ppermute | solution.py:59
  142.0 2.5 %collective-permute-start.26 = (f32[128,512]{1,0:T(8,128)}, f32[128,512]{1,0:T(8,128)}, u32[]{:S(2)}, u32[]{:S(2)}) collective-permute-start(f32[128,512]{1,0:T(8,128)} %collective-permute-done.25.refs_14_), channel_id=1, source_target_pairs={{0,8},{8,0},{1,9},{9,1},{2,10},{10,2},{3,11},{11,3},{4,12},{12,4},... | collective-permute-start | bytes 786440 | tf_op jit(solution)/shard_map/ppermute | solution.py:59
  150.2 15.9 %all-to-all-start.5 = ((f32[16,3,128]{2,1,0:T(4,128)}), f32[16,3,128]{2,1,0:T(4,128)S(1)}, u32[]{:S(2)}, u32[]{:S(2)}) async-start(f32[16,3,128]{2,1,0:T(4,128)} %logits.1), calls=%async_computation.5 | async-start | bytes 65536 | tf_op jit(solution)/shard_map/all_to_all | solution.py:556
  158.4 30.3 %collective-permute-start.11 = (f32[2,512,256]{2,1,0:T(8,128)}, f32[2,512,256]{2,1,0:T(8,128)S(1)}, u32[]{:S(2)}, u32[]{:S(2)}) collective-permute-start(f32[2,512,256]{2,1,0:T(8,128)} %get-tuple-element.17.refs_1_), channel_id=1, source_target_pairs={{0,8},{8,0},{1,9},{9,1},{2,10},{10,2},{3,11},{11,3},{4,12},{12,4},... | collective-permute-start | bytes 3145736 | tf_op jit(solution)/shard_map/ppermute | solution.py:59
  158.8 29.9 %collective-permute-start.10 = (f32[16,2,32,256]{3,2,1,0:T(8,128)S(1)}, f32[16,2,32,256]{3,2,1,0:T(8,128)S(1)}, u32[]{:S(2)}, u32[]{:S(2)}) collective-permute-start(f32[16,2,32,256]{3,2,1,0:T(8,128)S(1)} %bitcast.74), channel_id=1, source_target_pairs={{0,8},{8,0},{1,9},{9,1},{2,10},{10,2},{3,11},{11,3},{4,12},{12,4},... | collective-permute-start | bytes 3145736 | tf_op jit(solution)/shard_map/ppermute | solution.py:59
  166.8 21.1 %all-to-all-start.6 = ((f32[16,3,128]{2,1,0:T(4,128)}), f32[16,3,128]{2,1,0:T(4,128)S(1)}, u32[]{:S(2)}, u32[]{:S(2)}) async-start(f32[16,3,128]{2,1,0:T(4,128)} %broadcast_in_dim.17), calls=%async_computation.6 | async-start | bytes 65536 | tf_op jit(solution)/shard_map/all_to_all | solution.py:64
  (29 other events, 416.8 us)

commit v4 on v3

--- a/solution.py
+++ b/solution.py
@@ -16,6 +16,8 @@
 ALL = (Z, XL, CO, Y, XH)
 ZX = (Z, XL)
 CG = (CO, Y, XH)
+
+ROOM = pltpu.CompilerParams(vmem_limit_bytes=24 * 2**20)
 
 NEG_BIG = -1e30
 EPS = 1e-05
@@ -338,6 +340,7 @@
         in_specs=specs,
         out_specs=tuple(full(o.shape) for o in outs) if many else full(outs.shape),
         out_shape=outs,
+        compiler_params=ROOM,
     )(*args)
 
 
@@ -478,6 +481,7 @@
         ],
         out_specs=full((zx, 2 * rows + 8, n)),
         out_shape=shaped(zx, 2 * rows + 8, n),
+        compiler_params=ROOM,
         name="pair",
     )(core, keep, logs, came)
     kept_other = swapped(keep)
@@ -516,7 +520,8 @@
     def moved_y(value, by):
         return lax.ppermute(value, Y, [(i, (i + by) % ny) for i in range(ny)])
 
-    up, down = moved_y(own_cols, 1), moved_y(own_cols, 3)
+    up = moved_y(own_cols, 1)
+    down = moved_y(own_cols, 3)
     across = lax.ppermute(own_cols, XH, [(0, 1), (1, 0)])
     up_2 = moved_y(up, 1)
     across_up, across_down = moved_y(across, 1), moved_y(across, 3)

time: 204 us -> 193 us (0.946)
  Pallas kernels: 46.4 us -> 38.1 us
  local copies, waits for them, and re-layouts: 18.9 us -> 11.1 us
  waiting for transfers between devices: 35.1 us -> 41.4 us
    all_to_all x1, waiting for transfers between devices: 5.57 us -> 12.9 us  [body(): pieces = lax.all_to_all(pieces, ZX, 0, 0, tiled=True)]
    pallas_call x4, Pallas kernels: 9.79 us -> 3.03 us  [call(): pl.pallas_call(kernel, grid=(1,), in_specs=specs, out_specs=tuple((full(o...]
    reshape x5, local copies, waits for them, and re-layouts: 3.06 us -> 0.24 us  [by_q(): value = value.reshape(STEPS, seqs, per, *shape)]
    unnamed x61 -> x49, local copies, waits for them, and re-layouts: 4.76 us -> 4.16 us
  transfers between devices with their start and end apart: 32 -> 32, of which waited for: 11 -> 11; matrix products, arithmetic and copies ran while one was open for 8% -> 6% of each run, Pallas kernels for 10% -> 9%
where the time goes in v4:
time: 193 us; the launch traced here: 192 us
  starting transfers between devices  67.1 us (35%)
  waiting for transfers between devices  41.4 us (21%)
  Pallas kernels  38.1 us (20%)
  blocking collectives  31 us (16%)
  local copies, waits for them, and re-layouts  11.1 us (6%)
    ppermute x7, starting transfers between devices, body(): lax.ppermute(part, GRP, grp_perm(dy, dx))  18.8 us
    all_to_all x1, blocking collectives, body(): lax.all_to_all(partial.reshape(zx, many // zx, wide), ZX, 0, 0, tiled=True)  16.9 us
    all_to_all x1, blocking collectives, told(): lax.all_to_all(jnp.broadcast_to(value[None], (many, *value.shape)), axes,...  14.2 us
    all_to_all x1, waiting for transfers between devices, body(): pieces = lax.all_to_all(pieces, ZX, 0, 0, tiled=True)  12.9 us
    pallas_call x2, Pallas kernels, body(): pl.pallas_call(lambda *refs: carry_kernel(zx, p2, heads, *refs), grid=(bl...  11.9 us
    ppermute x6, starting transfers between devices, moved_y(): return lax.ppermute(value, Y, [(i, (i + by) % ny) for i in range(ny)])  10.4 us
    all_to_all x1, starting transfers between devices, body(): pieces = lax.all_to_all(pieces, ZX, 0, 0, tiled=True)  9.95 us
    pallas_call x1, Pallas kernels, body(): pl.pallas_call(inner_kernel, grid=(seqs, blocks), in_specs=[at_k(width),...  8.18 us
  transfers between devices with their start and end apart: 32, of which 11 were waited for; matrix products, arithmetic and copies ran while one was open for 6% of the time, Pallas kernels for 9%

profile of v4, /device:TPU:2, one launch (start us, length us, event | category | flops | bytes accessed | tf_op | source)
XLA Modules:
  0.0 192.0 jit_solution(8059538604416258169)
XLA Ops:
  0.6 8.1 %states.1 = (f32[2,1024,256]{2,1,0:T(8,128)}, f32[2,512,256]{2,1,0:T(8,128)}, f32[2,520,256]{2,1,0:T(8,128)}, f32[2,16,512]{2,1,0:T(8,128)}, f32[2,8,256]{2,1,0:T(8,128)}) custom-call(s32[1]{0:T(128)} %bitcast.refs_0_, bf16[2,512,1024]{2,1,0:T(8,128)(2,1)} %x.1, bf16[2,512,256]{2,1,0:T(8,128)(2,1)} %b.1, f32[2,16,512]{2,1,0:T(8,128)} %step.1, ...), custom_call_target="tpu_custom_call" | custom-call | tf_op jit(solution)/shard_map/states/pallas_call | solution.py:428
  8.9 2.9 %collective-permute-done.refs_3_.refs_7_.refs_8_ = f32[2,520,256]{2,1,0:T(8,128)S(1)} collective-permute-done((f32[2,520,256]{2,1,0:T(8,128)}, f32[2,520,256]{2,1,0:T(8,128)S(1)}, u32[]{:S(2)}, u32[]{:S(2)}) %collective-permute-start) | collective-permute-done | bytes 1064992 | tf_op jit(solution)/shard_map/ppermute | solution.py:61
  11.8 1.6 copy-done.1
  15.3 10.0 %all-to-all-start = ((f32[16,72,256]{2,1,0:T(8,128)}), f32[16,72,256]{2,1,0:T(8,128)S(1)}, u32[]{:S(2)}, u32[]{:S(2)}) async-start(f32[16,72,256]{2,1,0:T(8,128)} %pair.1), calls=%async_computation | async-start | bytes 2359296 | tf_op jit(solution)/shard_map/all_to_all | solution.py:488
  29.6 2.1 %collective-permute-start.3 = (f32[2,32,512]{2,1,0:T(8,128)S(1)}, f32[2,32,512]{2,1,0:T(8,128)S(1)}, u32[]{:S(2)}, u32[]{:S(2)}) collective-permute-start(f32[2,32,512]{2,1,0:T(8,128)S(1)} %get-tuple-element.29), channel_id=1, source_target_pairs={{0,1},{1,0},{2,3},{3,2},{4,5},{5,4},{6,7},{7,6},{8,9},{9,8},{10,11... | collective-permute-start | bytes 393224 | tf_op jit(solution)/shard_map/ppermute | solution.py:405
  31.7 1.6 collective-permute-start.4
  33.3 2.4 %collective-permute-start.5 = (f32[2,32,512]{2,1,0:T(8,128)}, f32[2,32,512]{2,1,0:T(8,128)S(1)}, u32[]{:S(2)}, u32[]{:S(2)}) collective-permute-start(f32[2,32,512]{2,1,0:T(8,128)} %get-tuple-element.31), channel_id=1, source_target_pairs={{0,3},{1,2},{2,5},{3,4},{4,7},{5,6},{6,1},{7,0},{8,11},{9,10},{10,... | collective-permute-start | bytes 393224 | tf_op jit(solution)/shard_map/ppermute | solution.py:405
  37.3 1.6 collective-permute-start.6
  38.9 4.0 %collective-permute-start.9 = (f32[2,32,512]{2,1,0:T(8,128)}, f32[2,32,512]{2,1,0:T(8,128)S(1)}, u32[]{:S(2)}, u32[]{:S(2)}) collective-permute-start(f32[2,32,512]{2,1,0:T(8,128)} %get-tuple-element.27), channel_id=1, source_target_pairs={{0,7},{1,6},{2,1},{3,0},{4,3},{5,2},{6,5},{7,4},{8,15},{9,14},{10,... | collective-permute-start | bytes 393224 | tf_op jit(solution)/shard_map/ppermute | solution.py:405
  42.8 12.9 %all-to-all-done.refs_0_ = f32[16,72,256]{2,1,0:T(8,128)S(1)} async-done(((f32[16,72,256]{2,1,0:T(8,128)}), f32[16,72,256]{2,1,0:T(8,128)S(1)}, u32[]{:S(2)}, u32[]{:S(2)}) %all-to-all-start) | async-done | bytes 1179680 | tf_op jit(solution)/shard_map/all_to_all | solution.py:488
  55.7 1.4 shard_map.185
  57.1 6.0 %all-to-all-start.1 = ((f32[8,32,128]{2,1,0:T(8,128)}), f32[8,32,128]{2,1,0:T(8,128)S(1)}, u32[]{:S(2)}, u32[]{:S(2)}) async-start(f32[8,32,128]{2,1,0:T(8,128)} %get-tuple-element.22), calls=%async_computation.1 | async-start | bytes 262144 | tf_op jit(solution)/shard_map/all_to_all | solution.py:511
  63.2 6.0 %collective-permute-start.7 = (f32[2,32,512]{2,1,0:T(8,128)S(1)}, f32[2,32,512]{2,1,0:T(8,128)S(1)}, u32[]{:S(2)}, u32[]{:S(2)}) collective-permute-start(f32[2,32,512]{2,1,0:T(8,128)S(1)} %get-tuple-element.34), channel_id=1, source_target_pairs={{0,5},{1,4},{2,7},{3,6},{4,1},{5,0},{6,3},{7,2},{8,13},{9,12},{10,... | collective-permute-start | bytes 393224 | tf_op jit(solution)/shard_map/ppermute | solution.py:405
  71.3 1.6 collective-permute-done.7.refs_7_
  74.5 16.9 %all_to_all.35 = f32[16,8,512]{2,1,0:T(8,128)S(1)} all-to-all(f32[16,8,512]{2,1,0:T(8,128)S(1)} %bitcast.74), channel_id=1, replica_groups=mesh['z'=8,'xl'=2,'co'=2,'y'=4,'xh'=2] {'z','xl'}, dimensions={0} | all-to-all | bytes 524288 | tf_op jit(solution)/shard_map/all_to_all | solution.py:515
  91.4 14.2 %all_to_all.36 = f32[16,8,512]{2,1,0:T(8,128)S(1)} all-to-all(f32[16,8,512]{2,1,0:T(8,128)S(1)} %broadcast_in_dim.15), channel_id=1, replica_groups=mesh['z'=8,'xl'=2,'co'=2,'y'=4,'xh'=2] {'z','xl'}, dimensions={0} | all-to-all | bytes 524288 | tf_op jit(solution)/shard_map/all_to_all | solution.py:66
  105.5 5.0 %all-to-all-start.4 = ((f32[16,64,256]{2,1,0:T(8,128)}), f32[16,64,256]{2,1,0:T(8,128)S(1)}, u32[]{:S(2)}, u32[]{:S(2)}) async-start(f32[16,64,256]{2,1,0:T(8,128)} %get-tuple-element.23), calls=%async_computation.4 | async-start | bytes 2097152 | tf_op jit(solution)/shard_map/all_to_all | solution.py:568
  111.7 2.1 %collective-permute-start.15 = (f32[128,512]{1,0:T(8,128)S(1)}, f32[128,512]{1,0:T(8,128)S(1)}, u32[]{:S(2)}, u32[]{:S(2)}) collective-permute-start(f32[128,512]{1,0:T(8,128)S(1)} %bitcast.91), channel_id=1, source_target_pairs={{0,6},{2,0},{4,2},{6,4},{1,7},{3,1},{5,3},{7,5},{8,14},{10,8},{12,... | collective-permute-start | bytes 786440 | tf_op jit(solution)/shard_map/ppermute | solution.py:521
  113.9 6.5 %collective-permute-done.17.refs_6_ = f32[128,512]{1,0:T(8,128)S(1)} collective-permute-done((f32[128,512]{1,0:T(8,128)S(1)}, f32[128,512]{1,0:T(8,128)S(1)}, u32[]{:S(2)}, u32[]{:S(2)}) %collective-permute-start.17) | collective-permute-done | bytes 262176 | tf_op jit(solution)/shard_map/ppermute | solution.py:525
  120.4 3.3 %collective-permute-start.23 = (f32[128,512]{1,0:T(8,128)S(1)}, f32[128,512]{1,0:T(8,128)S(1)}, u32[]{:S(2)}, u32[]{:S(2)}) collective-permute-start(f32[128,512]{1,0:T(8,128)S(1)} %collective-permute-done.17.refs_6_), channel_id=1, source_target_pairs={{0,6},{2,0},{4,2},{6,4},{1,7},{3,1},{5,3},{7,5},{8,14},{10,8},{12,... | collective-permute-start | bytes 786440 | tf_op jit(solution)/shard_map/ppermute | solution.py:521
  124.4 3.2 %collective-permute-done.23.refs_12_ = f32[128,512]{1,0:T(8,128)S(1)} collective-permute-done((f32[128,512]{1,0:T(8,128)S(1)}, f32[128,512]{1,0:T(8,128)S(1)}, u32[]{:S(2)}, u32[]{:S(2)}) %collective-permute-start.23) | collective-permute-done | bytes 262176 | tf_op jit(solution)/shard_map/ppermute | solution.py:521
  127.6 3.7 %collective-permute-start.25 = (f32[128,512]{1,0:T(8,128)S(1)}, f32[128,512]{1,0:T(8,128)}, u32[]{:S(2)}, u32[]{:S(2)}) collective-permute-start(f32[128,512]{1,0:T(8,128)S(1)} %collective-permute-done.23.refs_12_), channel_id=1, source_target_pairs={{0,6},{2,0},{4,2},{6,4},{1,7},{3,1},{5,3},{7,5},{8,14},{10,8},{12,... | collective-permute-start | bytes 786440 | tf_op jit(solution)/shard_map/ppermute | solution.py:521
  131.3 1.9 %collective-permute-done.19.refs_8_ = f32[128,512]{1,0:T(8,128)S(1)} collective-permute-done((f32[128,512]{1,0:T(8,128)S(1)}, f32[128,512]{1,0:T(8,128)S(1)}, u32[]{:S(2)}, u32[]{:S(2)}) %collective-permute-start.19) | collective-permute-done | bytes 262176 | tf_op jit(solution)/shard_map/ppermute | solution.py:521
  133.2 2.8 %collective-permute-done.21.refs_10_ = f32[128,512]{1,0:T(8,128)S(1)} collective-permute-done((f32[128,512]{1,0:T(8,128)S(1)}, f32[128,512]{1,0:T(8,128)S(1)}, u32[]{:S(2)}, u32[]{:S(2)}) %collective-permute-start.21) | collective-permute-done | bytes 262176 | tf_op jit(solution)/shard_map/ppermute | solution.py:521
  139.2 5.6 %logits.1 = f32[16,3,128]{2,1,0:T(4,128)} custom-call(f32[128,512]{1,0:T(8,128)} %bitcast.93, f32[128,512]{1,0:T(8,128)} %copy-done.10, f32[128,512]{1,0:T(8,128)} %copy-done.8, f32[128,512]{1,0:T(8,128)} %collective-permute-done.14.refs_3_, f32[128,512]{1,0:T(8,128)} %copy-done.9, f32[128,512]{1,0:T(8,128)} %collective-permute-done.16.refs_5_, ...), custom_call_target="tpu_custom_call" | custom-call | tf_op jit(solution)/shard_map/logits/pallas_call | solution.py:547
  144.9 8.0 %all-to-all-start.5 = ((f32[16,3,128]{2,1,0:T(4,128)}), f32[16,3,128]{2,1,0:T(4,128)S(1)}, u32[]{:S(2)}, u32[]{:S(2)}) async-start(f32[16,3,128]{2,1,0:T(4,128)} %logits.1), calls=%async_computation.5 | async-start | bytes 65536 | tf_op jit(solution)/shard_map/all_to_all | solution.py:561
  153.5 7.0 %all-to-all-done.5 = f32[16,3,128]{2,1,0:T(4,128)S(1)} async-done(((f32[16,3,128]{2,1,0:T(4,128)}), f32[16,3,128]{2,1,0:T(4,128)S(1)}, u32[]{:S(2)}, u32[]{:S(2)}) %all-to-all-start.5) | async-done | bytes 24608 | tf_op jit(solution)/shard_map/all_to_all | solution.py:561
  161.2 6.5 %all-to-all-start.6 = ((f32[16,3,128]{2,1,0:T(4,128)}), f32[16,3,128]{2,1,0:T(4,128)S(1)}, u32[]{:S(2)}, u32[]{:S(2)}) async-start(f32[16,3,128]{2,1,0:T(4,128)} %broadcast_in_dim.17), calls=%async_computation.6 | async-start | bytes 65536 | tf_op jit(solution)/shard_map/all_to_all | solution.py:66
  168.5 8.2 %inner.1.refs_1_ = f32[2,512,1024]{2,1,0:T(8,128)} custom-call(bf16[2,512,1024]{2,1,0:T(8,128)(2,1)} %x.1, bf16[2,512,256]{2,1,0:T(8,128)(2,1)} %b.1, bf16[2,512,256]{2,1,0:T(8,128)(2,1)} %refs_2_.5, f32[2,16,512]{2,1,0:T(8,128)} %step.1, f32[2,16,512]{2,1,0:T(8,128)} %get-tuple-element.15.run.refs_3_, f32[1,1024]{1,0:T(1,128)} %broadcast_in_dim_reshape.7.skip), custom_call_target="tpu_custom_call" | custom-call | tf_op jit(solution)/shard_map/inner/pallas_call | solution.py:458
  177.6 1.6 reshape.103
  180.1 6.0 %shard_map.187.refs_11_ = bf16[2,512,1024]{2,1,0:T(8,128)(2,1)} custom-call(s32[1]{0:T(128)} %bitcast.refs_0_, f32[2,512,1024]{2,1,0:T(8,128)} %inner.1.refs_1_, bf16[2,512,256]{2,1,0:T(8,128)(2,1)} %refs_2_.5, f32[2,16,512]{2,1,0:T(8,128)} %get-tuple-element.15.run.refs_3_, f32[2,8,256]{2,1,0:T(8,128)} %get-tuple-element.16.refs_2_.refs_4_, ...), custom_call_target="tpu_custom_call" | custom-call | tf_op jit(solution)/shard_map/pallas_call | solution.py:576
  186.0 6.0 %shard_map.188 = bf16[2,512,1024]{2,1,0:T(8,128)(2,1)} custom-call(s32[1]{0:T(128)} %bitcast.refs_0_, f32[2,512,1024]{2,1,0:T(8,128)} %inner.1.refs_1_, bf16[2,512,256]{2,1,0:T(8,128)(2,1)} %refs_2_.5, f32[2,16,512]{2,1,0:T(8,128)} %get-tuple-element.15.run.refs_3_, f32[2,8,256]{2,1,0:T(8,128)} %get-tuple-element.16.refs_2_.refs_4_, ...), custom_call_target="tpu_custom_call", output_to_operand_aliasing={{}: (11, {})} | custom-call | tf_op jit(solution)/shard_map/pallas_call | solution.py:576
  (141 shorter events, 20.3 us)
Async XLA Ops:
  8.8 3.0 %collective-permute-start = (f32[2,520,256]{2,1,0:T(8,128)}, f32[2,520,256]{2,1,0:T(8,128)S(1)}, u32[]{:S(2)}, u32[]{:S(2)}) collective-permute-start(f32[2,520,256]{2,1,0:T(8,128)} %get-tuple-element.18), channel_id=1, source_target_pairs={{0,8},{8,0},{1,9},{9,1},{2,10},{10,2},{3,11},{11,3},{4,12},{12,4},... | collective-permute-start | bytes 3194888 | tf_op jit(solution)/shard_map/ppermute | solution.py:61
  15.3 40.4 %all-to-all-start = ((f32[16,72,256]{2,1,0:T(8,128)}), f32[16,72,256]{2,1,0:T(8,128)S(1)}, u32[]{:S(2)}, u32[]{:S(2)}) async-start(f32[16,72,256]{2,1,0:T(8,128)} %pair.1), calls=%async_computation | async-start | bytes 2359296 | tf_op jit(solution)/shard_map/all_to_all | solution.py:488
  26.8 2.0 %collective-permute-start.2 = (f32[8,32,512]{2,1,0:T(8,128)S(1)}, f32[8,32,512]{2,1,0:T(8,128)S(1)}, u32[]{:S(2)}, u32[]{:S(2)}) collective-permute-start(f32[8,32,512]{2,1,0:T(8,128)S(1)} %bitcast.95), channel_id=1, source_target_pairs={{0,8},{8,0},{1,9},{9,1},{2,10},{10,2},{3,11},{11,3},{4,12},{12,4},... | collective-permute-start | bytes 1572872 | tf_op jit(solution)/shard_map/ppermute | solution.py:61
  29.6 33.6 %collective-permute-start.3 = (f32[2,32,512]{2,1,0:T(8,128)S(1)}, f32[2,32,512]{2,1,0:T(8,128)S(1)}, u32[]{:S(2)}, u32[]{:S(2)}) collective-permute-start(f32[2,32,512]{2,1,0:T(8,128)S(1)} %get-tuple-element.29), channel_id=1, source_target_pairs={{0,1},{1,0},{2,3},{3,2},{4,5},{5,4},{6,7},{7,6},{8,9},{9,8},{10,11... | collective-permute-start | bytes 393224 | tf_op jit(solution)/shard_map/ppermute | solution.py:405
  31.7 37.5 %collective-permute-start.4 = (f32[2,32,512]{2,1,0:T(8,128)}, f32[2,32,512]{2,1,0:T(8,128)S(1)}, u32[]{:S(2)}, u32[]{:S(2)}) collective-permute-start(f32[2,32,512]{2,1,0:T(8,128)} %get-tuple-element.30), channel_id=1, source_target_pairs={{0,2},{1,3},{2,4},{3,5},{4,6},{5,7},{6,0},{7,1},{8,10},{9,11},{10,... | collective-permute-start | bytes 393224 | tf_op jit(solution)/shard_map/ppermute | solution.py:405
  33.3 37.1 %collective-permute-start.5 = (f32[2,32,512]{2,1,0:T(8,128)}, f32[2,32,512]{2,1,0:T(8,128)S(1)}, u32[]{:S(2)}, u32[]{:S(2)}) collective-permute-start(f32[2,32,512]{2,1,0:T(8,128)} %get-tuple-element.31), channel_id=1, source_target_pairs={{0,3},{1,2},{2,5},{3,4},{4,7},{5,6},{6,1},{7,0},{8,11},{9,10},{10,... | collective-permute-start | bytes 393224 | tf_op jit(solution)/shard_map/ppermute | solution.py:405
  37.3 34.0 %collective-permute-start.6 = (f32[2,32,512]{2,1,0:T(8,128)}, f32[2,32,512]{2,1,0:T(8,128)S(1)}, u32[]{:S(2)}, u32[]{:S(2)}) collective-permute-start(f32[2,32,512]{2,1,0:T(8,128)} %get-tuple-element.32), channel_id=1, source_target_pairs={{0,4},{1,5},{2,6},{3,7},{4,0},{5,1},{6,2},{7,3},{8,12},{9,13},{10,... | collective-permute-start | bytes 393224 | tf_op jit(solution)/shard_map/ppermute | solution.py:405
  38.9 32.5 %collective-permute-start.9 = (f32[2,32,512]{2,1,0:T(8,128)}, f32[2,32,512]{2,1,0:T(8,128)S(1)}, u32[]{:S(2)}, u32[]{:S(2)}) collective-permute-start(f32[2,32,512]{2,1,0:T(8,128)} %get-tuple-element.27), channel_id=1, source_target_pairs={{0,7},{1,6},{2,1},{3,0},{4,3},{5,2},{6,5},{7,4},{8,15},{9,14},{10,... | collective-permute-start | bytes 393224 | tf_op jit(solution)/shard_map/ppermute | solution.py:405
  57.1 14.2 %all-to-all-start.1 = ((f32[8,32,128]{2,1,0:T(8,128)}), f32[8,32,128]{2,1,0:T(8,128)S(1)}, u32[]{:S(2)}, u32[]{:S(2)}) async-start(f32[8,32,128]{2,1,0:T(8,128)} %get-tuple-element.22), calls=%async_computation.1 | async-start | bytes 262144 | tf_op jit(solution)/shard_map/all_to_all | solution.py:511
  63.2 9.8 %collective-permute-start.7 = (f32[2,32,512]{2,1,0:T(8,128)S(1)}, f32[2,32,512]{2,1,0:T(8,128)S(1)}, u32[]{:S(2)}, u32[]{:S(2)}) collective-permute-start(f32[2,32,512]{2,1,0:T(8,128)S(1)} %get-tuple-element.34), channel_id=1, source_target_pairs={{0,5},{1,4},{2,7},{3,6},{4,1},{5,0},{6,3},{7,2},{8,13},{9,12},{10,... | collective-permute-start | bytes 393224 | tf_op jit(solution)/shard_map/ppermute | solution.py:405
  69.2 5.0 %collective-permute-start.8 = (f32[2,32,512]{2,1,0:T(8,128)S(1)}, f32[2,32,512]{2,1,0:T(8,128)S(1)}, u32[]{:S(2)}, u32[]{:S(2)}) collective-permute-start(f32[2,32,512]{2,1,0:T(8,128)S(1)} %get-tuple-element.33), channel_id=1, source_target_pairs={{0,6},{1,7},{2,0},{3,1},{4,2},{5,3},{6,4},{7,5},{8,14},{9,15},{10,... | collective-permute-start | bytes 393224 | tf_op jit(solution)/shard_map/ppermute | solution.py:405
  71.3 2.8 %collective-permute-start.1 = (f32[8,32,128]{2,1,0:T(8,128)S(1)}, f32[8,32,128]{2,1,0:T(8,128)S(1)}, u32[]{:S(2)}, u32[]{:S(2)}) collective-permute-start(f32[8,32,128]{2,1,0:T(8,128)S(1)} %all-to-all-done.1.refs_0_), channel_id=1, source_target_pairs={{0,8},{8,0},{1,9},{9,1},{2,10},{10,2},{3,11},{11,3},{4,12},{12,4},... | collective-permute-start | bytes 393224 | tf_op jit(solution)/shard_map/ppermute | solution.py:61
  105.5 39.3 %all-to-all-start.4 = ((f32[16,64,256]{2,1,0:T(8,128)}), f32[16,64,256]{2,1,0:T(8,128)S(1)}, u32[]{:S(2)}, u32[]{:S(2)}) async-start(f32[16,64,256]{2,1,0:T(8,128)} %get-tuple-element.23), calls=%async_computation.4 | async-start | bytes 2097152 | tf_op jit(solution)/shard_map/all_to_all | solution.py:568
  110.5 9.8 %collective-permute-start.17 = (f32[128,512]{1,0:T(8,128)S(1)}, f32[128,512]{1,0:T(8,128)S(1)}, u32[]{:S(2)}, u32[]{:S(2)}) collective-permute-start(f32[128,512]{1,0:T(8,128)S(1)} %bitcast.89), channel_id=1, source_target_pairs={{0,1},{1,0},{2,3},{3,2},{4,5},{5,4},{6,7},{7,6},{8,9},{9,8},{10,11... | collective-permute-start | bytes 786440 | tf_op jit(solution)/shard_map/ppermute | solution.py:525
  110.6 13.1 %collective-permute-start.13 = (f32[128,512]{1,0:T(8,128)S(1)}, f32[128,512]{1,0:T(8,128)S(1)}, u32[]{:S(2)}, u32[]{:S(2)}) collective-permute-start(f32[128,512]{1,0:T(8,128)S(1)} %bitcast.90), channel_id=1, source_target_pairs={{0,2},{2,4},{4,6},{6,0},{1,3},{3,5},{5,7},{7,1},{8,10},{10,12},{12... | collective-permute-start | bytes 786440 | tf_op jit(solution)/shard_map/ppermute | solution.py:521
  111.7 12.0 %collective-permute-start.15 = (f32[128,512]{1,0:T(8,128)S(1)}, f32[128,512]{1,0:T(8,128)S(1)}, u32[]{:S(2)}, u32[]{:S(2)}) collective-permute-start(f32[128,512]{1,0:T(8,128)S(1)} %bitcast.91), channel_id=1, source_target_pairs={{0,6},{2,0},{4,2},{6,4},{1,7},{3,1},{5,3},{7,5},{8,14},{10,8},{12,... | collective-permute-start | bytes 786440 | tf_op jit(solution)/shard_map/ppermute | solution.py:521
  113.9 10.0 %collective-permute-start.12 = (f32[128,512]{1,0:T(8,128)S(1)}, f32[128,512]{1,0:T(8,128)S(1)}, u32[]{:S(2)}, u32[]{:S(2)}) collective-permute-start(f32[128,512]{1,0:T(8,128)S(1)} %bitcast.92), channel_id=1, source_target_pairs={{0,8},{8,0},{1,9},{9,1},{2,10},{10,2},{3,11},{11,3},{4,12},{12,4},... | collective-permute-start | bytes 786440 | tf_op jit(solution)/shard_map/ppermute | solution.py:61
  120.4 7.2 %collective-permute-start.23 = (f32[128,512]{1,0:T(8,128)S(1)}, f32[128,512]{1,0:T(8,128)S(1)}, u32[]{:S(2)}, u32[]{:S(2)}) collective-permute-start(f32[128,512]{1,0:T(8,128)S(1)} %collective-permute-done.17.refs_6_), channel_id=1, source_target_pairs={{0,6},{2,0},{4,2},{6,4},{1,7},{3,1},{5,3},{7,5},{8,14},{10,8},{12,... | collective-permute-start | bytes 786440 | tf_op jit(solution)/shard_map/ppermute | solution.py:521
  123.7 9.5 %collective-permute-start.19 = (f32[128,512]{1,0:T(8,128)S(1)}, f32[128,512]{1,0:T(8,128)S(1)}, u32[]{:S(2)}, u32[]{:S(2)}) collective-permute-start(f32[128,512]{1,0:T(8,128)S(1)} %collective-permute-done.13.refs_2_), channel_id=1, source_target_pairs={{0,2},{2,4},{4,6},{6,0},{1,3},{3,5},{5,7},{7,1},{8,10},{10,12},{12... | collective-permute-start | bytes 786440 | tf_op jit(solution)/shard_map/ppermute | solution.py:521
  123.7 12.3 %collective-permute-start.21 = (f32[128,512]{1,0:T(8,128)S(1)}, f32[128,512]{1,0:T(8,128)S(1)}, u32[]{:S(2)}, u32[]{:S(2)}) collective-permute-start(f32[128,512]{1,0:T(8,128)S(1)} %collective-permute-done.17.refs_6_), channel_id=1, source_target_pairs={{0,2},{2,4},{4,6},{6,0},{1,3},{3,5},{5,7},{7,1},{8,10},{10,12},{12... | collective-permute-start | bytes 786440 | tf_op jit(solution)/shard_map/ppermute | solution.py:521
  123.8 12.2 %collective-permute-start.14 = (f32[128,512]{1,0:T(8,128)S(1)}, f32[128,512]{1,0:T(8,128)}, u32[]{:S(2)}, u32[]{:S(2)}) collective-permute-start(f32[128,512]{1,0:T(8,128)S(1)} %collective-permute-done.13.refs_2_), channel_id=1, source_target_pairs={{0,8},{8,0},{1,9},{9,1},{2,10},{10,2},{3,11},{11,3},{4,12},{12,4},... | collective-permute-start | bytes 786440 | tf_op jit(solution)/shard_map/ppermute | solution.py:61
  123.9 12.6 %collective-permute-start.16 = (f32[128,512]{1,0:T(8,128)S(1)}, f32[128,512]{1,0:T(8,128)}, u32[]{:S(2)}, u32[]{:S(2)}) collective-permute-start(f32[128,512]{1,0:T(8,128)S(1)} %collective-permute-done.15.refs_4_), channel_id=1, source_target_pairs={{0,8},{8,0},{1,9},{9,1},{2,10},{10,2},{3,11},{11,3},{4,12},{12,4},... | collective-permute-start | bytes 786440 | tf_op jit(solution)/shard_map/ppermute | solution.py:61
  127.6 9.0 %collective-permute-start.25 = (f32[128,512]{1,0:T(8,128)S(1)}, f32[128,512]{1,0:T(8,128)}, u32[]{:S(2)}, u32[]{:S(2)}) collective-permute-start(f32[128,512]{1,0:T(8,128)S(1)} %collective-permute-done.23.refs_12_), channel_id=1, source_target_pairs={{0,6},{2,0},{4,2},{6,4},{1,7},{3,1},{5,3},{7,5},{8,14},{10,8},{12,... | collective-permute-start | bytes 786440 | tf_op jit(solution)/shard_map/ppermute | solution.py:521
  133.2 5.9 %collective-permute-start.18 = (f32[128,512]{1,0:T(8,128)S(1)}, f32[128,512]{1,0:T(8,128)}, u32[]{:S(2)}, u32[]{:S(2)}) collective-permute-start(f32[128,512]{1,0:T(8,128)S(1)} %collective-permute-done.17.refs_6_), channel_id=1, source_target_pairs={{0,8},{8,0},{1,9},{9,1},{2,10},{10,2},{3,11},{11,3},{4,12},{12,4},... | collective-permute-start | bytes 786440 | tf_op jit(solution)/shard_map/ppermute | solution.py:61
  136.0 3.1 %collective-permute-start.24 = (f32[128,512]{1,0:T(8,128)S(1)}, f32[128,512]{1,0:T(8,128)}, u32[]{:S(2)}, u32[]{:S(2)}) collective-permute-start(f32[128,512]{1,0:T(8,128)S(1)} %collective-permute-done.23.refs_12_), channel_id=1, source_target_pairs={{0,8},{8,0},{1,9},{9,1},{2,10},{10,2},{3,11},{11,3},{4,12},{12,4},... | collective-permute-start | bytes 786440 | tf_op jit(solution)/shard_map/ppermute | solution.py:61
  136.0 3.1 %collective-permute-start.20 = (f32[128,512]{1,0:T(8,128)S(1)}, f32[128,512]{1,0:T(8,128)}, u32[]{:S(2)}, u32[]{:S(2)}) collective-permute-start(f32[128,512]{1,0:T(8,128)S(1)} %collective-permute-done.19.refs_8_), channel_id=1, source_target_pairs={{0,8},{8,0},{1,9},{9,1},{2,10},{10,2},{3,11},{11,3},{4,12},{12,4},... | collective-permute-start | bytes 786440 | tf_op jit(solution)/shard_map/ppermute | solution.py:61
  136.5 2.6 %collective-permute-start.22 = (f32[128,512]{1,0:T(8,128)S(1)}, f32[128,512]{1,0:T(8,128)}, u32[]{:S(2)}, u32[]{:S(2)}) collective-permute-start(f32[128,512]{1,0:T(8,128)S(1)} %collective-permute-done.21.refs_10_), channel_id=1, source_target_pairs={{0,8},{8,0},{1,9},{9,1},{2,10},{10,2},{3,11},{11,3},{4,12},{12,4},... | collective-permute-start | bytes 786440 | tf_op jit(solution)/shard_map/ppermute | solution.py:61
  136.6 2.5 %collective-permute-start.26 = (f32[128,512]{1,0:T(8,128)}, f32[128,512]{1,0:T(8,128)}, u32[]{:S(2)}, u32[]{:S(2)}) collective-permute-start(f32[128,512]{1,0:T(8,128)} %collective-permute-done.25.refs_14_), channel_id=1, source_target_pairs={{0,8},{8,0},{1,9},{9,1},{2,10},{10,2},{3,11},{11,3},{4,12},{12,4},... | collective-permute-start | bytes 786440 | tf_op jit(solution)/shard_map/ppermute | solution.py:61
  144.9 15.6 %all-to-all-start.5 = ((f32[16,3,128]{2,1,0:T(4,128)}), f32[16,3,128]{2,1,0:T(4,128)S(1)}, u32[]{:S(2)}, u32[]{:S(2)}) async-start(f32[16,3,128]{2,1,0:T(4,128)} %logits.1), calls=%async_computation.5 | async-start | bytes 65536 | tf_op jit(solution)/shard_map/all_to_all | solution.py:561
  152.9 27.2 %collective-permute-start.11 = (f32[2,512,256]{2,1,0:T(8,128)S(1)}, f32[2,512,256]{2,1,0:T(8,128)}, u32[]{:S(2)}, u32[]{:S(2)}) collective-permute-start(f32[2,512,256]{2,1,0:T(8,128)S(1)} %copy-done.2), channel_id=1, source_target_pairs={{0,8},{8,0},{1,9},{9,1},{2,10},{10,2},{3,11},{11,3},{4,12},{12,4},... | collective-permute-start | bytes 3145736 | tf_op jit(solution)/shard_map/ppermute | solution.py:61
  153.4 26.7 %collective-permute-start.10 = (f32[16,2,32,256]{3,2,1,0:T(8,128)S(1)}, f32[16,2,32,256]{3,2,1,0:T(8,128)}, u32[]{:S(2)}, u32[]{:S(2)}) collective-permute-start(f32[16,2,32,256]{3,2,1,0:T(8,128)S(1)} %bitcast.82), channel_id=1, source_target_pairs={{0,8},{8,0},{1,9},{9,1},{2,10},{10,2},{3,11},{11,3},{4,12},{12,4},... | collective-permute-start | bytes 3145736 | tf_op jit(solution)/shard_map/ppermute | solution.py:61
  161.2 18.0 %all-to-all-start.6 = ((f32[16,3,128]{2,1,0:T(4,128)}), f32[16,3,128]{2,1,0:T(4,128)S(1)}, u32[]{:S(2)}, u32[]{:S(2)}) async-start(f32[16,3,128]{2,1,0:T(4,128)} %broadcast_in_dim.17), calls=%async_computation.6 | async-start | bytes 65536 | tf_op jit(solution)/shard_map/all_to_all | solution.py:66
  (23 other events, 427.8 us)
